TPU v7x, 256 devices: a whole 4x4x8 slice. The times are simulated.
256 devices in a mesh: mp: 8 (over y, core), rows: 32 (over z, x).
Axes of the slice: x: 4, y: 4, z: 8, core: 2. Of those that a mesh axis runs over, the one named last changes fastest.
Arguments:
- hidden: bfloat16 [1024, 4096], P('rows'), may hold values from -60 to 60
- attn_gain: float32 [4096], replicated, may hold values from 0.3 to 1.7
- w_query: bfloat16 [4096, 4096], P(None, 'mp'), may hold values from -0.09375 to 0.09375
- w_key: bfloat16 [4096, 1024], P(None, 'mp'), may hold values from -0.09375 to 0.09375
- w_value: bfloat16 [4096, 1024], P(None, 'mp'), may hold values from -0.09375 to 0.09375
- w_output: bfloat16 [4096, 4096], P('mp'), may hold values from -0.09375 to 0.09375
- query_gain: float32 [128], replicated, may hold values from 0.5 to 1.5
- key_gain: float32 [128], replicated, may hold values from 0.5 to 1.5
- key_cache: bfloat16 [1024, 32, 1024], P('rows', None, 'mp'), may hold values from -730 to 730
- value_cache: bfloat16 [1024, 32, 1024], P('rows', None, 'mp'), may hold values from -6 to 6
- lengths: int32 [1024], P('rows'), may hold values from 1 to 32
- final_gain: float32 [4096], replicated, may hold values from 0.4 to 1.6
- old_embed: bfloat16 [1024, 4096], P('rows'), may hold values from -72 to 72
- slab: bfloat16 [16384, 4096], P('rows', 'mp'), may hold values from -6 to 6
- owners: int32 [16384, 1], P('rows'), may hold values from 0 to 31; in each aligned block of 512 rows (0 to 511, 512 to 1023, ...) at most 32 rows name the same one
Outputs:
- migrated: bfloat16 [32768, 4096], P('rows', 'mp')
Inputs may be any that keep to these rules, and one draw needn't show every extreme that they name: `owners`: in each aligned block of 512 cache rows no owner is named by more than 32 rows.
All inputs are finite; a program needn't handle non-finite values.
Results may differ from a plain program's by a relative error of at most 0.008.
Values may be sent and summed in bfloat16 or wider, within the bound.
No kernel may reach another device: no remote copies, remote signals or barrier semaphores. Data moves between devices by JAX's collectives and lax.ppermute only.
A program may use at most 64 MiB of HBM per device.

v0:
```python
import math

import jax
import jax.numpy as jnp
from jax import lax
from jax.sharding import PartitionSpec as P

D = 4096
HEADS = 32
KV_HEADS = 8
HEAD = 128
ITERS = 3


def rotate(values, position):
    half_width = values.shape[-1] // 2
    exponent = 2.0 * jnp.arange(half_width, dtype=jnp.float32) / values.shape[-1]
    frequency = jnp.exp(-exponent * math.log(1000000.0))
    angle = position[:, None, None] * frequency[None, None, :]
    cosine = jnp.cos(angle)
    sine = jnp.sin(angle)
    first = values[..., :half_width]
    second = values[..., half_width:]
    return jnp.concatenate(
        [first * cosine - second * sine, second * cosine + first * sine], axis=-1
    )


def head_norm(values, gain):
    scale = lax.rsqrt(jnp.mean(values * values, axis=-1, keepdims=True) + 1e-06)
    return values * scale * gain


def contract_first(left, right, precision):
    return lax.dot_general(
        left,
        right,
        (((0,), (0,)), ((), ())),
        precision=precision,
        preferred_element_type=jnp.float32,
    )


def local(
    hidden,
    attn_gain,
    w_query,
    w_key,
    w_value,
    w_output,
    query_gain,
    key_gain,
    key_cache,
    value_cache,
    lengths,
    final_gain,
    old_embed,
    slab,
    owners,
):
    docs = hidden.shape[0]
    width = hidden.shape[1]
    kv_local = w_key.shape[1] // HEAD
    group = HEADS // KV_HEADS
    rows_count = lax.axis_size("rows")
    mp_count = lax.axis_size("mp")
    cols = width // mp_count
    highest = lax.Precision.HIGHEST
    hidden32 = hidden.astype(jnp.float32)
    normed = (
        hidden32
        * lax.rsqrt(jnp.mean(hidden32 * hidden32, axis=-1, keepdims=True) + 1e-06)
        * attn_gain
    ).astype(jnp.bfloat16)
    position = lengths.astype(jnp.float32)
    query = jnp.dot(normed, w_query, preferred_element_type=jnp.float32).reshape(
        docs, kv_local * group, HEAD
    )
    query = rotate(head_norm(query, query_gain), position).astype(jnp.bfloat16)
    key_new = jnp.dot(normed, w_key, preferred_element_type=jnp.float32).reshape(
        docs, kv_local, HEAD
    )
    key_new = rotate(head_norm(key_new, key_gain), position).astype(jnp.bfloat16)
    value_new = (
        jnp.dot(normed, w_value, preferred_element_type=jnp.float32)
        .reshape(docs, kv_local, HEAD)
        .astype(jnp.bfloat16)
    )
    query_groups = query.reshape(docs, kv_local, group, HEAD)
    keys = key_cache.reshape(docs, key_cache.shape[1], kv_local, HEAD)
    values = value_cache.reshape(docs, value_cache.shape[1], kv_local, HEAD)
    scale = 1.0 / math.sqrt(HEAD)
    scores = (
        jnp.einsum("akgd,apkd->akgp", query_groups, keys, preferred_element_type=jnp.float32)
        * scale
    )
    own_score = (
        jnp.einsum("akgd,akd->akg", query_groups, key_new, preferred_element_type=jnp.float32)
        * scale
    )
    valid = jnp.arange(keys.shape[1], dtype=jnp.int32)[None, :] < lengths[:, None]
    scores = jnp.where(valid[:, None, None, :], scores, -jnp.inf)
    top = jnp.maximum(jnp.max(scores, axis=-1), own_score)
    expo = jnp.exp(scores - top[..., None])
    own_expo = jnp.exp(own_score - top)
    total = jnp.sum(expo, axis=-1) + own_expo
    weights = (expo / total[..., None]).astype(jnp.bfloat16)
    own_weight = (own_expo / total).astype(jnp.bfloat16)
    attended = jnp.einsum("akgp,apkd->akgd", weights, values, preferred_element_type=jnp.float32)
    attended = (
        attended
        + own_weight.astype(jnp.float32)[..., None] * value_new.astype(jnp.float32)[:, :, None, :]
    )
    attended = attended.reshape(docs, kv_local * group * HEAD).astype(jnp.bfloat16)
    partial_value = jnp.dot(attended, w_output, preferred_element_type=jnp.float32)
    state = hidden32 + lax.psum(partial_value, "mp")
    new_embed = (
        state * lax.rsqrt(jnp.mean(state * state, axis=-1, keepdims=True) + 1e-06) * final_gain
    ).astype(jnp.bfloat16)
    new_cols = lax.dynamic_slice_in_dim(new_embed, lax.axis_index("mp") * cols, cols, 1)
    old_cols = lax.all_to_all(old_embed, "rows", split_axis=1, concat_axis=0, tiled=True)
    block = old_embed
    cross = lax.psum_scatter(
        contract_first(block, new_cols, None), "rows", scatter_dimension=0, tiled=True
    )
    ridge = 0.125 * D
    old32 = old_cols.astype(jnp.float32)
    ridge_map = jnp.zeros_like(cross)
    residual = cross
    direction = cross

    def column_total(current):
        return lax.psum(jnp.sum(current * current, axis=0), "rows")

    res_sq = column_total(residual)
    for sweep in range(ITERS):
        image_docs, direction_sq = lax.psum(
            (jnp.dot(old32, direction, precision=highest), jnp.sum(direction * direction, axis=0)),
            "rows",
        )
        curvature = jnp.sum(image_docs * image_docs, axis=0) + ridge * direction_sq
        alpha = res_sq / curvature
        ridge_map = ridge_map + alpha * direction
        image = contract_first(old32, image_docs, highest) + ridge * direction
        residual = residual - alpha * image
        if sweep + 1 < ITERS:
            new_sq = column_total(residual)
            direction = residual + new_sq / res_sq * direction
            res_sq = new_sq
    map_b = ridge_map.astype(jnp.bfloat16)
    slab_full = lax.all_gather(slab, "mp", axis=1, tiled=True)
    block = slab_full
    moved = jnp.dot(
        block, lax.all_gather(map_b, "rows", axis=0, tiled=True), preferred_element_type=jnp.float32
    ).astype(jnp.bfloat16)
    capacity = 2 * slab.shape[0] // rows_count
    owner_ids = owners[:, 0]
    onehot = (owner_ids[:, None] == jnp.arange(rows_count, dtype=jnp.int32)[None, :]).astype(
        jnp.int32
    )
    counted = jnp.cumsum(onehot, axis=0)
    slot = jnp.sum((counted - 1) * onehot, axis=-1)
    target = owner_ids * capacity + slot
    outgoing = jnp.zeros((rows_count * capacity, cols), jnp.bfloat16).at[target].set(moved)
    return lax.all_to_all(outgoing, "rows", split_axis=0, concat_axis=0, tiled=True)


def solution(mesh):
    return jax.shard_map(
        local,
        mesh=mesh,
        in_specs=(
            P("rows", None),
            P(),
            P(None, "mp"),
            P(None, "mp"),
            P(None, "mp"),
            P("mp", None),
            P(),
            P(),
            P("rows", None, "mp"),
            P("rows", None, "mp"),
            P("rows"),
            P(),
            P("rows", None),
            P("rows", "mp"),
            P("rows", None),
        ),
        out_specs=P("rows", "mp"),
        check_vma=False,
    )
```

profile of v0, /device:TPU:2, one launch (start us, length us, event | category | flops | bytes accessed | tf_op | source)
XLA Modules:
  0.0 1109.6 jit_solution(4538609106002882769)
XLA Ops:
  6.6 0.7 convert_element_type.64
  7.3 0.7 iota_compare_fusion.2
  8.0 1.1 fusion.10
  9.2 1.4 multiply_reduce_fusion.10
  10.7 0.7 multiply_bitcast_fusion
  11.7 3.3 fusion.47
  15.4 0.2 fusion.37
  15.6 0.4 fusion.49
  16.3 0.3 fusion.9
  16.6 0.3 fusion.8
  16.9 3.9 fusion.22
  20.8 0.8 dynamic-slice
  21.6 68.5 %all-reduce.5.cloned.1.call-done = f32[32,4096]{1,0:T(8,128)} async-done(((f32[32,4096]{1,0:T(8,128)}), f32[32,4096]{1,0:T(8,128)}) %all-reduce.5.cloned.1.call-update) | async-done | bytes 524304 | tf_op jit(solution)/shard_map/psum | solution.py:116
  90.1 1.2 multiply_reduce_fusion.3
  91.3 4.6 convolution_bitcast_fusion
  96.0 21.7 %all_to_all.31 = bf16[32,32,128]{2,0,1:T(8,128)(2,1)S(1)} all-to-all(bf16[32,32,128]{2,0,1:T(8,128)(2,1)S(1)} %copy_bitcast_fusion), channel_id=1, replica_groups=mesh['mp'=8,'rows'=32] {'rows'}, dimensions={1} | all-to-all | bytes 524288 | tf_op jit(solution)/shard_map/all_to_all | solution.py:121
  117.7 209.6 %reduce-scatter.2.cloned.1.call-done = f32[128,512]{0,1:T(8,128)} async-done(((f32[4096,512]{0,1:T(8,128)}), f32[128,512]{0,1:T(8,128)}) %reduce-scatter.2.cloned.1.call-update) | async-done | bytes 262160 | tf_op jit(solution)/shard_map/reduce_scatter | solution.py:123
  327.3 3.3 convolution_bitcast_fusion.3
  330.8 71.1 %psum.67 = f32[512]{0:T(512)S(1)} all-reduce(f32[512]{0:T(512)S(1)} %multiply_reduce_fusion.8), channel_id=1, replica_groups=mesh['mp'=8,'rows'=32] {'rows'}, use_global_device_ids=true, to_apply=%region_12.13 | all-reduce | flops 512 | bytes 4096 | tf_op jit(solution)/shard_map/psum | solution.py:133
  402.0 81.2 %all-reduce.7.cloned.1.call-done = f32[1024,512]{0,1:T(8,128)} async-done(((f32[1024,512]{0,1:T(8,128)}), f32[1024,512]{0,1:T(8,128)}) %all-reduce.7.cloned.1.call-update) | async-done | bytes 2097168 | tf_op jit(solution)/shard_map/psum | solution.py:137
  483.1 2.0 multiply_reduce_fusion.2
  485.1 0.3 copy-done.2
  485.3 1.2 multiply_reduce_fusion.7
  486.5 71.5 %psum.69 = f32[512]{0:T(512)S(1)} all-reduce(f32[512]{0:T(512)S(1)} %get-tuple-element.21), channel_id=1, replica_groups=mesh['mp'=8,'rows'=32] {'rows'}, use_global_device_ids=true, to_apply=%region_16.17 | all-reduce | flops 512 | bytes 4096 | tf_op jit(solution)/shard_map/psum | solution.py:133
  558.0 0.2 multiply_reduce_fusion.6
  558.2 2.3 convolution_bitcast_fusion.2
  560.6 72.5 %psum.71 = f32[512]{0:T(512)S(1)} all-reduce(f32[512]{0:T(512)S(1)} %get-tuple-element.5), channel_id=1, replica_groups=mesh['mp'=8,'rows'=32] {'rows'}, use_global_device_ids=true, to_apply=%region_20.21 | all-reduce | flops 512 | bytes 4096 | tf_op jit(solution)/shard_map/psum | solution.py:137
  633.0 78.8 %all-reduce.9.cloned.1.call-done = f32[1024,512]{0,1:T(8,128)} async-done(((f32[1024,512]{0,1:T(8,128)}), f32[1024,512]{0,1:T(8,128)}) %all-reduce.9.cloned.1.call-update) | async-done | bytes 2097168 | tf_op jit(solution)/shard_map/psum | solution.py:137
  711.8 2.0 multiply_reduce_fusion.1
  713.8 0.3 copy-done.1
  714.1 1.2 multiply_reduce_fusion.5
  715.2 71.5 %psum.72 = f32[512]{0:T(512)S(1)} all-reduce(f32[512]{0:T(512)S(1)} %get-tuple-element.23), channel_id=1, replica_groups=mesh['mp'=8,'rows'=32] {'rows'}, use_global_device_ids=true, to_apply=%region_22.23 | all-reduce | flops 512 | bytes 4096 | tf_op jit(solution)/shard_map/psum | solution.py:133
  786.7 2.4 convolution_bitcast_fusion.1
  789.2 0.5 all-gather.5.cloned.1.call-update
  789.8 0.2 multiply_reduce_fusion.4
  790.0 72.5 %psum.74 = f32[512]{0:T(512)S(1)} all-reduce(f32[512]{0:T(512)S(1)} %multiply_reduce_fusion.4), channel_id=1, replica_groups=mesh['mp'=8,'rows'=32] {'rows'}, use_global_device_ids=true, to_apply=%region_26.27 | all-reduce | flops 512 | bytes 4096 | tf_op jit(solution)/shard_map/psum | solution.py:137
  862.5 77.8 %all-reduce.11.cloned.1.call-done = f32[1024,512]{0,1:T(8,128)} async-done(((f32[1024,512]{0,1:T(8,128)}), f32[1024,512]{0,1:T(8,128)}) %all-reduce.11.cloned.1.call-update) | async-done | bytes 2097168 | tf_op jit(solution)/shard_map/psum | solution.py:137
  940.3 1.8 multiply_reduce_fusion
  942.1 1.0 add_convert_fusion
  943.2 1.2 reduce-window.6
  944.4 0.2 slice_reduce_fusion
  944.7 30.8 %all-gather.5.cloned.1.call-done = bf16[512,4096]{1,0:T(8,128)(2,1)} async-done(((bf16[512,512]{1,0:T(8,128)(2,1)}), bf16[512,4096]{1,0:T(8,128)(2,1)}) %all-gather.5.cloned.1.call-update) | async-done | bytes 4194320 | tf_op jit(solution)/shard_map/all_gather | solution.py:151
  975.5 85.5 %all-gather.3.cloned.1.call-done = bf16[4096,512]{0,1:T(8,128)(2,1)} async-done(((bf16[128,512]{0,1:T(8,128)(2,1)}), bf16[4096,512]{0,1:T(8,128)(2,1)}) %all-gather.3.cloned.1.call-update) | async-done | bytes 4194320 | tf_op jit(solution)/shard_map/all_gather | solution.py:154
  1061.0 5.8 fusion
  1066.9 0.2 copy.32
  1067.1 2.7 scatter_custom_fusion
  1069.8 31.9 %all_to_all.32 = bf16[32,32,512]{2,1,0:T(8,128)(2,1)S(1)} all-to-all(bf16[32,32,512]{2,1,0:T(8,128)(2,1)S(1)} %bitcast.92), channel_id=1, replica_groups=mesh['mp'=8,'rows'=32] {'rows'}, dimensions={0} | all-to-all | bytes 2097152 | tf_op jit(solution)/shard_map/all_to_all | solution.py:165
  1101.7 1.0 copy.53
  (62 shorter events, 1.8 us)
Async XLA Ops:
  6.5 2.6 copy-start
  6.5 83.5 %all-reduce.5.cloned.1.call-start = ((), (), s32[]{:S(2)}) async-start(), calls=%async_computation.3 | async-start | bytes 1048576 | tf_op jit(solution)/shard_map/psum | solution.py:116
  11.6 3.6 copy-start.10
  11.6 4.0 copy-start.7
  11.6 4.6 copy-start.3
  11.6 4.6 copy-start.6
  11.6 4.6 copy-start.8
  14.9 1.7 copy-start.11
  16.9 74.4 %copy-start.5 = (bf16[32,4096]{1,0:T(8,128)(2,1)S(1)}, bf16[32,4096]{1,0:T(8,128)(2,1)}, u32[]{:S(2)}) copy-start(bf16[32,4096]{1,0:T(8,128)(2,1)} %param.27) | copy-start | bytes 786436
  20.8 306.5 %reduce-scatter.2.cloned.1.call-start = ((), (), s32[]{:S(2)}) async-start(), calls=%async_computation.4 | async-start | bytes 8650752 | tf_op jit(solution)/shard_map/reduce_scatter | solution.py:123
  95.9 387.2 %all-reduce.7.cloned.1.call-start = ((), (), s32[]{:S(2)}) async-start(), calls=%async_computation.5 | async-start | bytes 4194304 | tf_op jit(solution)/shard_map/psum | solution.py:137
  327.3 3.4 copy-start.4
  330.6 381.2 %all-reduce.9.cloned.1.call-start = ((), (), s32[]{:S(2)}) async-start(), calls=%async_computation.6 | async-start | bytes 4194304 | tf_op jit(solution)/shard_map/psum | solution.py:137
  483.1 2.2 copy-start.2
  560.5 379.8 %all-reduce.11.cloned.1.call-start = ((), (), s32[]{:S(2)}) async-start(), calls=%async_computation.7 | async-start | bytes 4194304 | tf_op jit(solution)/shard_map/psum | solution.py:137
  711.8 2.2 copy-start.1
  789.1 154.0 %copy-start.9 = (s32[512,1]{0,1:T(1,128)S(1)}, s32[512,1]{0,1:T(1,128)}, u32[]{:S(2)}) copy-start(s32[512,1]{0,1:T(1,128)} %param.29) | copy-start | bytes 6148
  789.1 186.4 %all-gather.5.cloned.1.call-start = ((), (), s32[]{:S(2)}) async-start(), calls=%async_computation.9 | async-start | bytes 4718592 | tf_op jit(solution)/shard_map/all_gather | solution.py:151
  789.7 271.3 %all-gather.3.cloned.1.call-start = ((), (), s32[]{:S(2)}) async-start(), calls=%async_computation.8 | async-start | bytes 4325376 | tf_op jit(solution)/shard_map/all_gather | solution.py:154
Sparse Core Ops, SparseCore 0:
  20.9 69.1 all-reduce.4
  96.0 231.2 reduce-scatter.1
  330.8 152.2 all-reduce.6
  560.7 151.1 all-reduce.8
  789.2 151.0 all-reduce.10
  942.0 33.4 all-gather.4
  978.0 83.0 all-gather.2
where the time goes:
time: 1110 us
  waiting for transfers between devices  633 us (57%)
  blocking collectives  413 us (37%)
  matrix products  30.4 us (3%)
  other arithmetic  14.2 us (1%)
  between operations  13.8 us (1%)
    psum x3, waiting for transfers between devices, local(): lax.psum((jnp.dot(old32, direction, precision=highest), jnp.sum(direction...  238 us
    psum x3, blocking collectives, column_total(): return lax.psum(jnp.sum(current * current, axis=0), 'rows')  214 us
    reduce_scatter x1, waiting for transfers between devices, local(): lax.psum_scatter(contract_first(block, new_cols, None), 'rows', scatter_d...  210 us
    psum x2, blocking collectives, local(): lax.psum((jnp.dot(old32, direction, precision=highest), jnp.sum(direction...  145 us
    all_gather x1, waiting for transfers between devices, local(): lax.all_gather(map_b, 'rows', axis=0, tiled=True)  85.5 us
    psum x1, waiting for transfers between devices, local(): state = hidden32 + lax.psum(partial_value, 'mp')  68.5 us
    all_to_all x1, blocking collectives, local(): lax.all_to_all(outgoing, 'rows', split_axis=0, concat_axis=0, tiled=True)  31.9 us
    all_gather x1, waiting for transfers between devices, local(): slab_full = lax.all_gather(slab, 'mp', axis=1, tiled=True)  30.8 us
  transfers between devices with their start and end apart: 7, of which 7 were waited for; matrix products, arithmetic and copies ran while one was open for 1% of the time, Pallas kernels for 0%

commit v1 on v0

--- a/solution.py
+++ b/solution.py
@@ -3,6 +3,8 @@
 import jax
 import jax.numpy as jnp
 from jax import lax
+from jax.experimental import pallas as pl
+from jax.experimental.pallas import tpu as pltpu
 from jax.sharding import PartitionSpec as P
 
 D = 4096
@@ -31,13 +33,166 @@
     return values * scale * gain
 
 
-def contract_first(left, right, precision):
+TILE = 256
+
+
+def contract_last(left, right):
     return lax.dot_general(
-        left,
-        right,
-        (((0,), (0,)), ((), ())),
-        precision=precision,
-        preferred_element_type=jnp.float32,
+        left, right, (((1,), (1,)), ((), ())), preferred_element_type=jnp.float32
+    )
+
+
+def spread(block, axis, count, groups=None):
+    copies = jnp.broadcast_to(block[None], (count,) + block.shape)
+    return lax.all_to_all(copies, axis, 0, 0, tiled=True, axis_index_groups=groups)
+
+
+def spread_mp(block):
+    size = lax.axis_size("mp")
+    groups = [list(range(core, size, 2)) for core in range(2)]
+    own = spread(block, "mp", size // 2, groups)
+    return own, lax.ppermute(own, "mp", [(i, i ^ 1) for i in range(size)])
+
+
+def tiles(body, init=0):
+    return lax.fori_loop(0, 1024 // TILE, body, init)
+
+
+def place(core, own, other, target, start):
+    for y in range(own.shape[0]):
+        for part, at in ((own, core), (other, 1 - core)):
+            first = pl.multiple_of((2 * y + at) * 128, 128)
+            target[:, pl.ds(first, 128)] = part[y, :, start : start + 128]
+
+
+def solve_kernel(
+    core_ref, own, other, state, scale, gain, result,
+    high, low, rho, rho_high, rho_low, image, way, way_image, total,
+):
+    core = core_ref[0]
+    ridge = 0.125 * D
+    place(core, own, other, high, 0)
+    place(core, own, other, low, 128)
+
+    def rows_of(i):
+        return pl.ds(pl.multiple_of(i * TILE, TILE), TILE)
+
+    def split(rows, value):
+        rho[rows, :] = value
+        top = value.astype(jnp.bfloat16)
+        rho_high[rows, :] = top
+        rho_low[rows, :] = (value - top.astype(jnp.float32)).astype(jnp.bfloat16)
+
+    def start(i, carry):
+        rows = rows_of(i)
+        value = state[rows, :].astype(jnp.float32) * scale[rows, :] * gain[...]
+        split(rows, value)
+        way[rows, :] = value
+        return carry
+
+    tiles(start)
+
+    def dot(left, right):
+        return jnp.dot(left, right, preferred_element_type=jnp.float32)
+
+    def product(i, square):
+        rows = rows_of(i)
+        value = dot(high[rows, :], rho_low[...]) + dot(low[rows, :], rho_high[...])
+        value = value + dot(high[rows, :], rho_high[...])
+        image[rows, :] = value
+        return square + jnp.sum(rho[rows, :] * value, axis=0, keepdims=True)
+
+    zero = jnp.zeros((1, state.shape[1]), jnp.float32)
+    res_sq = tiles(product, zero)
+    ratio = zero
+    for sweep in range(ITERS):
+
+        def turn(i, curvature):
+            rows = rows_of(i)
+            if sweep == 0:
+                step, step_image = way[rows, :], image[rows, :]
+            else:
+                step = rho[rows, :] + ratio * way[rows, :]
+                step_image = image[rows, :] + ratio * way_image[rows, :]
+                way[rows, :] = step
+            way_image[rows, :] = step_image
+            return curvature + jnp.sum(
+                step_image * (step_image + ridge * step), axis=0, keepdims=True
+            )
+
+        alpha = res_sq / tiles(turn, zero)
+
+        def update(i, carry):
+            rows = rows_of(i)
+            step = way[rows, :]
+            moved = alpha * step
+            if sweep:
+                moved = total[rows, :] + moved
+            if sweep + 1 < ITERS:
+                total[rows, :] = moved
+                split(rows, rho[rows, :] - alpha * (way_image[rows, :] + ridge * step))
+            else:
+                result[rows, :] = moved.astype(jnp.bfloat16)
+            return carry
+
+        tiles(update)
+        if sweep + 1 < ITERS:
+            new_sq = tiles(product, zero)
+            ratio = new_sq / res_sq
+            res_sq = new_sq
+
+
+def call(kernel, out_shape, scratch, operands, flops):
+    vmem = pl.BlockSpec(memory_space=pltpu.VMEM)
+    return pl.pallas_call(
+        kernel,
+        out_shape=out_shape,
+        in_specs=[pl.BlockSpec(memory_space=pltpu.SMEM)] + [vmem] * (len(operands) - 1),
+        out_specs=vmem,
+        scratch_shapes=scratch,
+        cost_estimate=pl.CostEstimate(flops=flops, bytes_accessed=1 << 23, transcendentals=0),
+        compiler_params=pltpu.CompilerParams(vmem_limit_bytes=40 << 20),
+    )(*operands)
+
+
+def solve(*operands):
+    anchors, cols = operands[3].shape
+    wide = pltpu.VMEM((anchors, anchors), jnp.bfloat16)
+    full = pltpu.VMEM((anchors, cols), jnp.float32)
+    half = pltpu.VMEM((anchors, cols), jnp.bfloat16)
+    return call(
+        solve_kernel,
+        jax.ShapeDtypeStruct((anchors, cols), jnp.bfloat16),
+        [wide, wide, full, half, half, full, full, full, full],
+        operands,
+        18 * anchors * anchors * cols,
+    )
+
+
+def apply_kernel(core_ref, own, other, dual_map, result, routed):
+    place(core_ref[0], own, other, routed, 0)
+
+    def rows_of(i):
+        return pl.ds(pl.multiple_of(i * TILE, TILE), TILE)
+
+    def product(i, carry):
+        rows = rows_of(i)
+        value = jnp.dot(routed[rows, :], dual_map[...], preferred_element_type=jnp.float32)
+        result[rows, :] = value.astype(jnp.bfloat16)
+        return carry
+
+    tiles(product)
+
+
+def apply_map(*operands):
+    anchors, cols = operands[3].shape
+    slots = operands[1].shape[1]
+    return call(
+        apply_kernel,
+        jax.ShapeDtypeStruct((slots, cols), jnp.bfloat16),
+        [pltpu.VMEM((slots, anchors), jnp.bfloat16)],
+        operands,
+        2 * slots * anchors * cols,
     )
 
 
@@ -65,7 +220,6 @@
     rows_count = lax.axis_size("rows")
     mp_count = lax.axis_size("mp")
     cols = width // mp_count
-    highest = lax.Precision.HIGHEST
     hidden32 = hidden.astype(jnp.float32)
     normed = (
         hidden32
@@ -113,46 +267,32 @@
     )
     attended = attended.reshape(docs, kv_local * group * HEAD).astype(jnp.bfloat16)
     partial_value = jnp.dot(attended, w_output, preferred_element_type=jnp.float32)
-    state = hidden32 + lax.psum(partial_value, "mp")
-    new_embed = (
-        state * lax.rsqrt(jnp.mean(state * state, axis=-1, keepdims=True) + 1e-06) * final_gain
-    ).astype(jnp.bfloat16)
-    new_cols = lax.dynamic_slice_in_dim(new_embed, lax.axis_index("mp") * cols, cols, 1)
-    old_cols = lax.all_to_all(old_embed, "rows", split_axis=1, concat_axis=0, tiled=True)
-    block = old_embed
-    cross = lax.psum_scatter(
-        contract_first(block, new_cols, None), "rows", scatter_dimension=0, tiled=True
-    )
-    ridge = 0.125 * D
-    old32 = old_cols.astype(jnp.float32)
-    ridge_map = jnp.zeros_like(cross)
-    residual = cross
-    direction = cross
-
-    def column_total(current):
-        return lax.psum(jnp.sum(current * current, axis=0), "rows")
-
-    res_sq = column_total(residual)
-    for sweep in range(ITERS):
-        image_docs, direction_sq = lax.psum(
-            (jnp.dot(old32, direction, precision=highest), jnp.sum(direction * direction, axis=0)),
-            "rows",
-        )
-        curvature = jnp.sum(image_docs * image_docs, axis=0) + ridge * direction_sq
-        alpha = res_sq / curvature
-        ridge_map = ridge_map + alpha * direction
-        image = contract_first(old32, image_docs, highest) + ridge * direction
-        residual = residual - alpha * image
-        if sweep + 1 < ITERS:
-            new_sq = column_total(residual)
-            direction = residual + new_sq / res_sq * direction
-            res_sq = new_sq
-    map_b = ridge_map.astype(jnp.bfloat16)
-    slab_full = lax.all_gather(slab, "mp", axis=1, tiled=True)
-    block = slab_full
-    moved = jnp.dot(
-        block, lax.all_gather(map_b, "rows", axis=0, tiled=True), preferred_element_type=jnp.float32
-    ).astype(jnp.bfloat16)
+    mine = lax.axis_index("mp") * cols
+    core = lax.axis_index("mp") % 2
+    my_cols = lambda array, axis: lax.dynamic_slice_in_dim(array, mine, cols, axis)
+    pieces = partial_value.astype(jnp.bfloat16).reshape(docs, mp_count, cols).transpose(1, 0, 2)
+    pieces = lax.all_to_all(pieces, "mp", 0, 0, tiled=True)
+    state = my_cols(hidden32, 1) + jnp.sum(pieces.astype(jnp.float32), axis=0)
+    squares = jnp.sum(state * state, axis=-1)[None, :]
+    squares = jnp.sum(spread(squares, "mp", mp_count), axis=0)
+    scale_rows = lax.rsqrt(spread(squares, "rows", rows_count) / width + 1e-06)
+    state_all = spread(state.astype(jnp.bfloat16), "rows", rows_count)
+
+    old_mine = my_cols(old_embed, 1)
+    old_all = spread(old_mine, "rows", rows_count).reshape(rows_count * docs, cols)
+    anchors = rows_count * docs
+    part = anchors // mp_count
+    gram_part = contract_last(old_mine, old_all).reshape(docs, mp_count, part).transpose(1, 0, 2)
+    gram_part = jnp.sum(lax.all_to_all(gram_part, "mp", 0, 0, tiled=True), axis=0)
+    high = lax.reduce_precision(gram_part, 8, 7)
+    gram_part = jnp.concatenate([high, gram_part - high], axis=1).astype(jnp.bfloat16)
+    gram = spread(gram_part, "rows", rows_count).reshape(anchors, 2 * part)
+    gram_own, gram_other = spread_mp(gram)
+
+    slab_part = contract_last(slab, old_all).astype(jnp.bfloat16)
+    slab_part = slab_part.reshape(-1, mp_count, part).transpose(1, 0, 2)
+    slab_part = lax.all_to_all(slab_part, "mp", 0, 0, tiled=True)
+    slab_dual = jnp.sum(slab_part.astype(jnp.float32), axis=0).astype(jnp.bfloat16)
     capacity = 2 * slab.shape[0] // rows_count
     owner_ids = owners[:, 0]
     onehot = (owner_ids[:, None] == jnp.arange(rows_count, dtype=jnp.int32)[None, :]).astype(
@@ -161,8 +301,20 @@
     counted = jnp.cumsum(onehot, axis=0)
     slot = jnp.sum((counted - 1) * onehot, axis=-1)
     target = owner_ids * capacity + slot
-    outgoing = jnp.zeros((rows_count * capacity, cols), jnp.bfloat16).at[target].set(moved)
-    return lax.all_to_all(outgoing, "rows", split_axis=0, concat_axis=0, tiled=True)
+    outgoing = jnp.zeros((rows_count * capacity, part), jnp.bfloat16).at[target].set(slab_dual)
+    routed = lax.all_to_all(outgoing, "rows", split_axis=0, concat_axis=0, tiled=True)
+    routed_own, routed_other = spread_mp(routed)
+
+    core = core.astype(jnp.int32).reshape(1)
+    dual_map = solve(
+        core,
+        gram_own,
+        gram_other,
+        state_all.reshape(anchors, cols),
+        scale_rows.reshape(anchors, 1),
+        my_cols(final_gain, 0).reshape(1, cols),
+    )
+    return apply_map(core, routed_own, routed_other, dual_map)
 
 
 def solution(mesh):

time: 1110 us -> 262 us (0.24)
  waiting for transfers between devices: 633 us -> 115 us
  blocking collectives: 413 us -> 42.9 us
  starting transfers between devices: 0.25 us -> 48.5 us
  Pallas kernels: 0 us -> 22.6 us
  matrix products: 30.4 us -> 11.6 us
  between operations: 13.8 us -> 0.4 us
    psum x5 -> x0, blocking collectives: 359 us -> none  [the longest x3 214 us: column_total(): return lax.psum(jnp.sum(current * current, axis=0), 'rows')]
    psum x4 -> x0, waiting for transfers between devices: 306 us -> none  [the longest x3 238 us: local(): lax.psum((jnp.dot(old32, direction, precision=highest), jnp.sum(direction...]
    reduce_scatter x1 -> x0, waiting for transfers between devices: 210 us -> none  [local(): lax.psum_scatter(contract_first(block, new_cols, None), 'rows', scatter_d...]
    all_gather x2 -> x0, waiting for transfers between devices: 116 us -> none  [the longest x1 85.5 us: local(): lax.all_gather(map_b, 'rows', axis=0, tiled=True)]
    all_to_all x0 -> x9, waiting for transfers between devices: none -> 115 us  [the longest x6 87.2 us: spread(): lax.all_to_all(copies, axis, 0, 0, tiled=True, axis_index_groups=groups)]
    all_to_all x0 -> x9, starting transfers between devices: none -> 48.1 us  [the longest x6 36.7 us: spread(): lax.all_to_all(copies, axis, 0, 0, tiled=True, axis_index_groups=groups)]
    pallas_call x0 -> x2, Pallas kernels: none -> 22.6 us  [call(): pl.pallas_call(kernel, out_shape=out_shape, in_specs=[pl.BlockSpec(memory...]
    dot_general x7 -> x2, matrix products: 20.7 us -> 2.77 us  [contract_last(): lax.dot_general(left, right, (((1,), (1,)), ((), ())), preferred_element_...]
  transfers between devices with their start and end apart: 7 -> 11, of which waited for: 7 -> 9; matrix products, arithmetic and copies ran while one was open for 1% -> 4% of each run, Pallas kernels for 0% -> 7%
where the time goes in v1:
time: 262 us; the launch traced here: 261 us
  waiting for transfers between devices  115 us (44%)
  starting transfers between devices  48.5 us (19%)
  blocking collectives  42.9 us (16%)
  Pallas kernels  22.6 us (9%)
  local copies, waits for them, and re-layouts  14 us (5%)
  matrix products  11.6 us (4%)
  other arithmetic  6.09 us (2%)
    all_to_all x6, waiting for transfers between devices, spread(): lax.all_to_all(copies, axis, 0, 0, tiled=True, axis_index_groups=groups)  87.2 us
    all_to_all x6, starting transfers between devices, spread(): lax.all_to_all(copies, axis, 0, 0, tiled=True, axis_index_groups=groups)  36.7 us
    all_to_all x1, blocking collectives, spread(): lax.all_to_all(copies, axis, 0, 0, tiled=True, axis_index_groups=groups)  27.3 us
    pallas_call x2, Pallas kernels, call(): pl.pallas_call(kernel, out_shape=out_shape, in_specs=[pl.BlockSpec(memory...  22.6 us
    all_to_all x1, waiting for transfers between devices, local(): slab_part = lax.all_to_all(slab_part, 'mp', 0, 0, tiled=True)  15.8 us
    all_to_all x1, blocking collectives, local(): lax.all_to_all(outgoing, 'rows', split_axis=0, concat_axis=0, tiled=True)  15.6 us
    all_to_all x1, waiting for transfers between devices, local(): pieces = lax.all_to_all(pieces, 'mp', 0, 0, tiled=True)  7.46 us
    broadcast_in_dim x7, local copies, waits for them, and re-layouts, spread(): copies = jnp.broadcast_to(block[None], (count,) + block.shape)  5.49 us
  transfers between devices with their start and end apart: 11, of which 9 were waited for; matrix products, arithmetic and copies ran while one was open for 4% of the time, Pallas kernels for 7%

profile of v1, /device:TPU:2, one launch (start us, length us, event | category | flops | bytes accessed | tf_op | source)
XLA Modules:
  0.0 260.9 jit_solution(9363737524009779758)
XLA Ops:
  0.1 0.8 convert_element_type.75
  0.9 0.7 iota_compare_fusion.2
  1.6 1.1 multiply_reduce_fusion
  2.7 1.5 multiply_reduce_fusion.3
  4.4 0.7 multiply_bitcast_fusion
  5.2 3.2 %fusion.31 = f32[32,512]{1,0:T(8,128)S(1)} fusion(bf16[4096,512]{1,0:T(8,128)(2,1)} %param.17, f32[4096]{0:T(1024)} %param.16, f32[32]{0:T(128)S(1)} %add_rsqrt_fusion.2, bf16[32,4096]{1,0:T(8,128)(2,1)} %param.15), kind=kOutput, calls=%fused_computation.77 | convolution fusion | flops 134742016 | bytes 4538496 | tf_op jit(solution)/shard_map/dot_general | solution.py:230
  9.1 0.4 fusion.32
  9.8 0.3 fusion.2
  10.4 3.0 %convolution_convert_fusion = bf16[32,4096]{1,0:T(8,128)(2,1)S(1)} fusion(bf16[512,4096]{1,0:T(8,128)(2,1)} %param.20, bf16[4,8,4,128]{3,2,1,0:T(4,128)(2,1)S(1)} %bitcast.77), kind=kOutput, calls=%fused_computation.1 | convolution fusion | flops 134348800 | bytes 4489216 | tf_op jit(solution)/shard_map/dot_general | solution.py:269
  13.4 0.7 copy.47
  14.1 4.5 %all-to-all-start.7 = ((bf16[8,32,512]{2,1,0:T(8,128)(2,1)}), bf16[8,32,512]{2,1,0:T(8,128)(2,1)S(1)}, u32[]{:S(2)}, u32[]{:S(2)}) async-start(bf16[8,32,512]{2,1,0:T(8,128)(2,1)} %bitcast.67), calls=%async_computation.7 | async-start | bytes 524288 | tf_op jit(solution)/shard_map/all_to_all | solution.py:274
  18.6 7.5 %all-to-all-done.7 = bf16[8,32,512]{2,1,0:T(8,128)(2,1)S(1)} async-done(((bf16[8,32,512]{2,1,0:T(8,128)(2,1)}), bf16[8,32,512]{2,1,0:T(8,128)(2,1)S(1)}, u32[]{:S(2)}, u32[]{:S(2)}) %all-to-all-start.7) | async-done | bytes 262176 | tf_op jit(solution)/shard_map/all_to_all | solution.py:274
  26.3 0.6 broadcast_in_dim.42
  26.9 3.3 %all-to-all-start.9 = ((f32[8,1,32]{2,1,0:T(1,128)}), f32[8,1,32]{2,1,0:T(1,128)S(1)}, u32[]{:S(2)}, u32[]{:S(2)}) async-start(f32[8,1,32]{2,1,0:T(1,128)} %broadcast_in_dim.42), calls=%async_computation.9 | async-start | bytes 8192 | tf_op jit(solution)/shard_map/all_to_all | solution.py:47
  30.2 0.8 constant_dynamic-slice_fusion
  30.9 4.4 %all-to-all-done.9 = f32[8,1,32]{2,1,0:T(1,128)S(1)} async-done(((f32[8,1,32]{2,1,0:T(1,128)}), f32[8,1,32]{2,1,0:T(1,128)S(1)}, u32[]{:S(2)}, u32[]{:S(2)}) %all-to-all-start.9) | async-done | bytes 1056 | tf_op jit(solution)/shard_map/all_to_all | solution.py:47
  35.3 1.1 broadcast_in_dim.33
  36.4 11.6 %all-to-all-start = ((bf16[32,32,512]{2,1,0:T(8,128)(2,1)}), bf16[32,32,512]{2,1,0:T(8,128)(2,1)S(1)}, u32[]{:S(2)}, u32[]{:S(2)}) async-start(bf16[32,32,512]{2,1,0:T(8,128)(2,1)} %broadcast_in_dim.33), calls=%async_computation | async-start | bytes 2097152 | tf_op jit(solution)/shard_map/all_to_all | solution.py:47
  48.0 28.0 %all-to-all-done = bf16[32,32,512]{2,1,0:T(8,128)(2,1)S(1)} async-done(((bf16[32,32,512]{2,1,0:T(8,128)(2,1)}), bf16[32,32,512]{2,1,0:T(8,128)(2,1)S(1)}, u32[]{:S(2)}, u32[]{:S(2)}) %all-to-all-start) | async-done | bytes 1048608 | tf_op jit(solution)/shard_map/all_to_all | solution.py:47
  76.1 0.6 broadcast_in_dim.43
  76.7 5.7 %all-to-all-start.10 = ((f32[32,1,32]{2,1,0:T(1,128)}), f32[32,1,32]{2,1,0:T(1,128)S(1)}, u32[]{:S(2)}, u32[]{:S(2)}) async-start(f32[32,1,32]{2,1,0:T(1,128)} %broadcast_in_dim.43), calls=%async_computation.10 | async-start | bytes 32768 | tf_op jit(solution)/shard_map/all_to_all | solution.py:47
  82.4 1.1 convolution_bitcast_fusion
  83.5 7.4 %all-to-all-done.10 = f32[32,1,32]{2,1,0:T(1,128)S(1)} async-done(((f32[32,1,32]{2,1,0:T(1,128)}), f32[32,1,32]{2,1,0:T(1,128)S(1)}, u32[]{:S(2)}, u32[]{:S(2)}) %all-to-all-start.10) | async-done | bytes 4128 | tf_op jit(solution)/shard_map/all_to_all | solution.py:47
  90.9 3.4 %all-to-all-start.4 = ((f32[8,32,128]{2,1,0:T(8,128)}), f32[8,32,128]{2,1,0:T(8,128)S(1)}, u32[]{:S(2)}, u32[]{:S(2)}) async-start(f32[8,32,128]{2,1,0:T(8,128)} %convolution_bitcast_fusion), calls=%async_computation.4 | async-start | bytes 262144 | tf_op jit(solution)/shard_map/all_to_all | solution.py:286
  94.3 1.7 convolution_convert_fusion.1
  96.0 4.3 %all-to-all-done.4 = f32[8,32,128]{2,1,0:T(8,128)S(1)} async-done(((f32[8,32,128]{2,1,0:T(8,128)}), f32[8,32,128]{2,1,0:T(8,128)S(1)}, u32[]{:S(2)}, u32[]{:S(2)}) %all-to-all-start.4) | async-done | bytes 131104 | tf_op jit(solution)/shard_map/all_to_all | solution.py:286
  100.3 3.6 %all-to-all-start.1 = ((bf16[8,512,128]{1,2,0:T(8,128)(2,1)}), bf16[8,512,128]{1,2,0:T(8,128)(2,1)S(1)}, u32[]{:S(2)}, u32[]{:S(2)}) async-start(bf16[8,512,128]{1,2,0:T(8,128)(2,1)} %bitcast.9), calls=%async_computation.1 | async-start | bytes 2097152 | tf_op jit(solution)/shard_map/all_to_all | solution.py:294
  103.9 15.8 %all-to-all-done.1 = bf16[8,512,128]{1,2,0:T(8,128)(2,1)S(1)} async-done(((bf16[8,512,128]{1,2,0:T(8,128)(2,1)}), bf16[8,512,128]{1,2,0:T(8,128)(2,1)S(1)}, u32[]{:S(2)}, u32[]{:S(2)}) %all-to-all-start.1) | async-done | bytes 1048608 | tf_op jit(solution)/shard_map/all_to_all | solution.py:294
  119.7 0.9 broadcast_in_dim.36
  120.6 5.0 %all-to-all-start.5 = ((bf16[32,32,256]{2,1,0:T(8,128)(2,1)}), bf16[32,32,256]{2,1,0:T(8,128)(2,1)S(1)}, u32[]{:S(2)}, u32[]{:S(2)}) async-start(bf16[32,32,256]{2,1,0:T(8,128)(2,1)} %broadcast_in_dim.36), calls=%async_computation.5 | async-start | bytes 1048576 | tf_op jit(solution)/shard_map/all_to_all | solution.py:47
  125.6 1.2 reduce-window.6
  127.4 1.8 scatter_custom_fusion
  129.3 13.2 %all-to-all-done.5 = bf16[32,32,256]{2,1,0:T(8,128)(2,1)S(1)} async-done(((bf16[32,32,256]{2,1,0:T(8,128)(2,1)}), bf16[32,32,256]{2,1,0:T(8,128)(2,1)S(1)}, u32[]{:S(2)}, u32[]{:S(2)}) %all-to-all-start.5) | async-done | bytes 524320 | tf_op jit(solution)/shard_map/all_to_all | solution.py:47
  142.5 15.6 %all_to_all.59 = bf16[32,32,128]{2,1,0:T(8,128)(2,1)S(1)} all-to-all(bf16[32,32,128]{2,1,0:T(8,128)(2,1)S(1)} %bitcast.74), channel_id=1, replica_groups=mesh['mp'=8,'rows'=32] {'rows'}, dimensions={0} | all-to-all | bytes 524288 | tf_op jit(solution)/shard_map/all_to_all | solution.py:305
  158.2 27.3 %all_to_all.60.own = bf16[4,1024,256]{2,1,0:T(8,128)(2,1)} all-to-all(bf16[4,1024,256]{2,1,0:T(8,128)(2,1)S(1)} %broadcast_in_dim.38), channel_id=1, replica_groups={{0,64,128,192},{32,96,160,224},{1,65,129,193},{33,97,161,225},{2,66,130..., dimensions={0} | all-to-all | bytes 4194304 | tf_op jit(solution)/shard_map/all_to_all | solution.py:47
  185.5 1.1 broadcast_in_dim.35
  186.6 3.5 %all-to-all-start.3 = ((bf16[4,1024,128]{2,1,0:T(8,128)(2,1)}), bf16[4,1024,128]{2,1,0:T(8,128)(2,1)S(1)}, u32[]{:S(2)}, u32[]{:S(2)}) async-start(bf16[4,1024,128]{2,1,0:T(8,128)(2,1)} %broadcast_in_dim.35), calls=%async_computation.3 | async-start | bytes 2097152 | tf_op jit(solution)/shard_map/all_to_all | solution.py:47
  190.2 11.8 %all-to-all-done.3.own = bf16[4,1024,128]{2,1,0:T(8,128)(2,1)S(1)} async-done(((bf16[4,1024,128]{2,1,0:T(8,128)(2,1)}), bf16[4,1024,128]{2,1,0:T(8,128)(2,1)S(1)}, u32[]{:S(2)}, u32[]{:S(2)}) %all-to-all-start.3) | async-done | bytes 1048608 | tf_op jit(solution)/shard_map/all_to_all | solution.py:47
  202.0 1.1 broadcast_in_dim.41
  203.1 7.6 %all-to-all-start.8 = ((bf16[32,32,512]{2,1,0:T(8,128)(2,1)}), bf16[32,32,512]{2,1,0:T(8,128)(2,1)}, u32[]{:S(2)}, u32[]{:S(2)}) async-start(bf16[32,32,512]{2,1,0:T(8,128)(2,1)} %broadcast_in_dim.41), calls=%async_computation.8 | async-start | bytes 2097152 | tf_op jit(solution)/shard_map/all_to_all | solution.py:47
  210.7 0.3 collective-permute-start
  211.0 0.8 dynamic_slice.11
  211.9 1.3 reshape.340.scale
  213.2 22.4 %all-to-all-done.8 = bf16[32,32,512]{2,1,0:T(8,128)(2,1)} async-done(((bf16[32,32,512]{2,1,0:T(8,128)(2,1)}), bf16[32,32,512]{2,1,0:T(8,128)(2,1)}, u32[]{:S(2)}, u32[]{:S(2)}) %all-to-all-start.8) | async-done | bytes 1048608 | tf_op jit(solution)/shard_map/all_to_all | solution.py:47
  235.6 1.6 copy-done.1
  237.2 1.0 copy-done.2
  238.2 19.3 %shard_map.145.dual_map = bf16[1024,512]{1,0:T(8,128)(2,1)S(1)} custom-call(s32[1]{0:T(128)} %bitcast.core_ref, bf16[4,1024,256]{2,1,0:T(8,128)(2,1)S(1)} %copy-done.1, bf16[4,1024,256]{2,1,0:T(8,128)(2,1)} %collective-permute-done.1.other, bf16[1024,512]{1,0:T(8,128)(2,1)} %bitcast.23.state, f32[1024,1]{1,0:T(8,128)S(1)} %copy-done.2, f32[1,512]{1,0:T(1,128)S(1)} %bitcast.68), custom_call_target="tpu_custom_call" | custom-call | flops 9663676416 | bytes 8388608 | tf_op jit(solution)/shard_map/pallas_call | solution.py:147
  257.6 3.3 %shard_map.146 = bf16[1024,512]{1,0:T(8,128)(2,1)} custom-call(s32[1]{0:T(128)} %bitcast.core_ref, bf16[4,1024,128]{2,1,0:T(8,128)(2,1)S(1)} %all-to-all-done.3.own, bf16[4,1024,128]{2,1,0:T(8,128)(2,1)S(1)} %collective-permute-done.other, bf16[1024,512]{1,0:T(8,128)(2,1)S(1)} %shard_map.145.dual_map), custom_call_target="tpu_custom_call" | custom-call | flops 1073741824 | bytes 8388608 | tf_op jit(solution)/shard_map/pallas_call | solution.py:147
  (56 shorter events, 2.7 us)
Async XLA Ops:
  0.0 2.7 %copy-start = (bf16[4096,128]{1,0:T(8,128)(2,1)S(1)}, bf16[4096,128]{1,0:T(8,128)(2,1)}, u32[]{:S(2)}) copy-start(bf16[4096,128]{1,0:T(8,128)(2,1)} %param.18) | copy-start | bytes 3145732
  0.0 9.7 %copy-start.3 = (bf16[32,4096]{1,0:T(8,128)(2,1)S(1)}, bf16[32,4096]{1,0:T(8,128)(2,1)}, u32[]{:S(2)}) copy-start(bf16[32,4096]{1,0:T(8,128)(2,1)} %param.15) | copy-start | bytes 786436
  0.0 9.7 %copy-start.6 = (f32[4096]{0:T(1024)S(1)}, f32[4096]{0:T(1024)}, u32[]{:S(2)}) copy-start(f32[4096]{0:T(1024)} %param.16) | copy-start | bytes 49156
  0.0 8.6 %copy-start.8 = (f32[128]{0:T(128)S(1)}, f32[128]{0:T(128)}, u32[]{:S(2)}) copy-start(f32[128]{0:T(128)} %param.21) | copy-start | bytes 1540
  0.0 9.1 %copy-start.5 = (bf16[32,32,128]{2,1,0:T(8,128)(2,1)S(1)}, bf16[32,32,128]{2,1,0:T(8,128)(2,1)}, u32[]{:S(2)}) copy-start(bf16[32,32,128]{2,1,0:T(8,128)(2,1)} %param.23) | copy-start | bytes 786436
  0.0 9.7 %copy-start.4 = (bf16[4096,128]{1,0:T(8,128)(2,1)S(1)}, bf16[4096,128]{1,0:T(8,128)(2,1)}, u32[]{:S(2)}) copy-start(bf16[4096,128]{1,0:T(8,128)(2,1)} %param.19) | copy-start | bytes 3145732
  2.7 7.4 %copy-start.10 = (bf16[32,32,128]{2,1,0:T(8,128)(2,1)S(1)}, bf16[32,32,128]{2,1,0:T(8,128)(2,1)}, u32[]{:S(2)}) copy-start(bf16[32,32,128]{2,1,0:T(8,128)(2,1)} %param.24) | copy-start | bytes 786436
  13.4 80.9 %copy-start.9 = (bf16[512,512]{1,0:T(8,128)(2,1)S(1)}, bf16[512,512]{1,0:T(8,128)(2,1)}, u32[]{:S(2)}) copy-start(bf16[512,512]{1,0:T(8,128)(2,1)} %param.28) | copy-start | bytes 1572868
  14.1 12.0 %all-to-all-start.7 = ((bf16[8,32,512]{2,1,0:T(8,128)(2,1)}), bf16[8,32,512]{2,1,0:T(8,128)(2,1)S(1)}, u32[]{:S(2)}, u32[]{:S(2)}) async-start(bf16[8,32,512]{2,1,0:T(8,128)(2,1)} %bitcast.67), calls=%async_computation.7 | async-start | bytes 524288 | tf_op jit(solution)/shard_map/all_to_all | solution.py:274
  26.9 8.5 %all-to-all-start.9 = ((f32[8,1,32]{2,1,0:T(1,128)}), f32[8,1,32]{2,1,0:T(1,128)S(1)}, u32[]{:S(2)}, u32[]{:S(2)}) async-start(f32[8,1,32]{2,1,0:T(1,128)} %broadcast_in_dim.42), calls=%async_computation.9 | async-start | bytes 8192 | tf_op jit(solution)/shard_map/all_to_all | solution.py:47
  36.4 39.7 %all-to-all-start = ((bf16[32,32,512]{2,1,0:T(8,128)(2,1)}), bf16[32,32,512]{2,1,0:T(8,128)(2,1)S(1)}, u32[]{:S(2)}, u32[]{:S(2)}) async-start(bf16[32,32,512]{2,1,0:T(8,128)(2,1)} %broadcast_in_dim.33), calls=%async_computation | async-start | bytes 2097152 | tf_op jit(solution)/shard_map/all_to_all | solution.py:47
  76.7 48.9 %copy-start.7 = (s32[512,1]{0,1:T(1,128)S(1)}, s32[512,1]{0,1:T(1,128)}, u32[]{:S(2)}) copy-start(s32[512,1]{0,1:T(1,128)} %param.29) | copy-start | bytes 6148
  76.7 14.2 %all-to-all-start.10 = ((f32[32,1,32]{2,1,0:T(1,128)}), f32[32,1,32]{2,1,0:T(1,128)S(1)}, u32[]{:S(2)}, u32[]{:S(2)}) async-start(f32[32,1,32]{2,1,0:T(1,128)} %broadcast_in_dim.43), calls=%async_computation.10 | async-start | bytes 32768 | tf_op jit(solution)/shard_map/all_to_all | solution.py:47
  90.9 9.4 %all-to-all-start.4 = ((f32[8,32,128]{2,1,0:T(8,128)}), f32[8,32,128]{2,1,0:T(8,128)S(1)}, u32[]{:S(2)}, u32[]{:S(2)}) async-start(f32[8,32,128]{2,1,0:T(8,128)} %convolution_bitcast_fusion), calls=%async_computation.4 | async-start | bytes 262144 | tf_op jit(solution)/shard_map/all_to_all | solution.py:286
  100.3 19.4 %all-to-all-start.1 = ((bf16[8,512,128]{1,2,0:T(8,128)(2,1)}), bf16[8,512,128]{1,2,0:T(8,128)(2,1)S(1)}, u32[]{:S(2)}, u32[]{:S(2)}) async-start(bf16[8,512,128]{1,2,0:T(8,128)(2,1)} %bitcast.9), calls=%async_computation.1 | async-start | bytes 2097152 | tf_op jit(solution)/shard_map/all_to_all | solution.py:294
  120.6 21.9 %all-to-all-start.5 = ((bf16[32,32,256]{2,1,0:T(8,128)(2,1)}), bf16[32,32,256]{2,1,0:T(8,128)(2,1)S(1)}, u32[]{:S(2)}, u32[]{:S(2)}) async-start(bf16[32,32,256]{2,1,0:T(8,128)(2,1)} %broadcast_in_dim.36), calls=%async_computation.5 | async-start | bytes 1048576 | tf_op jit(solution)/shard_map/all_to_all | solution.py:47
  186.6 15.4 %all-to-all-start.3 = ((bf16[4,1024,128]{2,1,0:T(8,128)(2,1)}), bf16[4,1024,128]{2,1,0:T(8,128)(2,1)S(1)}, u32[]{:S(2)}, u32[]{:S(2)}) async-start(bf16[4,1024,128]{2,1,0:T(8,128)(2,1)} %broadcast_in_dim.35), calls=%async_computation.3 | async-start | bytes 2097152 | tf_op jit(solution)/shard_map/all_to_all | solution.py:47
  190.1 45.5 %collective-permute-start.1 = (bf16[4,1024,256]{2,1,0:T(8,128)(2,1)}, bf16[4,1024,256]{2,1,0:T(8,128)(2,1)}, u32[]{:S(2)}, u32[]{:S(2)}) collective-permute-start(bf16[4,1024,256]{2,1,0:T(8,128)(2,1)} %all_to_all.60.own), channel_id=1, source_target_pairs={{0,32},{32,0},{64,96},{96,64},{128,160},{160,128},{192,224},{224,1... | collective-permute-start | bytes 6291464 | tf_op jit(solution)/shard_map/ppermute | solution.py:54
  203.1 32.5 %all-to-all-start.8 = ((bf16[32,32,512]{2,1,0:T(8,128)(2,1)}), bf16[32,32,512]{2,1,0:T(8,128)(2,1)}, u32[]{:S(2)}, u32[]{:S(2)}) async-start(bf16[32,32,512]{2,1,0:T(8,128)(2,1)} %broadcast_in_dim.41), calls=%async_computation.8 | async-start | bytes 2097152 | tf_op jit(solution)/shard_map/all_to_all | solution.py:47
  210.7 46.8 %collective-permute-start = (bf16[4,1024,128]{2,1,0:T(8,128)(2,1)S(1)}, bf16[4,1024,128]{2,1,0:T(8,128)(2,1)S(1)}, u32[]{:S(2)}, u32[]{:S(2)}) collective-permute-start(bf16[4,1024,128]{2,1,0:T(8,128)(2,1)S(1)} %all-to-all-done.3.own), channel_id=1, source_target_pairs={{0,32},{32,0},{64,96},{96,64},{128,160},{160,128},{192,224},{224,1... | collective-permute-start | bytes 3145736 | tf_op jit(solution)/shard_map/ppermute | solution.py:54
  235.6 1.6 copy-start.1
  237.2 1.0 copy-start.2

commit v2 on v1

--- a/solution.py
+++ b/solution.py
@@ -6,6 +6,7 @@
 from jax.experimental import pallas as pl
 from jax.experimental.pallas import tpu as pltpu
 from jax.sharding import PartitionSpec as P
+
 
 D = 4096
 HEADS = 32
@@ -47,32 +48,60 @@
     return lax.all_to_all(copies, axis, 0, 0, tiled=True, axis_index_groups=groups)
 
 
-def spread_mp(block):
-    size = lax.axis_size("mp")
-    groups = [list(range(core, size, 2)) for core in range(2)]
-    own = spread(block, "mp", size // 2, groups)
-    return own, lax.ppermute(own, "mp", [(i, i ^ 1) for i in range(size)])
+def ring(block, axis, count, size, stride):
+    def move(array, step):
+        pairs = []
+        for i in range(size):
+            at = i // stride % count
+            pairs.append((i, i + ((at + step) % count - at) * stride))
+        return lax.ppermute(array, axis, pairs)
+
+    below, above = [block], [block]
+    for _ in range(count // 2 - 1):
+        below.append(move(below[-1], 1))
+        above.append(move(above[-1], -1))
+    middle = block.shape[0] // 2
+    far = [move(below[-1][:middle], 1), move(above[-1][middle:], -1)]
+    far = jnp.concatenate(far, axis=0)
+    return above + [far] + below[:0:-1]
+
+
+def swap_cores(block, size):
+    return lax.ppermute(block, "mp", [(i, i ^ 1) for i in range(size)])
+
+
+def halves(array):
+    high = lax.reduce_precision(array, 8, 7)
+    return high.astype(jnp.bfloat16), (array - high).astype(jnp.bfloat16)
+
+
+def norm_rows(squares, width):
+    high, low = halves(squares)
+    line = jnp.concatenate([high, low])
+    return jnp.pad(line[None, :], ((0, 15), (0, width - line.shape[0])))
 
 
 def tiles(body, init=0):
     return lax.fori_loop(0, 1024 // TILE, body, init)
 
 
-def place(core, own, other, target, start):
-    for y in range(own.shape[0]):
+def place(here, own, other, target, start, rows):
+    core, chip = here[0], here[1]
+    for step in range(own.shape[0]):
+        at_chip = lax.rem(chip + step, own.shape[0])
         for part, at in ((own, core), (other, 1 - core)):
-            first = pl.multiple_of((2 * y + at) * 128, 128)
-            target[:, pl.ds(first, 128)] = part[y, :, start : start + 128]
+            first = pl.multiple_of((2 * at_chip + at) * 128, 128)
+            value = part[step, :, start : start + rows, :]
+            target[:, pl.ds(first, 128)] = value.reshape(target.shape[0], 128)
 
 
 def solve_kernel(
-    core_ref, own, other, state, scale, gain, result,
+    here, own, other, state, scale, gain, result,
     high, low, rho, rho_high, rho_low, image, way, way_image, total,
 ):
-    core = core_ref[0]
     ridge = 0.125 * D
-    place(core, own, other, high, 0)
-    place(core, own, other, low, 128)
+    place(here, own, other, high, 0, own.shape[2] // 2)
+    place(here, own, other, low, own.shape[2] // 2, own.shape[2] // 2)
 
     def rows_of(i):
         return pl.ds(pl.multiple_of(i * TILE, TILE), TILE)
@@ -169,8 +198,8 @@
     )
 
 
-def apply_kernel(core_ref, own, other, dual_map, result, routed):
-    place(core_ref[0], own, other, routed, 0)
+def apply_kernel(here, own, other, dual_map, result, routed):
+    place(here, own, other, routed, 0, own.shape[2])
 
     def rows_of(i):
         return pl.ds(pl.multiple_of(i * TILE, TILE), TILE)
@@ -186,7 +215,7 @@
 
 def apply_map(*operands):
     anchors, cols = operands[3].shape
-    slots = operands[1].shape[1]
+    slots = operands[1].shape[1] * operands[1].shape[2]
     return call(
         apply_kernel,
         jax.ShapeDtypeStruct((slots, cols), jnp.bfloat16),
@@ -266,34 +295,58 @@
         + own_weight.astype(jnp.float32)[..., None] * value_new.astype(jnp.float32)[:, :, None, :]
     )
     attended = attended.reshape(docs, kv_local * group * HEAD).astype(jnp.bfloat16)
-    partial_value = jnp.dot(attended, w_output, preferred_element_type=jnp.float32)
-    mine = lax.axis_index("mp") * cols
-    core = lax.axis_index("mp") % 2
+    partial_value = lax.optimization_barrier(
+        jnp.dot(attended, w_output, preferred_element_type=jnp.float32)
+    )
+    place_mp = lax.axis_index("mp")
+    mine = place_mp * cols
+    core, chip = place_mp % 2, place_mp // 2
+    chips = mp_count // 2
     my_cols = lambda array, axis: lax.dynamic_slice_in_dim(array, mine, cols, axis)
-    pieces = partial_value.astype(jnp.bfloat16).reshape(docs, mp_count, cols).transpose(1, 0, 2)
-    pieces = lax.all_to_all(pieces, "mp", 0, 0, tiled=True)
-    state = my_cols(hidden32, 1) + jnp.sum(pieces.astype(jnp.float32), axis=0)
-    squares = jnp.sum(state * state, axis=-1)[None, :]
-    squares = jnp.sum(spread(squares, "mp", mp_count), axis=0)
-    scale_rows = lax.rsqrt(spread(squares, "rows", rows_count) / width + 1e-06)
-    state_all = spread(state.astype(jnp.bfloat16), "rows", rows_count)
+    half = jnp.bfloat16
+
+    def shift_chips(block, step):
+        return lax.ppermute(
+            block, "mp", [(i, (i + 2 * step) % mp_count) for i in range(mp_count)]
+        )
+
+    pieces = partial_value.reshape(docs, chips, 2, cols)
+    theirs = lax.dynamic_index_in_dim(pieces, 1 - core, 2, False).astype(half)
+    pieces = lax.dynamic_index_in_dim(pieces, core, 2, False)
+    pieces = pieces + swap_cores(theirs, mp_count).astype(jnp.float32)
+    state = my_cols(hidden32, 1) + lax.dynamic_index_in_dim(pieces, chip, 1, False)
+    pieces = pieces.astype(half)
+    for step in range(1, chips):
+        piece = lax.dynamic_index_in_dim(pieces, (chip + step) % chips, 1, False)
+        state = state + shift_chips(piece, step).astype(jnp.float32)
+    squares = jnp.sum(state * state, axis=-1)
 
     old_mine = my_cols(old_embed, 1)
     old_all = spread(old_mine, "rows", rows_count).reshape(rows_count * docs, cols)
     anchors = rows_count * docs
     part = anchors // mp_count
-    gram_part = contract_last(old_mine, old_all).reshape(docs, mp_count, part).transpose(1, 0, 2)
-    gram_part = jnp.sum(lax.all_to_all(gram_part, "mp", 0, 0, tiled=True), axis=0)
-    high = lax.reduce_precision(gram_part, 8, 7)
-    gram_part = jnp.concatenate([high, gram_part - high], axis=1).astype(jnp.bfloat16)
-    gram = spread(gram_part, "rows", rows_count).reshape(anchors, 2 * part)
-    gram_own, gram_other = spread_mp(gram)
-
-    slab_part = contract_last(slab, old_all).astype(jnp.bfloat16)
-    slab_part = slab_part.reshape(-1, mp_count, part).transpose(1, 0, 2)
-    slab_part = lax.all_to_all(slab_part, "mp", 0, 0, tiled=True)
-    slab_dual = jnp.sum(slab_part.astype(jnp.float32), axis=0).astype(jnp.bfloat16)
-    capacity = 2 * slab.shape[0] // rows_count
+
+    def by_part(array):
+        return array.reshape(-1, mp_count, part).transpose(1, 0, 2)
+
+    gram_part = by_part(contract_last(old_mine, old_all))
+    slab_part = by_part(contract_last(slab, old_all).astype(half))
+    count = slab.shape[0]
+    head = count + 2 * docs
+    outgoing = jnp.concatenate(
+        [
+            slab_part,
+            *halves(gram_part),
+            jnp.broadcast_to(norm_rows(squares, part)[None], (mp_count, 16, part)),
+        ],
+        axis=1,
+    )
+    summed = jnp.sum(lax.all_to_all(outgoing, "mp", 0, 0, tiled=True).astype(jnp.float32), axis=0)
+    slab_dual = summed[:count].astype(half)
+    gram_part = summed[count : count + docs] + summed[count + docs : head]
+    squares = summed[head, :docs] + summed[head, docs : 2 * docs]
+
+    capacity = 2 * count // rows_count
     owner_ids = owners[:, 0]
     onehot = (owner_ids[:, None] == jnp.arange(rows_count, dtype=jnp.int32)[None, :]).astype(
         jnp.int32
@@ -301,20 +354,42 @@
     counted = jnp.cumsum(onehot, axis=0)
     slot = jnp.sum((counted - 1) * onehot, axis=-1)
     target = owner_ids * capacity + slot
-    outgoing = jnp.zeros((rows_count * capacity, part), jnp.bfloat16).at[target].set(slab_dual)
-    routed = lax.all_to_all(outgoing, "rows", split_axis=0, concat_axis=0, tiled=True)
-    routed_own, routed_other = spread_mp(routed)
-
-    core = core.astype(jnp.int32).reshape(1)
+    routed = jnp.zeros((rows_count * capacity, part), half).at[target].set(slab_dual)
+    shared = jnp.concatenate([*halves(gram_part), norm_rows(squares, part)], axis=0)
+    outgoing = jnp.concatenate(
+        [
+            routed.reshape(rows_count, capacity, part),
+            jnp.broadcast_to(shared[None], (rows_count,) + shared.shape),
+        ],
+        axis=1,
+    )
+    arrived = lax.all_to_all(outgoing, "rows", split_axis=0, concat_axis=0, tiled=True)
+    routed = arrived[:, :capacity]
+    gram = arrived[:, capacity : capacity + 2 * docs]
+    squares = arrived[:, capacity + 2 * docs].astype(jnp.float32)
+    squares = squares[:, :docs] + squares[:, docs : 2 * docs]
+    scale_rows = lax.rsqrt(squares / width + 1e-06).reshape(anchors, 1)
+
+    state, _ = lax.optimization_barrier((state.astype(half), arrived))
+    state_all = spread(state, "rows", rows_count)
+    gram_own = jnp.stack(ring(gram, "mp", chips, mp_count, 2))
+    gram_other = swap_cores(gram_own, mp_count)
+    routed, _ = lax.optimization_barrier((routed, state_all))
+    routed_own = spread(
+        routed, "mp", chips, [list(range(at, mp_count, 2)) for at in range(2)]
+    )
+    routed_other = swap_cores(routed_own, mp_count)
+
+    here = jnp.stack([core, chip]).astype(jnp.int32)
     dual_map = solve(
-        core,
+        here,
         gram_own,
         gram_other,
         state_all.reshape(anchors, cols),
-        scale_rows.reshape(anchors, 1),
+        scale_rows,
         my_cols(final_gain, 0).reshape(1, cols),
     )
-    return apply_map(core, routed_own, routed_other, dual_map)
+    return apply_map(here * jnp.array([1, 0], jnp.int32), routed_own, routed_other, dual_map)
 
 
 def solution(mesh):

time: 262 us -> 187 us (0.71)
  waiting for transfers between devices: 115 us -> 50.9 us
  blocking collectives: 42.9 us -> 31.6 us
  starting transfers between devices: 48.5 us -> 37.9 us
  other arithmetic: 6.09 us -> 10.2 us
  local copies, waits for them, and re-layouts: 14 us -> 17.6 us
    all_to_all x6 -> x3, waiting for transfers between devices: 87.2 us -> 24.1 us  [spread(): lax.all_to_all(copies, axis, 0, 0, tiled=True, axis_index_groups=groups)]
    all_to_all x1 -> x0, blocking collectives: 27.3 us -> none  [spread(): lax.all_to_all(copies, axis, 0, 0, tiled=True, axis_index_groups=groups)]
    all_to_all x1, blocking collectives: 15.6 us -> 31.6 us  [local(): lax.all_to_all(outgoing, 'rows', split_axis=0, concat_axis=0, tiled=True)]
    all_to_all x6 -> x3, starting transfers between devices: 36.7 us -> 20.8 us  [spread(): lax.all_to_all(copies, axis, 0, 0, tiled=True, axis_index_groups=groups)]
    ppermute x2 -> x10, starting transfers between devices: 0.37 us -> 12.6 us  [the longest x4 6.61 us: move(): return lax.ppermute(array, axis, pairs)]
    all_to_all x3 -> x1, waiting for transfers between devices: 27.6 us -> 16.1 us  [local(): lax.all_to_all(outgoing, 'mp', 0, 0, tiled=True).astype(jnp.float32)]
    ppermute x2 -> x10, waiting for transfers between devices: 0.01 us -> 10.7 us  [the longest x4 7.22 us: move(): return lax.ppermute(array, axis, pairs)]
    all_to_all x3 -> x1, starting transfers between devices: 11.4 us -> 4.47 us  [local(): lax.all_to_all(outgoing, 'mp', 0, 0, tiled=True).astype(jnp.float32)]
  transfers between devices with their start and end apart: 11 -> 14, of which waited for: 9 -> 10; matrix products, arithmetic and copies ran while one was open for 4% -> 15% of each run, Pallas kernels for 7% -> 11%
where the time goes in v2:
time: 187 us; the launch traced here: 184 us
  waiting for transfers between devices  50.9 us (27%)
  starting transfers between devices  37.9 us (20%)
  blocking collectives  31.6 us (17%)
  Pallas kernels  23.6 us (13%)
  local copies, waits for them, and re-layouts  17.6 us (9%)
  matrix products  12 us (6%)
  other arithmetic  10.2 us (5%)
    all_to_all x1, blocking collectives, local(): lax.all_to_all(outgoing, 'rows', split_axis=0, concat_axis=0, tiled=True)  31.6 us
    all_to_all x3, waiting for transfers between devices, spread(): lax.all_to_all(copies, axis, 0, 0, tiled=True, axis_index_groups=groups)  24.1 us
    pallas_call x2, Pallas kernels, call(): pl.pallas_call(kernel, out_shape=out_shape, in_specs=[pl.BlockSpec(memory...  23.6 us
    all_to_all x3, starting transfers between devices, spread(): lax.all_to_all(copies, axis, 0, 0, tiled=True, axis_index_groups=groups)  20.8 us
    all_to_all x1, waiting for transfers between devices, local(): lax.all_to_all(outgoing, 'mp', 0, 0, tiled=True).astype(jnp.float32)  16.1 us
    ppermute x4, waiting for transfers between devices, move(): return lax.ppermute(array, axis, pairs)  7.22 us
    ppermute x4, starting transfers between devices, move(): return lax.ppermute(array, axis, pairs)  6.61 us
    ppermute x3, starting transfers between devices, shift_chips(): lax.ppermute(block, 'mp', [(i, (i + 2 * step) % mp_count) for i in range(...  5.9 us
  transfers between devices with their start and end apart: 14, of which 10 were waited for; matrix products, arithmetic and copies ran while one was open for 15% of the time, Pallas kernels for 11%

profile of v2, /device:TPU:2, one launch (start us, length us, event | category | flops | bytes accessed | tf_op | source)
XLA Modules:
  0.0 184.3 jit_solution(10188135191759158578)
XLA Ops:
  0.0 0.9 constant_dynamic-slice_fusion.2
  0.9 1.1 broadcast_in_dim.29
  2.0 11.7 %all-to-all-start = ((bf16[32,32,512]{2,1,0:T(8,128)(2,1)}), bf16[32,32,512]{2,1,0:T(8,128)(2,1)S(1)}, u32[]{:S(2)}, u32[]{:S(2)}) async-start(bf16[32,32,512]{2,1,0:T(8,128)(2,1)} %broadcast_in_dim.29), calls=%async_computation | async-start | bytes 2097152 | tf_op jit(solution)/shard_map/all_to_all | solution.py:48
  13.8 0.7 iota_compare_fusion.3
  15.3 0.8 fusion.38
  16.1 3.8 %fusion.43 = f32[32,512]{1,0:T(8,128)} fusion(bf16[4096,512]{1,0:T(8,128)(2,1)} %param.18, f32[4096]{0:T(1024)S(1)} %copy-done.8, f32[32]{0:T(128)S(1)} %add_rsqrt_fusion.2, bf16[32,4096]{1,0:T(8,128)(2,1)S(1)} %copy-done.4), kind=kOutput, calls=%fused_computation.110 | convolution fusion | flops 134742016 | bytes 4538496 | tf_op jit(solution)/shard_map/dot_general | solution.py:259
  19.9 0.9 reshape.304
  20.9 1.0 fusion.2
  21.9 0.8 maximum_bitcast_fusion.1
  22.7 0.8 multiply_multiply_fusion
  23.8 1.1 fusion.50
  25.4 3.0 %fusion.17 = f32[32,4096]{1,0:T(8,128)S(1)} fusion(bf16[512,4096]{1,0:T(8,128)(2,1)} %param.21, bf16[4,8,4,128]{3,2,1,0:T(4,128)(2,1)S(1)} %bitcast.103), kind=kOutput, calls=%fused_computation.50 | convolution fusion | flops 134217728 | bytes 4751360 | tf_op jit(solution)/shard_map/dot_general | solution.py:299
  29.7 1.0 collective-permute-done
  30.8 1.7 collective-permute-start.1
  32.4 2.9 %collective-permute-start.2 = (bf16[32,512]{1,0:T(8,128)(2,1)S(1)}, bf16[32,512]{1,0:T(8,128)(2,1)S(1)}, u32[]{:S(2)}, u32[]{:S(2)}) collective-permute-start(bf16[32,512]{1,0:T(8,128)(2,1)S(1)} %get-tuple-element.27), channel_id=1, source_target_pairs={{0,128},{32,160},{64,192},{96,224},{128,0},{160,32},{192,64},{224,... | collective-permute-start | bytes 98312 | tf_op jit(solution)/shard_map/ppermute | solution.py:309
  35.3 1.3 collective-permute-start.3
  36.7 1.1 collective-permute-done.2
  37.9 1.4 collective-permute-done.3
  39.5 2.3 %all-to-all-done = bf16[32,32,512]{2,1,0:T(8,128)(2,1)S(1)} async-done(((bf16[32,32,512]{2,1,0:T(8,128)(2,1)}), bf16[32,32,512]{2,1,0:T(8,128)(2,1)S(1)}, u32[]{:S(2)}, u32[]{:S(2)}) %all-to-all-start) | async-done | bytes 1048608 | tf_op jit(solution)/shard_map/all_to_all | solution.py:48
  42.2 1.8 convolution_convert_fusion
  44.0 0.7 copy.36
  44.7 1.1 pad_maximum_fusion.1
  45.8 4.5 %all-to-all-start.1 = ((bf16[8,592,128]{2,1,0:T(8,128)(2,1)}), bf16[8,592,128]{2,1,0:T(8,128)(2,1)S(1)}, u32[]{:S(2)}, u32[]{:S(2)}) async-start(bf16[8,592,128]{2,1,0:T(8,128)(2,1)} %pad_maximum_fusion.1), calls=%async_computation.1 | async-start | bytes 2424832 | tf_op jit(solution)/shard_map/all_to_all | solution.py:344
  50.3 1.2 reduce-window.6
  51.9 16.1 %all-to-all-done.1 = bf16[8,592,128]{2,1,0:T(8,128)(2,1)S(1)} async-done(((bf16[8,592,128]{2,1,0:T(8,128)(2,1)}), bf16[8,592,128]{2,1,0:T(8,128)(2,1)S(1)}, u32[]{:S(2)}, u32[]{:S(2)}) %all-to-all-start.1) | async-done | bytes 1212448 | tf_op jit(solution)/shard_map/all_to_all | solution.py:344
  69.4 1.8 scatter_custom_fusion
  71.5 31.6 %all_to_all.25 = bf16[32,112,128]{2,1,0:T(8,128)(2,1)S(1)} all-to-all(bf16[32,112,128]{2,1,0:T(8,128)(2,1)S(1)} %pad_maximum_fusion.2), channel_id=1, replica_groups=mesh['mp'=8,'rows'=32] {'rows'}, dimensions={0} | all-to-all | bytes 1835008 | tf_op jit(solution)/shard_map/all_to_all | solution.py:366
  103.1 1.2 slice_bitcast_fusion
  104.9 2.7 %collective-permute-start.5 = (bf16[32,64,128]{2,1,0:T(8,128)(2,1)}, bf16[32,64,128]{2,1,0:T(8,128)(2,1)}, u32[]{:S(2)}, u32[]{:S(2)}) collective-permute-start(bf16[32,64,128]{2,1,0:T(8,128)(2,1)} %get-tuple-element.16), channel_id=1, source_target_pairs={{0,192},{32,224},{64,0},{96,32},{128,64},{160,96},{192,128},{224,1... | collective-permute-start | bytes 1572872 | tf_op jit(solution)/shard_map/ppermute | solution.py:57
  107.5 1.1 broadcast_in_dim.36
  108.6 5.6 %all-to-all-start.3 = ((bf16[32,32,512]{2,1,0:T(8,128)(2,1)}), bf16[32,32,512]{2,1,0:T(8,128)(2,1)S(1)}, u32[]{:S(2)}, u32[]{:S(2)}) async-start(bf16[32,32,512]{2,1,0:T(8,128)(2,1)} %broadcast_in_dim.36), calls=%async_computation.3 | async-start | bytes 2097152 | tf_op jit(solution)/shard_map/all_to_all | solution.py:48
  114.2 3.3 %collective-permute-done.6 = bf16[32,64,128]{2,1,0:T(8,128)(2,1)} collective-permute-done((bf16[32,64,128]{2,1,0:T(8,128)(2,1)}, bf16[32,64,128]{2,1,0:T(8,128)(2,1)}, u32[]{:S(2)}, u32[]{:S(2)}) %collective-permute-start.6) | collective-permute-done | bytes 524320 | tf_op jit(solution)/shard_map/ppermute | solution.py:57
  117.5 1.0 slice.85
  118.6 1.0 slice.86
  119.6 3.3 %collective-permute-start.8 = (bf16[16,64,128]{2,1,0:T(8,128)(2,1)S(1)}, bf16[16,64,128]{2,1,0:T(8,128)(2,1)S(1)}, u32[]{:S(2)}, u32[]{:S(2)}) collective-permute-start(bf16[16,64,128]{2,1,0:T(8,128)(2,1)S(1)} %slice.86), channel_id=1, source_target_pairs={{0,192},{32,224},{64,0},{96,32},{128,64},{160,96},{192,128},{224,1... | collective-permute-start | bytes 786440 | tf_op jit(solution)/shard_map/ppermute | solution.py:57
  122.9 3.3 %collective-permute-done.7 = bf16[16,64,128]{2,1,0:T(8,128)(2,1)S(1)} collective-permute-done((bf16[16,64,128]{2,1,0:T(8,128)(2,1)S(1)}, bf16[16,64,128]{2,1,0:T(8,128)(2,1)S(1)}, u32[]{:S(2)}, u32[]{:S(2)}) %collective-permute-start.7) | collective-permute-done | bytes 262176 | tf_op jit(solution)/shard_map/ppermute | solution.py:57
  126.2 0.6 collective-permute-done.8
  126.8 2.8 %pad_maximum_fusion.own = bf16[4,32,64,128]{3,2,1,0:T(8,128)(2,1)} fusion(bf16[1,32,64,128]{3,2,1,0:T(8,128)(2,1)} %bitcast.32, bf16[1,32,64,128]{3,2,1,0:T(8,128)(2,1)S(1)} %maximum_bitcast_fusion, bf16[1,32,64,128]{3,2,1,0:T(8,128)(2,1)} %bitcast.30, bf16[1,32,64,128]{3,2,1,0:T(8,128)(2,1)S(1)} %copy-done.5), kind=kLoop, calls=%fused_computation.2 | loop fusion | flops 3145728 | bytes 4194304 | tf_op jit(solution)/shard_map/stack | solution.py:375
  129.6 10.8 %all-to-all-done.3 = bf16[32,32,512]{2,1,0:T(8,128)(2,1)S(1)} async-done(((bf16[32,32,512]{2,1,0:T(8,128)(2,1)}), bf16[32,32,512]{2,1,0:T(8,128)(2,1)S(1)}, u32[]{:S(2)}, u32[]{:S(2)}) %all-to-all-start.3) | async-done | bytes 1048608 | tf_op jit(solution)/shard_map/all_to_all | solution.py:48
  140.5 1.3 broadcast_in_dim.37
  141.8 3.5 %all-to-all-start.4 = ((bf16[4,32,32,128]{3,2,1,0:T(8,128)(2,1)}), bf16[4,32,32,128]{3,2,1,0:T(8,128)(2,1)S(1)}, u32[]{:S(2)}, u32[]{:S(2)}) async-start(bf16[4,32,32,128]{3,2,1,0:T(8,128)(2,1)} %broadcast_in_dim.37), calls=%async_computation.4 | async-start | bytes 2097152 | tf_op jit(solution)/shard_map/all_to_all | solution.py:48
  145.3 0.8 dynamic_slice.38
  146.2 10.9 %all-to-all-done.4.own = bf16[4,32,32,128]{3,2,1,0:T(8,128)(2,1)S(1)} async-done(((bf16[4,32,32,128]{3,2,1,0:T(8,128)(2,1)}), bf16[4,32,32,128]{3,2,1,0:T(8,128)(2,1)S(1)}, u32[]{:S(2)}, u32[]{:S(2)}) %all-to-all-start.4) | async-done | bytes 1048608 | tf_op jit(solution)/shard_map/all_to_all | solution.py:48
  157.2 1.3 reshape.322.scale
  158.5 1.2 copy-done.2
  159.7 1.0 copy-done.3
  160.8 19.7 %shard_map.154.dual_map = bf16[1024,512]{1,0:T(8,128)(2,1)S(1)} custom-call(s32[2]{0:T(128)S(1)} %get-tuple-element.14.here, bf16[4,32,64,128]{3,2,1,0:T(8,128)(2,1)} %pad_maximum_fusion.own, bf16[4,32,64,128]{3,2,1,0:T(8,128)(2,1)} %collective-permute-done.9.other, bf16[1024,512]{1,0:T(8,128)(2,1)S(1)} %bitcast.92, f32[1024,1]{1,0:T(8,128)S(1)} %copy-done.3, ...), custom_call_target="tpu_custom_call" | custom-call | flops 9663676416 | bytes 8388608 | tf_op jit(solution)/shard_map/pallas_call | solution.py:176
  180.5 3.9 %shard_map.155 = bf16[1024,512]{1,0:T(8,128)(2,1)} custom-call(s32[2]{0:T(128)S(1)} %get-tuple-element.13.here, bf16[4,32,32,128]{3,2,1,0:T(8,128)(2,1)S(1)} %all-to-all-done.4.own, bf16[4,32,32,128]{3,2,1,0:T(8,128)(2,1)S(1)} %collective-permute-done.4.other, bf16[1024,512]{1,0:T(8,128)(2,1)S(1)} %shard_map.154.dual_map), custom_call_target="tpu_custom_call" | custom-call | flops 1073741824 | bytes 8388608 | tf_op jit(solution)/shard_map/pallas_call | solution.py:176
  (97 shorter events, 6.6 us)
Async XLA Ops:
  0.0 14.6 %copy-start = (bf16[4096,128]{1,0:T(8,128)(2,1)S(1)}, bf16[4096,128]{1,0:T(8,128)(2,1)}, u32[]{:S(2)}) copy-start(bf16[4096,128]{1,0:T(8,128)(2,1)} %param.19) | copy-start | bytes 3145732
  0.0 13.8 %copy-start.12 = (s32[32]{0:T(128)S(1)}, s32[32]{0:T(128)}, u32[]{:S(2)}) copy-start(s32[32]{0:T(128)} %param.26) | copy-start | bytes 388
  0.0 14.4 %copy-start.4 = (bf16[32,4096]{1,0:T(8,128)(2,1)S(1)}, bf16[32,4096]{1,0:T(8,128)(2,1)}, u32[]{:S(2)}) copy-start(bf16[32,4096]{1,0:T(8,128)(2,1)} %param.16) | copy-start | bytes 786436
  0.0 14.6 %copy-start.8 = (f32[4096]{0:T(1024)S(1)}, f32[4096]{0:T(1024)}, u32[]{:S(2)}) copy-start(f32[4096]{0:T(1024)} %param.17) | copy-start | bytes 49156
  2.0 13.3 %copy-start.11 = (f32[128]{0:T(128)S(1)}, f32[128]{0:T(128)}, u32[]{:S(2)}) copy-start(f32[128]{0:T(128)} %param.23) | copy-start | bytes 1540
  2.0 39.8 %all-to-all-start = ((bf16[32,32,512]{2,1,0:T(8,128)(2,1)}), bf16[32,32,512]{2,1,0:T(8,128)(2,1)S(1)}, u32[]{:S(2)}, u32[]{:S(2)}) async-start(bf16[32,32,512]{2,1,0:T(8,128)(2,1)} %broadcast_in_dim.29), calls=%async_computation | async-start | bytes 2097152 | tf_op jit(solution)/shard_map/all_to_all | solution.py:48
  14.6 1.5 copy-start.10
  16.1 4.8 %copy-start.6 = (bf16[4096,128]{1,0:T(8,128)(2,1)S(1)}, bf16[4096,128]{1,0:T(8,128)(2,1)}, u32[]{:S(2)}) copy-start(bf16[4096,128]{1,0:T(8,128)(2,1)} %param.20) | copy-start | bytes 3145732
  20.7 3.1 %copy-start.7 = (bf16[32,32,128]{2,1,0:T(8,128)(2,1)S(1)}, bf16[32,32,128]{2,1,0:T(8,128)(2,1)}, u32[]{:S(2)}) copy-start(bf16[32,32,128]{2,1,0:T(8,128)(2,1)} %param.24) | copy-start | bytes 786436
  20.8 4.4 %copy-start.14 = (bf16[32,32,128]{2,1,0:T(8,128)(2,1)S(1)}, bf16[32,32,128]{2,1,0:T(8,128)(2,1)}, u32[]{:S(2)}) copy-start(bf16[32,32,128]{2,1,0:T(8,128)(2,1)} %param.25) | copy-start | bytes 786436
  29.2 1.4 collective-permute-start
  30.8 6.0 %collective-permute-start.1 = (bf16[32,512]{1,0:T(8,128)(2,1)S(1)}, bf16[32,512]{1,0:T(8,128)(2,1)S(1)}, u32[]{:S(2)}, u32[]{:S(2)}) collective-permute-start(bf16[32,512]{1,0:T(8,128)(2,1)S(1)} %get-tuple-element.25), channel_id=1, source_target_pairs={{0,64},{32,96},{64,128},{96,160},{128,192},{160,224},{192,0},{224,... | collective-permute-start | bytes 98312 | tf_op jit(solution)/shard_map/ppermute | solution.py:309
  32.4 5.4 %collective-permute-start.2 = (bf16[32,512]{1,0:T(8,128)(2,1)S(1)}, bf16[32,512]{1,0:T(8,128)(2,1)S(1)}, u32[]{:S(2)}, u32[]{:S(2)}) collective-permute-start(bf16[32,512]{1,0:T(8,128)(2,1)S(1)} %get-tuple-element.27), channel_id=1, source_target_pairs={{0,128},{32,160},{64,192},{96,224},{128,0},{160,32},{192,64},{224,... | collective-permute-start | bytes 98312 | tf_op jit(solution)/shard_map/ppermute | solution.py:309
  35.3 3.9 %collective-permute-start.3 = (bf16[32,512]{1,0:T(8,128)(2,1)S(1)}, bf16[32,512]{1,0:T(8,128)(2,1)S(1)}, u32[]{:S(2)}, u32[]{:S(2)}) collective-permute-start(bf16[32,512]{1,0:T(8,128)(2,1)S(1)} %get-tuple-element.26), channel_id=1, source_target_pairs={{0,192},{32,224},{64,0},{96,32},{128,64},{160,96},{192,128},{224,1... | collective-permute-start | bytes 98312 | tf_op jit(solution)/shard_map/ppermute | solution.py:309
  44.7 5.6 %copy-start.9 = (s32[512,1]{0,1:T(1,128)S(1)}, s32[512,1]{0,1:T(1,128)}, u32[]{:S(2)}) copy-start(s32[512,1]{0,1:T(1,128)} %param.30) | copy-start | bytes 6148
  45.8 22.2 %all-to-all-start.1 = ((bf16[8,592,128]{2,1,0:T(8,128)(2,1)}), bf16[8,592,128]{2,1,0:T(8,128)(2,1)S(1)}, u32[]{:S(2)}, u32[]{:S(2)}) async-start(bf16[8,592,128]{2,1,0:T(8,128)(2,1)} %pad_maximum_fusion.1), calls=%async_computation.1 | async-start | bytes 2424832 | tf_op jit(solution)/shard_map/all_to_all | solution.py:344
  104.3 13.2 %collective-permute-start.6 = (bf16[32,64,128]{2,1,0:T(8,128)(2,1)}, bf16[32,64,128]{2,1,0:T(8,128)(2,1)}, u32[]{:S(2)}, u32[]{:S(2)}) collective-permute-start(bf16[32,64,128]{2,1,0:T(8,128)(2,1)} %get-tuple-element.16), channel_id=1, source_target_pairs={{0,64},{32,96},{64,128},{96,160},{128,192},{160,224},{192,0},{224,... | collective-permute-start | bytes 1572872 | tf_op jit(solution)/shard_map/ppermute | solution.py:57
  104.9 13.7 %collective-permute-start.5 = (bf16[32,64,128]{2,1,0:T(8,128)(2,1)}, bf16[32,64,128]{2,1,0:T(8,128)(2,1)}, u32[]{:S(2)}, u32[]{:S(2)}) collective-permute-start(bf16[32,64,128]{2,1,0:T(8,128)(2,1)} %get-tuple-element.16), channel_id=1, source_target_pairs={{0,192},{32,224},{64,0},{96,32},{128,64},{160,96},{192,128},{224,1... | collective-permute-start | bytes 1572872 | tf_op jit(solution)/shard_map/ppermute | solution.py:57
  108.6 31.9 %all-to-all-start.3 = ((bf16[32,32,512]{2,1,0:T(8,128)(2,1)}), bf16[32,32,512]{2,1,0:T(8,128)(2,1)S(1)}, u32[]{:S(2)}, u32[]{:S(2)}) async-start(bf16[32,32,512]{2,1,0:T(8,128)(2,1)} %broadcast_in_dim.36), calls=%async_computation.3 | async-start | bytes 2097152 | tf_op jit(solution)/shard_map/all_to_all | solution.py:48
  114.2 12.6 %copy-start.5 = (bf16[1,32,64,128]{3,2,1,0:T(8,128)(2,1)S(1)}, bf16[1,32,64,128]{3,2,1,0:T(8,128)(2,1)}, u32[]{:S(2)}) copy-start(bf16[1,32,64,128]{3,2,1,0:T(8,128)(2,1)} %get-tuple-element.15) | copy-start | bytes 1572868
  118.5 7.7 %collective-permute-start.7 = (bf16[16,64,128]{2,1,0:T(8,128)(2,1)S(1)}, bf16[16,64,128]{2,1,0:T(8,128)(2,1)S(1)}, u32[]{:S(2)}, u32[]{:S(2)}) collective-permute-start(bf16[16,64,128]{2,1,0:T(8,128)(2,1)S(1)} %slice.85), channel_id=1, source_target_pairs={{0,64},{32,96},{64,128},{96,160},{128,192},{160,224},{192,0},{224,... | collective-permute-start | bytes 786440 | tf_op jit(solution)/shard_map/ppermute | solution.py:57
  119.6 7.2 %collective-permute-start.8 = (bf16[16,64,128]{2,1,0:T(8,128)(2,1)S(1)}, bf16[16,64,128]{2,1,0:T(8,128)(2,1)S(1)}, u32[]{:S(2)}, u32[]{:S(2)}) collective-permute-start(bf16[16,64,128]{2,1,0:T(8,128)(2,1)S(1)} %slice.86), channel_id=1, source_target_pairs={{0,192},{32,224},{64,0},{96,32},{128,64},{160,96},{192,128},{224,1... | collective-permute-start | bytes 786440 | tf_op jit(solution)/shard_map/ppermute | solution.py:57
  129.6 16.5 %copy-start.13 = (s32[2]{0:T(128)S(1)}, s32[2]{0:T(128)}, u32[]{:S(2)}) copy-start(s32[2]{0:T(128)} %constant.119.clone) | copy-start | bytes 28
  129.6 28.9 %collective-permute-start.9 = (bf16[4,32,64,128]{3,2,1,0:T(8,128)(2,1)}, bf16[4,32,64,128]{3,2,1,0:T(8,128)(2,1)}, u32[]{:S(2)}, u32[]{:S(2)}) collective-permute-start(bf16[4,32,64,128]{3,2,1,0:T(8,128)(2,1)} %pad_maximum_fusion.own), channel_id=1, source_target_pairs={{0,32},{32,0},{64,96},{96,64},{128,160},{160,128},{192,224},{224,1... | collective-permute-start | bytes 6291464 | tf_op jit(solution)/shard_map/ppermute | solution.py:70
  140.5 1.3 copy-start.1
  141.8 15.3 %all-to-all-start.4 = ((bf16[4,32,32,128]{3,2,1,0:T(8,128)(2,1)}), bf16[4,32,32,128]{3,2,1,0:T(8,128)(2,1)S(1)}, u32[]{:S(2)}, u32[]{:S(2)}) async-start(bf16[4,32,32,128]{3,2,1,0:T(8,128)(2,1)} %broadcast_in_dim.37), calls=%async_computation.4 | async-start | bytes 2097152 | tf_op jit(solution)/shard_map/all_to_all | solution.py:48
  157.1 23.4 %collective-permute-start.4 = (bf16[4,32,32,128]{3,2,1,0:T(8,128)(2,1)S(1)}, bf16[4,32,32,128]{3,2,1,0:T(8,128)(2,1)S(1)}, u32[]{:S(2)}, u32[]{:S(2)}) collective-permute-start(bf16[4,32,32,128]{3,2,1,0:T(8,128)(2,1)S(1)} %all-to-all-done.4.own), channel_id=1, source_target_pairs={{0,32},{32,0},{64,96},{96,64},{128,160},{160,128},{192,224},{224,1... | collective-permute-start | bytes 3145736 | tf_op jit(solution)/shard_map/ppermute | solution.py:70
  158.5 1.2 copy-start.2
  159.7 1.0 copy-start.3

commit v3 on v2

--- a/solution.py
+++ b/solution.py
@@ -62,8 +62,7 @@
         above.append(move(above[-1], -1))
     middle = block.shape[0] // 2
     far = [move(below[-1][:middle], 1), move(above[-1][middle:], -1)]
-    far = jnp.concatenate(far, axis=0)
-    return above + [far] + below[:0:-1]
+    return above + below[:0:-1] + far
 
 
 def swap_cores(block, size):
@@ -85,23 +84,23 @@
     return lax.fori_loop(0, 1024 // TILE, body, init)
 
 
-def place(here, own, other, target, start, rows):
-    core, chip = here[0], here[1]
-    for step in range(own.shape[0]):
-        at_chip = lax.rem(chip + step, own.shape[0])
-        for part, at in ((own, core), (other, 1 - core)):
-            first = pl.multiple_of((2 * at_chip + at) * 128, 128)
-            value = part[step, :, start : start + rows, :]
-            target[:, pl.ds(first, 128)] = value.reshape(target.shape[0], 128)
-
-
-def solve_kernel(
-    here, own, other, state, scale, gain, result,
-    high, low, rho, rho_high, rho_low, image, way, way_image, total,
-):
+def put(block, target, place, row=0):
+    first = pl.multiple_of(place * 128, 128)
+    value = block.reshape(block.shape[0] * block.shape[1], 128)
+    target[row : row + value.shape[0], pl.ds(first, 128)] = value
+
+
+def solve_kernel(here, scale, gain, *refs):
+    states, grams, result = refs[:4], refs[4:14], refs[14]
+    high, low, rho, rho_high, rho_low, image, way, way_image, total = refs[15:]
     ridge = 0.125 * D
-    place(here, own, other, high, 0, own.shape[2] // 2)
-    place(here, own, other, low, own.shape[2] // 2, own.shape[2] // 2)
+    for index, piece in enumerate(grams):
+        step, row = ((0, 0), (1, 0), (3, 0), (2, 0), (2, 512))[index % 5]
+        side = here[0] if index < 5 else 1 - here[0]
+        at = 2 * lax.rem(here[1] + step, 4) + side
+        docs = piece.shape[1] // 2
+        put(piece[:, :docs, :], high, at, row)
+        put(piece[:, docs:, :], low, at, row)
 
     def rows_of(i):
         return pl.ds(pl.multiple_of(i * TILE, TILE), TILE)
@@ -112,14 +111,11 @@
         rho_high[rows, :] = top
         rho_low[rows, :] = (value - top.astype(jnp.float32)).astype(jnp.bfloat16)
 
-    def start(i, carry):
-        rows = rows_of(i)
-        value = state[rows, :].astype(jnp.float32) * scale[rows, :] * gain[...]
+    for step, state in enumerate(states):
+        rows = rows_of(lax.rem(here[2] + step, 4))
+        value = state[...].astype(jnp.float32) * scale[rows, :] * gain[...]
         split(rows, value)
         way[rows, :] = value
-        return carry
-
-    tiles(start)
 
     def dot(left, right):
         return jnp.dot(left, right, preferred_element_type=jnp.float32)
@@ -131,7 +127,7 @@
         image[rows, :] = value
         return square + jnp.sum(rho[rows, :] * value, axis=0, keepdims=True)
 
-    zero = jnp.zeros((1, state.shape[1]), jnp.float32)
+    zero = jnp.zeros((1, rho.shape[1]), jnp.float32)
     res_sq = tiles(product, zero)
     ratio = zero
     for sweep in range(ITERS):
@@ -180,12 +176,12 @@
         out_specs=vmem,
         scratch_shapes=scratch,
         cost_estimate=pl.CostEstimate(flops=flops, bytes_accessed=1 << 23, transcendentals=0),
-        compiler_params=pltpu.CompilerParams(vmem_limit_bytes=40 << 20),
+        compiler_params=pltpu.CompilerParams(vmem_limit_bytes=32 << 20),
     )(*operands)
 
 
 def solve(*operands):
-    anchors, cols = operands[3].shape
+    anchors, cols = operands[1].shape[0], operands[2].shape[1]
     wide = pltpu.VMEM((anchors, anchors), jnp.bfloat16)
     full = pltpu.VMEM((anchors, cols), jnp.float32)
     half = pltpu.VMEM((anchors, cols), jnp.bfloat16)
@@ -199,7 +195,9 @@
 
 
 def apply_kernel(here, own, other, dual_map, result, routed):
-    place(here, own, other, routed, 0, own.shape[2])
+    for y in range(own.shape[0]):
+        put(own[y], routed, 2 * y + here[0])
+        put(other[y], routed, 2 * y + 1 - here[0])
 
     def rows_of(i):
         return pl.ds(pl.multiple_of(i * TILE, TILE), TILE)
@@ -259,16 +257,16 @@
     query = jnp.dot(normed, w_query, preferred_element_type=jnp.float32).reshape(
         docs, kv_local * group, HEAD
     )
-    query = rotate(head_norm(query, query_gain), position).astype(jnp.bfloat16)
     key_new = jnp.dot(normed, w_key, preferred_element_type=jnp.float32).reshape(
         docs, kv_local, HEAD
     )
-    key_new = rotate(head_norm(key_new, key_gain), position).astype(jnp.bfloat16)
     value_new = (
         jnp.dot(normed, w_value, preferred_element_type=jnp.float32)
         .reshape(docs, kv_local, HEAD)
         .astype(jnp.bfloat16)
     )
+    query = rotate(head_norm(query, query_gain), position).astype(jnp.bfloat16)
+    key_new = rotate(head_norm(key_new, key_gain), position).astype(jnp.bfloat16)
     query_groups = query.reshape(docs, kv_local, group, HEAD)
     keys = key_cache.reshape(docs, key_cache.shape[1], kv_local, HEAD)
     values = value_cache.reshape(docs, value_cache.shape[1], kv_local, HEAD)
@@ -321,30 +319,53 @@
         state = state + shift_chips(piece, step).astype(jnp.float32)
     squares = jnp.sum(state * state, axis=-1)
 
+    line = 4
+    column = rows_count // line
+    by_z = [[x + line * z for z in range(column)] for x in range(line)]
+    by_x = [[x + line * z for x in range(line)] for z in range(column)]
+    by_y = [list(range(at, mp_count, 2)) for at in range(2)]
     old_mine = my_cols(old_embed, 1)
-    old_all = spread(old_mine, "rows", rows_count).reshape(rows_count * docs, cols)
+    old_all = spread(old_mine, "rows", column, by_z)
+    old_all = spread(old_all, "rows", line, by_x)
     anchors = rows_count * docs
     part = anchors // mp_count
+    old_all = old_all.reshape(anchors, cols)
 
     def by_part(array):
         return array.reshape(-1, mp_count, part).transpose(1, 0, 2)
 
     gram_part = by_part(contract_last(old_mine, old_all))
+    gram_part = lax.all_to_all(gram_part, "mp", 0, 0, tiled=True)
+    gram = jnp.concatenate(halves(jnp.sum(gram_part, axis=0)), axis=0)
+    gram = spread(gram, "rows", column, by_z)
+    gram = spread(gram, "rows", line, by_x)
+    gram = gram.reshape(rows_count, 2 * docs, part)
+
+    count = slab.shape[0]
     slab_part = by_part(contract_last(slab, old_all).astype(half))
-    count = slab.shape[0]
-    head = count + 2 * docs
-    outgoing = jnp.concatenate(
-        [
-            slab_part,
-            *halves(gram_part),
-            jnp.broadcast_to(norm_rows(squares, part)[None], (mp_count, 16, part)),
-        ],
-        axis=1,
-    )
-    summed = jnp.sum(lax.all_to_all(outgoing, "mp", 0, 0, tiled=True).astype(jnp.float32), axis=0)
-    slab_dual = summed[:count].astype(half)
-    gram_part = summed[count : count + docs] + summed[count + docs : head]
-    squares = summed[head, :docs] + summed[head, docs : 2 * docs]
+    slab_part = slab_part.reshape(chips, 2, count, part)
+    theirs = lax.dynamic_index_in_dim(slab_part, 1 - core, 1, False)
+    slab_part = lax.dynamic_index_in_dim(slab_part, core, 1, False).astype(jnp.float32)
+    theirs, others = jnp.split(
+        swap_cores(
+            jnp.concatenate(
+                [theirs.reshape(chips * count, part), norm_rows(squares, part)], axis=0
+            ),
+            mp_count,
+        ).astype(jnp.float32),
+        [chips * count],
+    )
+    slab_part = slab_part + theirs.reshape(chips, count, part)
+    squares = squares + others[0, :docs] + others[0, docs : 2 * docs]
+    slab_dual = lax.dynamic_index_in_dim(slab_part, chip, 0, False)
+    slab_part = slab_part.astype(half)
+    pair_rows = norm_rows(squares, part)
+    for step in range(1, chips):
+        piece = lax.dynamic_index_in_dim(slab_part, (chip + step) % chips, 0, False)
+        piece = shift_chips(jnp.concatenate([piece, pair_rows], axis=0), step)
+        piece = piece.astype(jnp.float32)
+        slab_dual = slab_dual + piece[:count]
+        squares = squares + piece[count, :docs] + piece[count, docs : 2 * docs]
 
     capacity = 2 * count // rows_count
     owner_ids = owners[:, 0]
@@ -354,42 +375,40 @@
     counted = jnp.cumsum(onehot, axis=0)
     slot = jnp.sum((counted - 1) * onehot, axis=-1)
     target = owner_ids * capacity + slot
-    routed = jnp.zeros((rows_count * capacity, part), half).at[target].set(slab_dual)
-    shared = jnp.concatenate([*halves(gram_part), norm_rows(squares, part)], axis=0)
+    routed = jnp.zeros((rows_count * capacity, part), half).at[target].set(slab_dual.astype(half))
     outgoing = jnp.concatenate(
         [
             routed.reshape(rows_count, capacity, part),
-            jnp.broadcast_to(shared[None], (rows_count,) + shared.shape),
+            jnp.broadcast_to(norm_rows(squares, part)[None], (rows_count, 16, part)),
         ],
         axis=1,
     )
+
+    state, gram = lax.optimization_barrier((state.astype(half), gram))
+    state_column = spread(state, "rows", column, by_z)
+    outgoing, state_column = lax.optimization_barrier((outgoing, state_column))
     arrived = lax.all_to_all(outgoing, "rows", split_axis=0, concat_axis=0, tiled=True)
+    states = [state_column.reshape(anchors // line, cols)]
+    for step in range(1, line):
+        pairs = [(i, i // line * line + (i - step) % line) for i in range(rows_count)]
+        states.append(lax.ppermute(states[0], "rows", pairs))
     routed = arrived[:, :capacity]
-    gram = arrived[:, capacity : capacity + 2 * docs]
-    squares = arrived[:, capacity + 2 * docs].astype(jnp.float32)
+    squares = arrived[:, capacity].astype(jnp.float32)
     squares = squares[:, :docs] + squares[:, docs : 2 * docs]
+    squares = squares.reshape(column, line, docs).transpose(1, 0, 2)
     scale_rows = lax.rsqrt(squares / width + 1e-06).reshape(anchors, 1)
 
-    state, _ = lax.optimization_barrier((state.astype(half), arrived))
-    state_all = spread(state, "rows", rows_count)
-    gram_own = jnp.stack(ring(gram, "mp", chips, mp_count, 2))
-    gram_other = swap_cores(gram_own, mp_count)
-    routed, _ = lax.optimization_barrier((routed, state_all))
-    routed_own = spread(
-        routed, "mp", chips, [list(range(at, mp_count, 2)) for at in range(2)]
-    )
+    grams = ring(gram, "mp", chips, mp_count, 2)
+    grams = grams + [swap_cores(piece, mp_count) for piece in grams]
+    routed_own = spread(routed, "mp", chips, by_y)
     routed_other = swap_cores(routed_own, mp_count)
 
-    here = jnp.stack([core, chip]).astype(jnp.int32)
+    zero = jnp.zeros_like(core)
+    here = jnp.stack([core, chip, lax.axis_index("rows") % line, zero]).astype(jnp.int32)
     dual_map = solve(
-        here,
-        gram_own,
-        gram_other,
-        state_all.reshape(anchors, cols),
-        scale_rows,
-        my_cols(final_gain, 0).reshape(1, cols),
-    )
-    return apply_map(here * jnp.array([1, 0], jnp.int32), routed_own, routed_other, dual_map)
+        here, scale_rows, my_cols(final_gain, 0).reshape(1, cols), *states, *grams
+    )
+    return apply_map(here, routed_own, routed_other, dual_map)
 
 
 def solution(mesh):

time: 187 us -> 190 us (1.016)
  the two profiles are of different devices: /device:TPU:2 before, /device:TPU:1 now
where the time goes in v3:
time: 190 us; the launch traced here: 188 us
  starting transfers between devices  73.5 us (39%)
  waiting for transfers between devices  44.1 us (23%)
  Pallas kernels  23.2 us (12%)
  local copies, waits for them, and re-layouts  21.8 us (11%)
  other arithmetic  13.5 us (7%)
  matrix products  11.7 us (6%)
    all_to_all x6, waiting for transfers between devices, spread(): lax.all_to_all(copies, axis, 0, 0, tiled=True, axis_index_groups=groups)  32.3 us
    all_to_all x6, starting transfers between devices, spread(): lax.all_to_all(copies, axis, 0, 0, tiled=True, axis_index_groups=groups)  25.7 us
    pallas_call x2, Pallas kernels, call(): pl.pallas_call(kernel, out_shape=out_shape, in_specs=[pl.BlockSpec(memory...  23.2 us
    ppermute x8, starting transfers between devices, swap_cores(): return lax.ppermute(block, 'mp', [(i, i ^ 1) for i in range(size)])  18.1 us
    ppermute x6, starting transfers between devices, shift_chips(): lax.ppermute(block, 'mp', [(i, (i + 2 * step) % mp_count) for i in range(...  8.25 us
    unnamed x35, local copies, waits for them, and re-layouts  7.97 us
    ppermute x4, starting transfers between devices, move(): return lax.ppermute(array, axis, pairs)  6.38 us
    all_to_all x1, starting transfers between devices, local(): gram_part = lax.all_to_all(gram_part, 'mp', 0, 0, tiled=True)  6.07 us
  transfers between devices with their start and end apart: 29, of which 8 were waited for; matrix products, arithmetic and copies ran while one was open for 11% of the time, Pallas kernels for 10%

profile of v3, /device:TPU:1, one launch (start us, length us, event | category | flops | bytes accessed | tf_op | source)
XLA Modules:
  0.0 188.2 jit_solution(10891792222609559735)
XLA Ops:
  1.6 1.1 multiply_reduce_fusion
  2.7 1.4 multiply_reduce_fusion.3
  5.2 3.2 %fusion.57 = f32[32,512]{1,0:T(8,128)S(1)} fusion(bf16[4096,512]{1,0:T(8,128)(2,1)} %param.17, f32[4096]{0:T(1024)} %param.16, f32[32]{0:T(128)S(1)} %add_rsqrt_fusion.2, bf16[32,4096]{1,0:T(8,128)(2,1)} %param.15), kind=kOutput, calls=%fused_computation.137 | convolution fusion | flops 134742016 | bytes 4538496 | tf_op jit(solution)/shard_map/dot_general | solution.py:257
  10.4 3.0 %fusion.21 = f32[32,4096]{1,0:T(8,128)S(1)} fusion(bf16[512,4096]{1,0:T(8,128)(2,1)} %param.20, bf16[4,8,4,128]{3,2,1,0:T(4,128)(2,1)S(1)} %bitcast.181), kind=kOutput, calls=%fused_computation.53 | convolution fusion | flops 134217728 | bytes 4751360 | tf_op jit(solution)/shard_map/dot_general | solution.py:297
  14.2 3.3 %collective-permute-start = (bf16[32,4,512]{2,0,1:T(8,128)(2,1)S(1)}, bf16[32,4,512]{2,0,1:T(8,128)(2,1)S(1)}, u32[]{:S(2)}, u32[]{:S(2)}) collective-permute-start(bf16[32,4,512]{2,0,1:T(8,128)(2,1)S(1)} %bitcast.177), channel_id=1, source_target_pairs={{0,32},{32,0},{64,96},{96,64},{128,160},{160,128},{192,224},{224,1... | collective-permute-start | bytes 393224 | tf_op jit(solution)/shard_map/ppermute | solution.py:69
  19.0 6.5 %all-to-all-start = ((bf16[8,32,512]{2,1,0:T(8,128)(2,1)}), bf16[8,32,512]{2,1,0:T(8,128)(2,1)S(1)}, u32[]{:S(2)}, u32[]{:S(2)}) async-start(bf16[8,32,512]{2,1,0:T(8,128)(2,1)} %broadcast_in_dim.35), calls=%async_computation | async-start | bytes 524288 | tf_op jit(solution)/shard_map/all_to_all | solution.py:48
  25.9 1.4 collective-permute-start.1
  27.2 2.6 %collective-permute-start.2 = (bf16[32,512]{1,0:T(8,128)(2,1)S(1)}, bf16[32,512]{1,0:T(8,128)(2,1)S(1)}, u32[]{:S(2)}, u32[]{:S(2)}) collective-permute-start(bf16[32,512]{1,0:T(8,128)(2,1)S(1)} %get-tuple-element.30), channel_id=1, source_target_pairs={{0,128},{32,160},{64,192},{96,224},{128,0},{160,32},{192,64},{224,... | collective-permute-start | bytes 98312 | tf_op jit(solution)/shard_map/ppermute | solution.py:307
  29.9 1.1 collective-permute-start.3
  30.9 6.9 %all-to-all-done = bf16[8,32,512]{2,1,0:T(8,128)(2,1)S(1)} async-done(((bf16[8,32,512]{2,1,0:T(8,128)(2,1)}), bf16[8,32,512]{2,1,0:T(8,128)(2,1)S(1)}, u32[]{:S(2)}, u32[]{:S(2)}) %all-to-all-start) | async-done | bytes 262176 | tf_op jit(solution)/shard_map/all_to_all | solution.py:48
  37.8 1.1 broadcast_in_dim.36
  38.9 4.0 %all-to-all-start.1 = ((bf16[4,8,32,512]{3,2,1,0:T(8,128)(2,1)}), bf16[4,8,32,512]{3,2,1,0:T(8,128)(2,1)S(1)}, u32[]{:S(2)}, u32[]{:S(2)}) async-start(bf16[4,8,32,512]{3,2,1,0:T(8,128)(2,1)} %broadcast_in_dim.36), calls=%async_computation.1 | async-start | bytes 2097152 | tf_op jit(solution)/shard_map/all_to_all | solution.py:48
  43.0 1.2 reduce-window.6
  44.4 13.0 %all-to-all-done.1 = bf16[4,8,32,512]{3,2,1,0:T(8,128)(2,1)S(1)} async-done(((bf16[4,8,32,512]{3,2,1,0:T(8,128)(2,1)}), bf16[4,8,32,512]{3,2,1,0:T(8,128)(2,1)S(1)}, u32[]{:S(2)}, u32[]{:S(2)}) %all-to-all-start.1) | async-done | bytes 1048608 | tf_op jit(solution)/shard_map/all_to_all | solution.py:48
  57.4 1.8 convolution_convert_fusion
  60.1 1.3 copy.43
  61.4 1.1 convolution_bitcast_fusion
  62.4 6.1 %all-to-all-start.2 = ((f32[8,32,128]{2,1,0:T(8,128)}), f32[8,32,128]{2,1,0:T(8,128)S(1)}, u32[]{:S(2)}, u32[]{:S(2)}) async-start(f32[8,32,128]{2,1,0:T(8,128)} %convolution_bitcast_fusion), calls=%async_computation.2 | async-start | bytes 262144 | tf_op jit(solution)/shard_map/all_to_all | solution.py:338
  69.3 4.4 %all-to-all-done.2 = f32[8,32,128]{2,1,0:T(8,128)S(1)} async-done(((f32[8,32,128]{2,1,0:T(8,128)}), f32[8,32,128]{2,1,0:T(8,128)S(1)}, u32[]{:S(2)}, u32[]{:S(2)}) %all-to-all-start.2) | async-done | bytes 131104 | tf_op jit(solution)/shard_map/all_to_all | solution.py:338
  74.5 3.4 %all-to-all-start.3 = ((bf16[8,64,128]{2,1,0:T(8,128)(2,1)}), bf16[8,64,128]{2,1,0:T(8,128)(2,1)S(1)}, u32[]{:S(2)}, u32[]{:S(2)}) async-start(bf16[8,64,128]{2,1,0:T(8,128)(2,1)} %broadcast_in_dim.43), calls=%async_computation.3 | async-start | bytes 262144 | tf_op jit(solution)/shard_map/all_to_all | solution.py:48
  79.2 6.3 %all-to-all-done.3 = bf16[8,64,128]{2,1,0:T(8,128)(2,1)S(1)} async-done(((bf16[8,64,128]{2,1,0:T(8,128)(2,1)}), bf16[8,64,128]{2,1,0:T(8,128)(2,1)S(1)}, u32[]{:S(2)}, u32[]{:S(2)}) %all-to-all-start.3) | async-done | bytes 131104 | tf_op jit(solution)/shard_map/all_to_all | solution.py:48
  86.4 3.5 %all-to-all-start.4 = ((bf16[4,8,64,128]{3,2,1,0:T(8,128)(2,1)}), bf16[4,8,64,128]{3,2,1,0:T(8,128)(2,1)S(1)}, u32[]{:S(2)}, u32[]{:S(2)}) async-start(bf16[4,8,64,128]{3,2,1,0:T(8,128)(2,1)} %broadcast_in_dim.44), calls=%async_computation.4 | async-start | bytes 1048576 | tf_op jit(solution)/shard_map/all_to_all | solution.py:48
  90.0 2.2 %fusion.61 = (bf16[4,512,128]{2,1,0:T(8,128)(2,1)S(1)}, f32[4,512,128]{2,1,0:T(8,128)}) fusion(f32[4,512,128]{2,1,0:T(8,128)S(1)} %bitcast.170, bf16[4,1,512,128]{3,2,0,1:T(8,128)(2,1)} %copy.42), kind=kLoop, calls=%fused_computation.139 | loop fusion | flops 786432 | bytes 3145728 | tf_op jit(solution)/shard_map/convert_element_type | solution.py:361
  92.8 1.8 collective-permute-start.6
  94.6 1.0 collective-permute-start.7
  95.6 3.8 %collective-permute-done.5 = bf16[528,128]{1,0:T(8,128)(2,1)S(1)} collective-permute-done((bf16[528,128]{1,0:T(8,128)(2,1)S(1)}, bf16[528,128]{1,0:T(8,128)(2,1)S(1)}, u32[]{:S(2)}, u32[]{:S(2)}) %collective-permute-start.5) | collective-permute-done | bytes 135200 | tf_op jit(solution)/shard_map/ppermute | solution.py:307
  100.7 3.4 %all-to-all-start.5 = ((bf16[8,32,512]{2,1,0:T(8,128)(2,1)}), bf16[8,32,512]{2,1,0:T(8,128)(2,1)S(1)}, u32[]{:S(2)}, u32[]{:S(2)}) async-start(bf16[8,32,512]{2,1,0:T(8,128)(2,1)} %broadcast_in_dim.45), calls=%async_computation.5 | async-start | bytes 524288 | tf_op jit(solution)/shard_map/all_to_all | solution.py:48
  104.3 2.3 %scatter_custom_fusion = bf16[1024,128]{1,0:T(8,128)(2,1)S(1)} fusion(s32[512]{0:T(512)S(1)} %bitcast.185, f32[528,128]{1,0:T(8,128)S(1)} %convert_element_type.166, f32[528,128]{1,0:T(8,128)S(1)} %convert_element_type.165, f32[528,128]{1,0:T(8,128)S(1)} %convert_element_type.164, f32[4,512,128]{2,1,0:T(8,128)} %get-tuple-element.18, s32[]{:T(128)S(6)} %select_n.85, ...), kind=kCustom, calls=%fused_computation.28 | custom fusion | flops 262144 | bytes 1311748 | tf_op jit(solution)/shard_map/scatter | solution.py:378
  107.4 6.2 %all-to-all-done.5 = bf16[8,32,512]{2,1,0:T(8,128)(2,1)S(1)} async-done(((bf16[8,32,512]{2,1,0:T(8,128)(2,1)}), bf16[8,32,512]{2,1,0:T(8,128)(2,1)S(1)}, u32[]{:S(2)}, u32[]{:S(2)}) %all-to-all-start.5) | async-done | bytes 262176 | tf_op jit(solution)/shard_map/all_to_all | solution.py:48
  113.6 4.5 %all-to-all-start.6 = ((bf16[32,48,128]{2,1,0:T(8,128)(2,1)}), bf16[32,48,128]{2,1,0:T(8,128)(2,1)S(1)}, u32[]{:S(2)}, u32[]{:S(2)}) async-start(bf16[32,48,128]{2,1,0:T(8,128)(2,1)} %pad_maximum_fusion), calls=%async_computation.6 | async-start | bytes 786432 | tf_op jit(solution)/shard_map/all_to_all | solution.py:390
  118.7 3.1 %collective-permute-start.12 = (bf16[32,64,128]{2,1,0:T(8,128)(2,1)S(1)}, bf16[32,64,128]{2,1,0:T(8,128)(2,1)}, u32[]{:S(2)}, u32[]{:S(2)}) collective-permute-start(bf16[32,64,128]{2,1,0:T(8,128)(2,1)S(1)} %bitcast.162), channel_id=1, source_target_pairs={{0,192},{32,224},{64,0},{96,32},{128,64},{160,96},{192,128},{224,1... | collective-permute-start | bytes 1572872 | tf_op jit(solution)/shard_map/ppermute | solution.py:57
  121.8 4.7 %collective-permute-start.16 = (bf16[32,64,128]{2,1,0:T(8,128)(2,1)S(1)}, bf16[32,64,128]{2,1,0:T(8,128)(2,1)S(1)}, u32[]{:S(2)}, u32[]{:S(2)}) collective-permute-start(bf16[32,64,128]{2,1,0:T(8,128)(2,1)S(1)} %bitcast.163), channel_id=1, source_target_pairs={{0,32},{32,0},{64,96},{96,64},{128,160},{160,128},{192,224},{224,1... | collective-permute-start | bytes 1572872 | tf_op jit(solution)/shard_map/ppermute | solution.py:69
  126.5 3.1 %all-to-all-done.6 = bf16[32,48,128]{2,1,0:T(8,128)(2,1)S(1)} async-done(((bf16[32,48,128]{2,1,0:T(8,128)(2,1)}), bf16[32,48,128]{2,1,0:T(8,128)(2,1)S(1)}, u32[]{:S(2)}, u32[]{:S(2)}) %all-to-all-start.6) | async-done | bytes 393248 | tf_op jit(solution)/shard_map/all_to_all | solution.py:390
  129.6 1.1 broadcast_in_dim.46
  130.7 4.9 %all-to-all-start.7 = ((bf16[4,32,32,128]{3,2,1,0:T(8,128)(2,1)}), bf16[4,32,32,128]{3,2,1,0:T(8,128)(2,1)S(1)}, u32[]{:S(2)}, u32[]{:S(2)}) async-start(bf16[4,32,32,128]{3,2,1,0:T(8,128)(2,1)} %broadcast_in_dim.46), calls=%async_computation.7 | async-start | bytes 2097152 | tf_op jit(solution)/shard_map/all_to_all | solution.py:48
  135.6 1.8 collective-permute-start.10
  137.7 1.7 slice.114
  139.4 1.5 collective-permute-start.14
  140.9 1.7 slice.115
  142.5 1.2 collective-permute-start.15
  144.5 2.4 %collective-permute-start.9 = (bf16[256,512]{1,0:T(8,128)(2,1)S(1)}, bf16[256,512]{1,0:T(8,128)(2,1)S(1)}, u32[]{:S(2)}, u32[]{:S(2)}) collective-permute-start(bf16[256,512]{1,0:T(8,128)(2,1)S(1)} %bitcast.167), channel_id=1, source_target_pairs={{0,3},{1,0},{2,1},{3,2},{4,7},{5,4},{6,5},{7,6},{8,11},{9,8},{10,9... | collective-permute-start | bytes 786440 | tf_op jit(solution)/shard_map/ppermute | solution.py:394
  146.9 6.3 %collective-permute-start.17 = (bf16[32,64,128]{2,1,0:T(8,128)(2,1)}, bf16[32,64,128]{2,1,0:T(8,128)(2,1)}, u32[]{:S(2)}, u32[]{:S(2)}) collective-permute-start(bf16[32,64,128]{2,1,0:T(8,128)(2,1)} %collective-permute-done.12.refs_5_), channel_id=1, source_target_pairs={{0,32},{32,0},{64,96},{96,64},{128,160},{160,128},{192,224},{224,1... | collective-permute-start | bytes 1572872 | tf_op jit(solution)/shard_map/ppermute | solution.py:69
  154.2 3.2 %collective-permute-start.19 = (bf16[16,64,128]{2,1,0:T(8,128)(2,1)}, bf16[16,64,128]{2,1,0:T(8,128)(2,1)}, u32[]{:S(2)}, u32[]{:S(2)}) collective-permute-start(bf16[16,64,128]{2,1,0:T(8,128)(2,1)} %collective-permute-done.14.refs_7_), channel_id=1, source_target_pairs={{0,32},{32,0},{64,96},{96,64},{128,160},{160,128},{192,224},{224,1... | collective-permute-start | bytes 786440 | tf_op jit(solution)/shard_map/ppermute | solution.py:69
  159.6 1.3 reshape.349.scale
  162.0 1.0 copy-done.3
  163.0 1.0 copy-done.5
  165.0 19.3 %shard_map.145.dual_map = bf16[1024,512]{1,0:T(8,128)(2,1)S(1)} custom-call(s32[4]{0:T(128)S(1)} %pad_add_fusion.here, f32[1024,1]{1,0:T(8,128)S(1)} %copy-done.3, f32[1,512]{1,0:T(1,128)S(1)} %bitcast.169, bf16[256,512]{1,0:T(8,128)(2,1)S(1)} %bitcast.168, bf16[256,512]{1,0:T(8,128)(2,1)S(1)} %copy-done.7, ...), custom_call_target="tpu_custom_call" | custom-call | flops 9663676416 | bytes 8388608 | tf_op jit(solution)/shard_map/pallas_call | solution.py:172
  184.4 3.9 %shard_map.146 = bf16[1024,512]{1,0:T(8,128)(2,1)} custom-call(s32[4]{0:T(128)S(1)} %pad_add_fusion.here, bf16[4,32,32,128]{3,2,1,0:T(8,128)(2,1)S(1)} %all-to-all-done.7.own, bf16[4,32,32,128]{3,2,1,0:T(8,128)(2,1)S(1)} %collective-permute-done.8.other, bf16[1024,512]{1,0:T(8,128)(2,1)S(1)} %shard_map.145.dual_map), custom_call_target="tpu_custom_call" | custom-call | flops 1073741824 | bytes 8388608 | tf_op jit(solution)/shard_map/pallas_call | solution.py:172
  (130 shorter events, 21.8 us)
Async XLA Ops:
  0.0 2.7 %copy-start = (bf16[4096,128]{1,0:T(8,128)(2,1)S(1)}, bf16[4096,128]{1,0:T(8,128)(2,1)}, u32[]{:S(2)}) copy-start(bf16[4096,128]{1,0:T(8,128)(2,1)} %param.18) | copy-start | bytes 3145732
  0.0 9.7 %copy-start.8 = (bf16[32,4096]{1,0:T(8,128)(2,1)S(1)}, bf16[32,4096]{1,0:T(8,128)(2,1)}, u32[]{:S(2)}) copy-start(bf16[32,4096]{1,0:T(8,128)(2,1)} %param.15) | copy-start | bytes 786436
  0.0 9.7 %copy-start.12 = (f32[4096]{0:T(1024)S(1)}, f32[4096]{0:T(1024)}, u32[]{:S(2)}) copy-start(f32[4096]{0:T(1024)} %param.16) | copy-start | bytes 49156
  0.0 8.6 %copy-start.14 = (f32[128]{0:T(128)S(1)}, f32[128]{0:T(128)}, u32[]{:S(2)}) copy-start(f32[128]{0:T(128)} %param.21) | copy-start | bytes 1540
  0.0 9.1 %copy-start.11 = (bf16[32,32,128]{2,1,0:T(8,128)(2,1)S(1)}, bf16[32,32,128]{2,1,0:T(8,128)(2,1)}, u32[]{:S(2)}) copy-start(bf16[32,32,128]{2,1,0:T(8,128)(2,1)} %param.23) | copy-start | bytes 786436
  0.0 9.7 %copy-start.10 = (bf16[4096,128]{1,0:T(8,128)(2,1)S(1)}, bf16[4096,128]{1,0:T(8,128)(2,1)}, u32[]{:S(2)}) copy-start(bf16[4096,128]{1,0:T(8,128)(2,1)} %param.19) | copy-start | bytes 3145732
  2.7 7.4 %copy-start.15 = (bf16[32,32,128]{2,1,0:T(8,128)(2,1)S(1)}, bf16[32,32,128]{2,1,0:T(8,128)(2,1)}, u32[]{:S(2)}) copy-start(bf16[32,32,128]{2,1,0:T(8,128)(2,1)} %param.24) | copy-start | bytes 786436
  13.4 29.5 %copy-start.13 = (s32[512,1]{0,1:T(1,128)S(1)}, s32[512,1]{0,1:T(1,128)}, u32[]{:S(2)}) copy-start(s32[512,1]{0,1:T(1,128)} %param.29) | copy-start | bytes 6148
  14.2 11.5 %collective-permute-start = (bf16[32,4,512]{2,0,1:T(8,128)(2,1)S(1)}, bf16[32,4,512]{2,0,1:T(8,128)(2,1)S(1)}, u32[]{:S(2)}, u32[]{:S(2)}) collective-permute-start(bf16[32,4,512]{2,0,1:T(8,128)(2,1)S(1)} %bitcast.177), channel_id=1, source_target_pairs={{0,32},{32,0},{64,96},{96,64},{128,160},{160,128},{192,224},{224,1... | collective-permute-start | bytes 393224 | tf_op jit(solution)/shard_map/ppermute | solution.py:69
  19.0 18.9 %all-to-all-start = ((bf16[8,32,512]{2,1,0:T(8,128)(2,1)}), bf16[8,32,512]{2,1,0:T(8,128)(2,1)S(1)}, u32[]{:S(2)}, u32[]{:S(2)}) async-start(bf16[8,32,512]{2,1,0:T(8,128)(2,1)} %broadcast_in_dim.35), calls=%async_computation | async-start | bytes 524288 | tf_op jit(solution)/shard_map/all_to_all | solution.py:48
  25.9 18.3 %collective-permute-start.1 = (bf16[32,512]{1,0:T(8,128)(2,1)S(1)}, bf16[32,512]{1,0:T(8,128)(2,1)S(1)}, u32[]{:S(2)}, u32[]{:S(2)}) collective-permute-start(bf16[32,512]{1,0:T(8,128)(2,1)S(1)} %get-tuple-element.28), channel_id=1, source_target_pairs={{0,64},{32,96},{64,128},{96,160},{128,192},{160,224},{192,0},{224,... | collective-permute-start | bytes 98312 | tf_op jit(solution)/shard_map/ppermute | solution.py:307
  27.2 16.9 %collective-permute-start.2 = (bf16[32,512]{1,0:T(8,128)(2,1)S(1)}, bf16[32,512]{1,0:T(8,128)(2,1)S(1)}, u32[]{:S(2)}, u32[]{:S(2)}) collective-permute-start(bf16[32,512]{1,0:T(8,128)(2,1)S(1)} %get-tuple-element.30), channel_id=1, source_target_pairs={{0,128},{32,160},{64,192},{96,224},{128,0},{160,32},{192,64},{224,... | collective-permute-start | bytes 98312 | tf_op jit(solution)/shard_map/ppermute | solution.py:307
  29.9 14.3 %collective-permute-start.3 = (bf16[32,512]{1,0:T(8,128)(2,1)S(1)}, bf16[32,512]{1,0:T(8,128)(2,1)S(1)}, u32[]{:S(2)}, u32[]{:S(2)}) collective-permute-start(bf16[32,512]{1,0:T(8,128)(2,1)S(1)} %get-tuple-element.29), channel_id=1, source_target_pairs={{0,192},{32,224},{64,0},{96,32},{128,64},{160,96},{192,128},{224,1... | collective-permute-start | bytes 98312 | tf_op jit(solution)/shard_map/ppermute | solution.py:307
  38.9 18.5 %all-to-all-start.1 = ((bf16[4,8,32,512]{3,2,1,0:T(8,128)(2,1)}), bf16[4,8,32,512]{3,2,1,0:T(8,128)(2,1)S(1)}, u32[]{:S(2)}, u32[]{:S(2)}) async-start(bf16[4,8,32,512]{3,2,1,0:T(8,128)(2,1)} %broadcast_in_dim.36), calls=%async_computation.1 | async-start | bytes 2097152 | tf_op jit(solution)/shard_map/all_to_all | solution.py:48
  62.4 11.3 %all-to-all-start.2 = ((f32[8,32,128]{2,1,0:T(8,128)}), f32[8,32,128]{2,1,0:T(8,128)S(1)}, u32[]{:S(2)}, u32[]{:S(2)}) async-start(f32[8,32,128]{2,1,0:T(8,128)} %convolution_bitcast_fusion), calls=%async_computation.2 | async-start | bytes 262144 | tf_op jit(solution)/shard_map/all_to_all | solution.py:338
  69.3 20.6 %collective-permute-start.4 = (bf16[2064,128]{1,0:T(8,128)(2,1)}, bf16[2064,128]{1,0:T(8,128)(2,1)S(1)}, u32[]{:S(2)}, u32[]{:S(2)}) collective-permute-start(bf16[2064,128]{1,0:T(8,128)(2,1)} %fusion.4), channel_id=1, source_target_pairs={{0,32},{32,0},{64,96},{96,64},{128,160},{160,128},{192,224},{224,1... | collective-permute-start | bytes 1585160 | tf_op jit(solution)/shard_map/ppermute | solution.py:69
  74.5 11.0 %all-to-all-start.3 = ((bf16[8,64,128]{2,1,0:T(8,128)(2,1)}), bf16[8,64,128]{2,1,0:T(8,128)(2,1)S(1)}, u32[]{:S(2)}, u32[]{:S(2)}) async-start(bf16[8,64,128]{2,1,0:T(8,128)(2,1)} %broadcast_in_dim.43), calls=%async_computation.3 | async-start | bytes 262144 | tf_op jit(solution)/shard_map/all_to_all | solution.py:48
  86.4 13.5 %all-to-all-start.4 = ((bf16[4,8,64,128]{3,2,1,0:T(8,128)(2,1)}), bf16[4,8,64,128]{3,2,1,0:T(8,128)(2,1)S(1)}, u32[]{:S(2)}, u32[]{:S(2)}) async-start(bf16[4,8,64,128]{3,2,1,0:T(8,128)(2,1)} %broadcast_in_dim.44), calls=%async_computation.4 | async-start | bytes 1048576 | tf_op jit(solution)/shard_map/all_to_all | solution.py:48
  92.4 7.0 %collective-permute-start.5 = (bf16[528,128]{1,0:T(8,128)(2,1)S(1)}, bf16[528,128]{1,0:T(8,128)(2,1)S(1)}, u32[]{:S(2)}, u32[]{:S(2)}) collective-permute-start(bf16[528,128]{1,0:T(8,128)(2,1)S(1)} %get-tuple-element.41), channel_id=1, source_target_pairs={{0,64},{32,96},{64,128},{96,160},{128,192},{160,224},{192,0},{224,... | collective-permute-start | bytes 405512 | tf_op jit(solution)/shard_map/ppermute | solution.py:307
  92.8 6.7 %collective-permute-start.6 = (bf16[528,128]{1,0:T(8,128)(2,1)S(1)}, bf16[528,128]{1,0:T(8,128)(2,1)S(1)}, u32[]{:S(2)}, u32[]{:S(2)}) collective-permute-start(bf16[528,128]{1,0:T(8,128)(2,1)S(1)} %get-tuple-element.42), channel_id=1, source_target_pairs={{0,128},{32,160},{64,192},{96,224},{128,0},{160,32},{192,64},{224,... | collective-permute-start | bytes 405512 | tf_op jit(solution)/shard_map/ppermute | solution.py:307
  94.6 5.3 %collective-permute-start.7 = (bf16[528,128]{1,0:T(8,128)(2,1)S(1)}, bf16[528,128]{1,0:T(8,128)(2,1)S(1)}, u32[]{:S(2)}, u32[]{:S(2)}) collective-permute-start(bf16[528,128]{1,0:T(8,128)(2,1)S(1)} %get-tuple-element.43), channel_id=1, source_target_pairs={{0,192},{32,224},{64,0},{96,32},{128,64},{160,96},{192,128},{224,1... | collective-permute-start | bytes 405512 | tf_op jit(solution)/shard_map/ppermute | solution.py:307
  99.9 42.6 %copy-start.1 = (bf16[4,8,64,128]{3,2,1,0:T(8,128)(2,1)}, bf16[4,8,64,128]{3,2,1,0:T(8,128)(2,1)S(1)}, u32[]{:S(2)}) copy-start(bf16[4,8,64,128]{3,2,1,0:T(8,128)(2,1)S(1)} %all-to-all-done.4) | copy-start | bytes 1572868
  100.7 12.8 %all-to-all-start.5 = ((bf16[8,32,512]{2,1,0:T(8,128)(2,1)}), bf16[8,32,512]{2,1,0:T(8,128)(2,1)S(1)}, u32[]{:S(2)}, u32[]{:S(2)}) async-start(bf16[8,32,512]{2,1,0:T(8,128)(2,1)} %broadcast_in_dim.45), calls=%async_computation.5 | async-start | bytes 524288 | tf_op jit(solution)/shard_map/all_to_all | solution.py:48
  113.6 16.0 %all-to-all-start.6 = ((bf16[32,48,128]{2,1,0:T(8,128)(2,1)}), bf16[32,48,128]{2,1,0:T(8,128)(2,1)S(1)}, u32[]{:S(2)}, u32[]{:S(2)}) async-start(bf16[32,48,128]{2,1,0:T(8,128)(2,1)} %pad_maximum_fusion), calls=%async_computation.6 | async-start | bytes 786432 | tf_op jit(solution)/shard_map/all_to_all | solution.py:390
  118.1 19.6 %collective-permute-start.13 = (bf16[32,64,128]{2,1,0:T(8,128)(2,1)S(1)}, bf16[32,64,128]{2,1,0:T(8,128)(2,1)}, u32[]{:S(2)}, u32[]{:S(2)}) collective-permute-start(bf16[32,64,128]{2,1,0:T(8,128)(2,1)S(1)} %bitcast.161), channel_id=1, source_target_pairs={{0,64},{32,96},{64,128},{96,160},{128,192},{160,224},{192,0},{224,... | collective-permute-start | bytes 1572872 | tf_op jit(solution)/shard_map/ppermute | solution.py:57
  118.7 22.1 %collective-permute-start.12 = (bf16[32,64,128]{2,1,0:T(8,128)(2,1)S(1)}, bf16[32,64,128]{2,1,0:T(8,128)(2,1)}, u32[]{:S(2)}, u32[]{:S(2)}) collective-permute-start(bf16[32,64,128]{2,1,0:T(8,128)(2,1)S(1)} %bitcast.162), channel_id=1, source_target_pairs={{0,192},{32,224},{64,0},{96,32},{128,64},{160,96},{192,128},{224,1... | collective-permute-start | bytes 1572872 | tf_op jit(solution)/shard_map/ppermute | solution.py:57
  121.8 22.0 %collective-permute-start.16 = (bf16[32,64,128]{2,1,0:T(8,128)(2,1)S(1)}, bf16[32,64,128]{2,1,0:T(8,128)(2,1)S(1)}, u32[]{:S(2)}, u32[]{:S(2)}) collective-permute-start(bf16[32,64,128]{2,1,0:T(8,128)(2,1)S(1)} %bitcast.163), channel_id=1, source_target_pairs={{0,32},{32,0},{64,96},{96,64},{128,160},{160,128},{192,224},{224,1... | collective-permute-start | bytes 1572872 | tf_op jit(solution)/shard_map/ppermute | solution.py:69
  129.5 1.2 copy-start.9
  130.7 28.3 %all-to-all-start.7 = ((bf16[4,32,32,128]{3,2,1,0:T(8,128)(2,1)}), bf16[4,32,32,128]{3,2,1,0:T(8,128)(2,1)S(1)}, u32[]{:S(2)}, u32[]{:S(2)}) async-start(bf16[4,32,32,128]{3,2,1,0:T(8,128)(2,1)} %broadcast_in_dim.46), calls=%async_computation.7 | async-start | bytes 2097152 | tf_op jit(solution)/shard_map/all_to_all | solution.py:48
  135.6 11.3 %collective-permute-start.10 = (bf16[256,512]{1,0:T(8,128)(2,1)S(1)}, bf16[256,512]{1,0:T(8,128)(2,1)}, u32[]{:S(2)}, u32[]{:S(2)}) collective-permute-start(bf16[256,512]{1,0:T(8,128)(2,1)S(1)} %bitcast.165), channel_id=1, source_target_pairs={{0,2},{1,3},{2,0},{3,1},{4,6},{5,7},{6,4},{7,5},{8,10},{9,11},{10,... | collective-permute-start | bytes 786440 | tf_op jit(solution)/shard_map/ppermute | solution.py:394
  137.4 15.8 %collective-permute-start.11 = (bf16[256,512]{1,0:T(8,128)(2,1)S(1)}, bf16[256,512]{1,0:T(8,128)(2,1)}, u32[]{:S(2)}, u32[]{:S(2)}) collective-permute-start(bf16[256,512]{1,0:T(8,128)(2,1)S(1)} %bitcast.166), channel_id=1, source_target_pairs={{0,1},{1,2},{2,3},{3,0},{4,5},{5,6},{6,7},{7,4},{8,9},{9,10},{10,1... | collective-permute-start | bytes 786440 | tf_op jit(solution)/shard_map/ppermute | solution.py:394
  139.4 14.8 %collective-permute-start.14 = (bf16[16,64,128]{2,1,0:T(8,128)(2,1)}, bf16[16,64,128]{2,1,0:T(8,128)(2,1)}, u32[]{:S(2)}, u32[]{:S(2)}) collective-permute-start(bf16[16,64,128]{2,1,0:T(8,128)(2,1)} %slice.114), channel_id=1, source_target_pairs={{0,64},{32,96},{64,128},{96,160},{128,192},{160,224},{192,0},{224,... | collective-permute-start | bytes 786440 | tf_op jit(solution)/shard_map/ppermute | solution.py:57
  142.5 14.9 %collective-permute-start.15 = (bf16[16,64,128]{2,1,0:T(8,128)(2,1)}, bf16[16,64,128]{2,1,0:T(8,128)(2,1)}, u32[]{:S(2)}, u32[]{:S(2)}) collective-permute-start(bf16[16,64,128]{2,1,0:T(8,128)(2,1)} %slice.115), channel_id=1, source_target_pairs={{0,192},{32,224},{64,0},{96,32},{128,64},{160,96},{192,128},{224,1... | collective-permute-start | bytes 786440 | tf_op jit(solution)/shard_map/ppermute | solution.py:57
  143.8 0.8 copy-start.4
  144.5 13.7 %collective-permute-start.9 = (bf16[256,512]{1,0:T(8,128)(2,1)S(1)}, bf16[256,512]{1,0:T(8,128)(2,1)S(1)}, u32[]{:S(2)}, u32[]{:S(2)}) collective-permute-start(bf16[256,512]{1,0:T(8,128)(2,1)S(1)} %bitcast.167), channel_id=1, source_target_pairs={{0,3},{1,0},{2,1},{3,2},{4,7},{5,4},{6,5},{7,6},{8,11},{9,8},{10,9... | collective-permute-start | bytes 786440 | tf_op jit(solution)/shard_map/ppermute | solution.py:394
  146.9 14.0 %collective-permute-start.17 = (bf16[32,64,128]{2,1,0:T(8,128)(2,1)}, bf16[32,64,128]{2,1,0:T(8,128)(2,1)}, u32[]{:S(2)}, u32[]{:S(2)}) collective-permute-start(bf16[32,64,128]{2,1,0:T(8,128)(2,1)} %collective-permute-done.12.refs_5_), channel_id=1, source_target_pairs={{0,32},{32,0},{64,96},{96,64},{128,160},{160,128},{192,224},{224,1... | collective-permute-start | bytes 1572872 | tf_op jit(solution)/shard_map/ppermute | solution.py:69
  153.3 7.7 %collective-permute-start.18 = (bf16[32,64,128]{2,1,0:T(8,128)(2,1)}, bf16[32,64,128]{2,1,0:T(8,128)(2,1)}, u32[]{:S(2)}, u32[]{:S(2)}) collective-permute-start(bf16[32,64,128]{2,1,0:T(8,128)(2,1)} %collective-permute-done.13.refs_6_), channel_id=1, source_target_pairs={{0,32},{32,0},{64,96},{96,64},{128,160},{160,128},{192,224},{224,1... | collective-permute-start | bytes 1572872 | tf_op jit(solution)/shard_map/ppermute | solution.py:69
  154.2 6.7 %collective-permute-start.19 = (bf16[16,64,128]{2,1,0:T(8,128)(2,1)}, bf16[16,64,128]{2,1,0:T(8,128)(2,1)}, u32[]{:S(2)}, u32[]{:S(2)}) collective-permute-start(bf16[16,64,128]{2,1,0:T(8,128)(2,1)} %collective-permute-done.14.refs_7_), channel_id=1, source_target_pairs={{0,32},{32,0},{64,96},{96,64},{128,160},{160,128},{192,224},{224,1... | collective-permute-start | bytes 786440 | tf_op jit(solution)/shard_map/ppermute | solution.py:69
  157.4 3.5 %collective-permute-start.20 = (bf16[16,64,128]{2,1,0:T(8,128)(2,1)}, bf16[16,64,128]{2,1,0:T(8,128)(2,1)}, u32[]{:S(2)}, u32[]{:S(2)}) collective-permute-start(bf16[16,64,128]{2,1,0:T(8,128)(2,1)} %collective-permute-done.15.refs_8_), channel_id=1, source_target_pairs={{0,32},{32,0},{64,96},{96,64},{128,160},{160,128},{192,224},{224,1... | collective-permute-start | bytes 786440 | tf_op jit(solution)/shard_map/ppermute | solution.py:69
  158.3 0.7 copy-start.6
  159.0 25.4 %collective-permute-start.8 = (bf16[4,32,32,128]{3,2,1,0:T(8,128)(2,1)S(1)}, bf16[4,32,32,128]{3,2,1,0:T(8,128)(2,1)S(1)}, u32[]{:S(2)}, u32[]{:S(2)}) collective-permute-start(bf16[4,32,32,128]{3,2,1,0:T(8,128)(2,1)S(1)} %all-to-all-done.7.own), channel_id=1, source_target_pairs={{0,32},{32,0},{64,96},{96,64},{128,160},{160,128},{192,224},{224,1... | collective-permute-start | bytes 3145736 | tf_op jit(solution)/shard_map/ppermute | solution.py:69
  160.9 1.0 copy-start.2
  162.0 1.0 copy-start.3
  163.0 1.0 copy-start.5
  164.1 0.9 copy-start.7

commit v4 on v3

--- a/solution.py
+++ b/solution.py
@@ -35,6 +35,9 @@
 
 
 TILE = 256
+SMEM = pl.BlockSpec(memory_space=pltpu.SMEM)
+VMEM = pl.BlockSpec(memory_space=pltpu.VMEM)
+ANY = pl.BlockSpec(memory_space=pl.ANY)
 
 
 def contract_last(left, right):
@@ -84,23 +87,38 @@
     return lax.fori_loop(0, 1024 // TILE, body, init)
 
 
-def put(block, target, place, row=0):
-    first = pl.multiple_of(place * 128, 128)
-    value = block.reshape(block.shape[0] * block.shape[1], 128)
-    target[row : row + value.shape[0], pl.ds(first, 128)] = value
+def columns(place):
+    return pl.ds(pl.multiple_of(place * 128, 128), 128)
+
+
+def copy_all(pairs, sems):
+    copies = [pltpu.make_async_copy(a, b, sems.at[i]) for i, (a, b) in enumerate(pairs)]
+    for copy in copies:
+        copy.start()
+    return copies
 
 
 def solve_kernel(here, scale, gain, *refs):
     states, grams, result = refs[:4], refs[4:14], refs[14]
-    high, low, rho, rho_high, rho_low, image, way, way_image, total = refs[15:]
+    state, high, low, rho, rho_high, rho_low, image, way, way_image, total = refs[15:25]
+    state_sems, gram_sems = refs[25:]
     ridge = 0.125 * D
+    placed = [
+        (piece, state.at[:, lax.rem(here[2] + step, 4)]) for step, piece in enumerate(states)
+    ]
+    state_copies = copy_all(placed, state_sems)
+    placed = []
     for index, piece in enumerate(grams):
-        step, row = ((0, 0), (1, 0), (3, 0), (2, 0), (2, 512))[index % 5]
+        step, row = ((0, 0), (1, 0), (3, 0), (2, 0), (2, 16))[index % 5]
         side = here[0] if index < 5 else 1 - here[0]
-        at = 2 * lax.rem(here[1] + step, 4) + side
+        at = columns(2 * lax.rem(here[1] + step, 4) + side)
         docs = piece.shape[1] // 2
-        put(piece[:, :docs, :], high, at, row)
-        put(piece[:, docs:, :], low, at, row)
+        rows = slice(row, row + piece.shape[0])
+        placed.append((piece.at[:, :docs], high.at[rows, :, at]))
+        placed.append((piece.at[:, docs:], low.at[rows, :, at]))
+    gram_copies = copy_all(placed, gram_sems)
+    for copy in state_copies:
+        copy.wait()
 
     def rows_of(i):
         return pl.ds(pl.multiple_of(i * TILE, TILE), TILE)
@@ -111,19 +129,29 @@
         rho_high[rows, :] = top
         rho_low[rows, :] = (value - top.astype(jnp.float32)).astype(jnp.bfloat16)
 
-    for step, state in enumerate(states):
-        rows = rows_of(lax.rem(here[2] + step, 4))
-        value = state[...].astype(jnp.float32) * scale[rows, :] * gain[...]
+    def start(i, carry):
+        rows = rows_of(i)
+        value = state[pl.ds(2 * i, 2)].reshape(TILE, -1).astype(jnp.float32)
+        value = value * scale[rows, :] * gain[...]
         split(rows, value)
         way[rows, :] = value
+        return carry
+
+    tiles(start)
+    for copy in gram_copies:
+        copy.wait()
+
+    def gram_rows(block, i):
+        return block[pl.ds(8 * i, 8)].reshape(TILE, -1)
 
     def dot(left, right):
         return jnp.dot(left, right, preferred_element_type=jnp.float32)
 
     def product(i, square):
         rows = rows_of(i)
-        value = dot(high[rows, :], rho_low[...]) + dot(low[rows, :], rho_high[...])
-        value = value + dot(high[rows, :], rho_high[...])
+        top = gram_rows(high, i)
+        value = dot(top, rho_low[...]) + dot(gram_rows(low, i), rho_high[...])
+        value = value + dot(top, rho_high[...])
         image[rows, :] = value
         return square + jnp.sum(rho[rows, :] * value, axis=0, keepdims=True)
 
@@ -167,45 +195,47 @@
             res_sq = new_sq
 
 
-def call(kernel, out_shape, scratch, operands, flops):
-    vmem = pl.BlockSpec(memory_space=pltpu.VMEM)
+def call(kernel, out_shape, in_specs, scratch, operands, flops):
     return pl.pallas_call(
         kernel,
         out_shape=out_shape,
-        in_specs=[pl.BlockSpec(memory_space=pltpu.SMEM)] + [vmem] * (len(operands) - 1),
-        out_specs=vmem,
+        in_specs=in_specs,
+        out_specs=VMEM,
         scratch_shapes=scratch,
         cost_estimate=pl.CostEstimate(flops=flops, bytes_accessed=1 << 23, transcendentals=0),
-        compiler_params=pltpu.CompilerParams(vmem_limit_bytes=32 << 20),
+        compiler_params=pltpu.CompilerParams(vmem_limit_bytes=62 << 20),
     )(*operands)
 
 
 def solve(*operands):
     anchors, cols = operands[1].shape[0], operands[2].shape[1]
-    wide = pltpu.VMEM((anchors, anchors), jnp.bfloat16)
+    wide = pltpu.VMEM((32, anchors // 32, anchors), jnp.bfloat16)
     full = pltpu.VMEM((anchors, cols), jnp.float32)
     half = pltpu.VMEM((anchors, cols), jnp.bfloat16)
     return call(
         solve_kernel,
         jax.ShapeDtypeStruct((anchors, cols), jnp.bfloat16),
-        [wide, wide, full, half, half, full, full, full, full],
+        [SMEM, VMEM, VMEM] + [ANY] * 14,
+        [pltpu.VMEM((8, 4, anchors // 32, cols), jnp.bfloat16), wide, wide, full, half, half]
+        + [full] * 4
+        + [pltpu.SemaphoreType.DMA((4,)), pltpu.SemaphoreType.DMA((20,))],
         operands,
         18 * anchors * anchors * cols,
     )
 
 
-def apply_kernel(here, own, other, dual_map, result, routed):
-    for y in range(own.shape[0]):
-        put(own[y], routed, 2 * y + here[0])
-        put(other[y], routed, 2 * y + 1 - here[0])
-
-    def rows_of(i):
-        return pl.ds(pl.multiple_of(i * TILE, TILE), TILE)
+def apply_kernel(here, own, other, dual_map, result, routed, sems):
+    placed = []
+    for y in range(4):
+        placed.append((own.at[y], routed.at[:, :, columns(2 * y + here[0])]))
+        placed.append((other.at[y], routed.at[:, :, columns(2 * y + 1 - here[0])]))
+    for copy in copy_all(placed, sems):
+        copy.wait()
 
     def product(i, carry):
-        rows = rows_of(i)
-        value = jnp.dot(routed[rows, :], dual_map[...], preferred_element_type=jnp.float32)
-        result[rows, :] = value.astype(jnp.bfloat16)
+        rows = routed[pl.ds(8 * i, 8)].reshape(TILE, -1)
+        value = jnp.dot(rows, dual_map[...], preferred_element_type=jnp.float32)
+        result[pl.ds(pl.multiple_of(i * TILE, TILE), TILE), :] = value.astype(jnp.bfloat16)
         return carry
 
     tiles(product)
@@ -213,13 +243,17 @@
 
 def apply_map(*operands):
     anchors, cols = operands[3].shape
-    slots = operands[1].shape[1] * operands[1].shape[2]
+    blocks, slots = operands[1].shape[1:3]
     return call(
         apply_kernel,
-        jax.ShapeDtypeStruct((slots, cols), jnp.bfloat16),
-        [pltpu.VMEM((slots, anchors), jnp.bfloat16)],
+        jax.ShapeDtypeStruct((blocks * slots, cols), jnp.bfloat16),
+        [SMEM, ANY, ANY, VMEM],
+        [
+            pltpu.VMEM((blocks, slots, anchors), jnp.bfloat16),
+            pltpu.SemaphoreType.DMA((8,)),
+        ],
         operands,
-        2 * slots * anchors * cols,
+        2 * anchors * anchors * cols,
     )
 
 
@@ -322,51 +356,52 @@
     line = 4
     column = rows_count // line
     by_z = [[x + line * z for z in range(column)] for x in range(line)]
-    by_x = [[x + line * z for x in range(line)] for z in range(column)]
     by_y = [list(range(at, mp_count, 2)) for at in range(2)]
     old_mine = my_cols(old_embed, 1)
-    old_all = spread(old_mine, "rows", column, by_z)
-    old_all = spread(old_all, "rows", line, by_x)
+    old_all = spread(old_mine, "rows", rows_count)
     anchors = rows_count * docs
     part = anchors // mp_count
     old_all = old_all.reshape(anchors, cols)
 
     def by_part(array):
-        return array.reshape(-1, mp_count, part).transpose(1, 0, 2)
-
-    gram_part = by_part(contract_last(old_mine, old_all))
-    gram_part = lax.all_to_all(gram_part, "mp", 0, 0, tiled=True)
-    gram = jnp.concatenate(halves(jnp.sum(gram_part, axis=0)), axis=0)
-    gram = spread(gram, "rows", column, by_z)
-    gram = spread(gram, "rows", line, by_x)
-    gram = gram.reshape(rows_count, 2 * docs, part)
+        return array.reshape(-1, mp_count, part).transpose(1, 0, 2).reshape(chips, 2, -1, part)
+
+    def reduce_mp(parts, extra):
+        count, kind = parts.shape[2], parts.dtype
+        theirs = lax.dynamic_index_in_dim(parts, 1 - core, 1, False)
+        theirs = jnp.concatenate([theirs.reshape(chips * count, part), *extra], axis=0)
+        theirs = swap_cores(theirs, mp_count).astype(jnp.float32)
+        parts = lax.dynamic_index_in_dim(parts, core, 1, False).astype(jnp.float32)
+        parts = parts + theirs[: chips * count].reshape(parts.shape)
+        extra = [rows + theirs[chips * count :] for rows in extra]
+        total = lax.dynamic_index_in_dim(parts, chip, 0, False)
+        parts = parts.astype(kind)
+        total = jnp.concatenate([total, *extra], axis=0)
+        for step in range(1, chips):
+            piece = lax.dynamic_index_in_dim(parts, (chip + step) % chips, 0, False)
+            piece = shift_chips(jnp.concatenate([piece, *extra], axis=0), step)
+            total = total + piece.astype(jnp.float32)
+        return total
+
+    state = state.astype(half)
+    state_column = spread(state, "rows", column, by_z)
+    states = [state_column]
+    for step in range(1, line):
+        pairs = [(i, i // line * line + (i - step) % line) for i in range(rows_count)]
+        states.append(lax.ppermute(state_column, "rows", pairs))
+
+    extra = jnp.pad(squares[None, :], ((0, 7), (0, part - docs)))
+    gram = reduce_mp(by_part(contract_last(old_mine, old_all)), [extra])
+    gram = jnp.concatenate([*halves(gram[:docs]), norm_rows(gram[docs, :docs], part)], axis=0)
+    arrived = spread(gram, "rows", rows_count)
+    gram = arrived[:, : 2 * docs]
+    squares = arrived[:, 2 * docs].astype(jnp.float32)
+    squares = squares[:, :docs] + squares[:, docs : 2 * docs]
+    scale_rows = lax.rsqrt(squares / width + 1e-06).reshape(anchors, 1)
 
     count = slab.shape[0]
     slab_part = by_part(contract_last(slab, old_all).astype(half))
-    slab_part = slab_part.reshape(chips, 2, count, part)
-    theirs = lax.dynamic_index_in_dim(slab_part, 1 - core, 1, False)
-    slab_part = lax.dynamic_index_in_dim(slab_part, core, 1, False).astype(jnp.float32)
-    theirs, others = jnp.split(
-        swap_cores(
-            jnp.concatenate(
-                [theirs.reshape(chips * count, part), norm_rows(squares, part)], axis=0
-            ),
-            mp_count,
-        ).astype(jnp.float32),
-        [chips * count],
-    )
-    slab_part = slab_part + theirs.reshape(chips, count, part)
-    squares = squares + others[0, :docs] + others[0, docs : 2 * docs]
-    slab_dual = lax.dynamic_index_in_dim(slab_part, chip, 0, False)
-    slab_part = slab_part.astype(half)
-    pair_rows = norm_rows(squares, part)
-    for step in range(1, chips):
-        piece = lax.dynamic_index_in_dim(slab_part, (chip + step) % chips, 0, False)
-        piece = shift_chips(jnp.concatenate([piece, pair_rows], axis=0), step)
-        piece = piece.astype(jnp.float32)
-        slab_dual = slab_dual + piece[:count]
-        squares = squares + piece[count, :docs] + piece[count, docs : 2 * docs]
-
+    slab_dual = reduce_mp(slab_part, []).astype(half)
     capacity = 2 * count // rows_count
     owner_ids = owners[:, 0]
     onehot = (owner_ids[:, None] == jnp.arange(rows_count, dtype=jnp.int32)[None, :]).astype(
@@ -375,28 +410,9 @@
     counted = jnp.cumsum(onehot, axis=0)
     slot = jnp.sum((counted - 1) * onehot, axis=-1)
     target = owner_ids * capacity + slot
-    routed = jnp.zeros((rows_count * capacity, part), half).at[target].set(slab_dual.astype(half))
-    outgoing = jnp.concatenate(
-        [
-            routed.reshape(rows_count, capacity, part),
-            jnp.broadcast_to(norm_rows(squares, part)[None], (rows_count, 16, part)),
-        ],
-        axis=1,
-    )
-
-    state, gram = lax.optimization_barrier((state.astype(half), gram))
-    state_column = spread(state, "rows", column, by_z)
-    outgoing, state_column = lax.optimization_barrier((outgoing, state_column))
-    arrived = lax.all_to_all(outgoing, "rows", split_axis=0, concat_axis=0, tiled=True)
-    states = [state_column.reshape(anchors // line, cols)]
-    for step in range(1, line):
-        pairs = [(i, i // line * line + (i - step) % line) for i in range(rows_count)]
-        states.append(lax.ppermute(states[0], "rows", pairs))
-    routed = arrived[:, :capacity]
-    squares = arrived[:, capacity].astype(jnp.float32)
-    squares = squares[:, :docs] + squares[:, docs : 2 * docs]
-    squares = squares.reshape(column, line, docs).transpose(1, 0, 2)
-    scale_rows = lax.rsqrt(squares / width + 1e-06).reshape(anchors, 1)
+    routed = jnp.zeros((rows_count * capacity, part), half).at[target].set(slab_dual)
+    routed, _ = lax.optimization_barrier((routed, arrived))
+    routed = lax.all_to_all(routed.reshape(rows_count, capacity, part), "rows", 0, 0, tiled=True)
 
     grams = ring(gram, "mp", chips, mp_count, 2)
     grams = grams + [swap_cores(piece, mp_count) for piece in grams]

time: 190 us -> 174 us (0.916)
  the two profiles are of different devices: /device:TPU:1 before, /device:TPU:2 now
where the time goes in v4:
time: 174 us; the launch traced here: 171 us
  starting transfers between devices  66.3 us (38%)
  waiting for transfers between devices  37.3 us (21%)
  Pallas kernels  25.8 us (15%)
  matrix products  14 us (8%)
  other arithmetic  13.6 us (8%)
  local copies, waits for them, and re-layouts  13.1 us (8%)
    all_to_all x4, starting transfers between devices, spread(): lax.all_to_all(copies, axis, 0, 0, tiled=True, axis_index_groups=groups)  29.1 us
    pallas_call x2, Pallas kernels, call(): pl.pallas_call(kernel, out_shape=out_shape, in_specs=in_specs, out_specs=...  25.8 us
    ppermute x9, starting transfers between devices, shift_chips(): lax.ppermute(block, 'mp', [(i, (i + 2 * step) % mp_count) for i in range(...  13.6 us
    all_to_all x4, waiting for transfers between devices, spread(): lax.all_to_all(copies, axis, 0, 0, tiled=True, axis_index_groups=groups)  13.1 us
    ppermute x9, waiting for transfers between devices, shift_chips(): lax.ppermute(block, 'mp', [(i, (i + 2 * step) % mp_count) for i in range(...  11.3 us
    all_to_all x1, starting transfers between devices, local(): lax.all_to_all(routed.reshape(rows_count, capacity, part), 'rows', 0, 0,...  10.2 us
    ppermute x4, starting transfers between devices, move(): return lax.ppermute(array, axis, pairs)  7.05 us
    all_to_all x1, waiting for transfers between devices, local(): lax.all_to_all(routed.reshape(rows_count, capacity, part), 'rows', 0, 0,...  6.43 us
  transfers between devices with their start and end apart: 30, of which 13 were waited for; matrix products, arithmetic and copies ran while one was open for 21% of the time, Pallas kernels for 12%

profile of v4, /device:TPU:2, one launch (start us, length us, event | category | flops | bytes accessed | tf_op | source)
XLA Modules:
  0.0 170.9 jit_solution(2486066238145367410)
XLA Ops:
  0.9 1.1 broadcast_in_dim.27
  2.0 11.6 %all-to-all-start = ((bf16[32,32,512]{2,1,0:T(8,128)(2,1)}), bf16[32,32,512]{2,1,0:T(8,128)(2,1)S(1)}, u32[]{:S(2)}, u32[]{:S(2)}) async-start(bf16[32,32,512]{2,1,0:T(8,128)(2,1)} %broadcast_in_dim.27), calls=%async_computation | async-start | bytes 2097152 | tf_op jit(solution)/shard_map/all_to_all | solution.py:51
  14.4 1.3 iota_compare_fusion.3
  15.7 1.1 multiply_reduce_fusion
  16.8 1.4 multiply_reduce_fusion.3
  19.3 3.7 %fusion.49 = f32[32,512]{1,0:T(8,128)} fusion(bf16[4096,512]{1,0:T(8,128)(2,1)} %param.17, f32[4096]{0:T(1024)S(1)} %copy-done.5, f32[32]{0:T(128)S(1)} %add_rsqrt_fusion.2, bf16[32,4096]{1,0:T(8,128)(2,1)S(1)} %copy-done.1), kind=kOutput, calls=%fused_computation.121 | convolution fusion | flops 134742016 | bytes 4538496 | tf_op jit(solution)/shard_map/dot_general | solution.py:291
  25.8 1.4 fusion.54
  27.4 1.0 fusion.2
  28.4 1.2 fusion.1
  29.6 3.0 %fusion.18 = f32[32,4096]{1,0:T(8,128)S(1)} fusion(bf16[512,4096]{1,0:T(8,128)(2,1)} %param.20, bf16[4,8,4,128]{3,2,1,0:T(4,128)(2,1)S(1)} %bitcast.140), kind=kOutput, calls=%fused_computation.51 | convolution fusion | flops 134217728 | bytes 4751360 | tf_op jit(solution)/shard_map/dot_general | solution.py:331
  33.9 1.0 collective-permute-done.4
  35.0 1.7 collective-permute-start.5
  36.7 2.9 %collective-permute-start.6 = (bf16[32,512]{1,0:T(8,128)(2,1)S(1)}, bf16[32,512]{1,0:T(8,128)(2,1)S(1)}, u32[]{:S(2)}, u32[]{:S(2)}) collective-permute-start(bf16[32,512]{1,0:T(8,128)(2,1)S(1)} %get-tuple-element.18), channel_id=1, source_target_pairs={{0,128},{32,160},{64,192},{96,224},{128,0},{160,32},{192,64},{224,... | collective-permute-start | bytes 98312 | tf_op jit(solution)/shard_map/ppermute | solution.py:341
  39.6 1.3 collective-permute-start.7
  41.0 1.1 collective-permute-done.6
  42.1 1.4 collective-permute-done.7
  44.2 1.2 collective-permute-done.8
  45.5 1.6 collective-permute-start.10
  47.1 1.3 collective-permute-start.11
  49.2 1.8 %collective-permute-done.10 = f32[40,128]{1,0:T(8,128)S(1)} collective-permute-done((f32[40,128]{1,0:T(8,128)S(1)}, f32[40,128]{1,0:T(8,128)S(1)}, u32[]{:S(2)}, u32[]{:S(2)}) %collective-permute-start.10) | collective-permute-done | bytes 20512 | tf_op jit(solution)/shard_map/ppermute | solution.py:341
  51.0 2.5 %collective-permute-done.9 = f32[40,128]{1,0:T(8,128)S(1)} collective-permute-done((f32[40,128]{1,0:T(8,128)S(1)}, f32[40,128]{1,0:T(8,128)S(1)}, u32[]{:S(2)}, u32[]{:S(2)}) %collective-permute-start.9) | collective-permute-done | bytes 20512 | tf_op jit(solution)/shard_map/ppermute | solution.py:341
  54.5 9.8 %all-to-all-start.1 = ((bf16[32,80,128]{2,1,0:T(8,128)(2,1)}), bf16[32,80,128]{2,1,0:T(8,128)(2,1)S(1)}, u32[]{:S(2)}, u32[]{:S(2)}) async-start(bf16[32,80,128]{2,1,0:T(8,128)(2,1)} %broadcast_in_dim.32), calls=%async_computation.1 | async-start | bytes 1310720 | tf_op jit(solution)/shard_map/all_to_all | solution.py:51
  64.3 1.7 %convolution_convert_fusion = bf16[1024,512]{1,0:T(8,128)(2,1)} fusion(bf16[1024,512]{1,0:T(8,128)(2,1)S(1)} %bitcast.127, bf16[512,512]{1,0:T(8,128)(2,1)S(1)} %copy-done.10), kind=kOutput, calls=%fused_computation.1 | convolution fusion | flops 537395200 | bytes 2621440 | tf_op jit(solution)/shard_map/dot_general | solution.py:44
  66.0 1.6 copy.26
  68.0 1.2 reduce-window.6
  69.6 13.1 %all-to-all-done.1 = bf16[32,80,128]{2,1,0:T(8,128)(2,1)S(1)} async-done(((bf16[32,80,128]{2,1,0:T(8,128)(2,1)}), bf16[32,80,128]{2,1,0:T(8,128)(2,1)S(1)}, u32[]{:S(2)}, u32[]{:S(2)}) %all-to-all-start.1) | async-done | bytes 655392 | tf_op jit(solution)/shard_map/all_to_all | solution.py:51
  83.4 3.4 %all-to-all-start.4 = ((bf16[8,32,512]{2,1,0:T(8,128)(2,1)}), bf16[8,32,512]{2,1,0:T(8,128)(2,1)S(1)}, u32[]{:S(2)}, u32[]{:S(2)}) async-start(bf16[8,32,512]{2,1,0:T(8,128)(2,1)} %broadcast_in_dim.34), calls=%async_computation.4 | async-start | bytes 524288 | tf_op jit(solution)/shard_map/all_to_all | solution.py:51
  86.8 2.2 %fusion.53 = (bf16[4,512,128]{2,1,0:T(8,128)(2,1)S(1)}, f32[4,512,128]{2,1,0:T(8,128)}) fusion(bf16[4,512,128]{2,1,0:T(8,128)(2,1)} %bitcast.53, bf16[4,2,512,128]{3,2,1,0:T(8,128)(2,1)S(1)} %bitcast.129, s32[]{:T(128)S(6)} %select_n.96), kind=kLoop, calls=%fused_computation.124 | loop fusion | flops 1048576 | bytes 2621444 | tf_op jit(solution)/shard_map/convert_element_type | solution.py:378
  89.1 2.0 %collective-permute-start.2 = (bf16[512,128]{1,0:T(8,128)(2,1)S(1)}, bf16[512,128]{1,0:T(8,128)(2,1)S(1)}, u32[]{:S(2)}, u32[]{:S(2)}) collective-permute-start(bf16[512,128]{1,0:T(8,128)(2,1)S(1)} %get-tuple-element.15), channel_id=1, source_target_pairs={{0,128},{32,160},{64,192},{96,224},{128,0},{160,32},{192,64},{224,... | collective-permute-start | bytes 393224 | tf_op jit(solution)/shard_map/ppermute | solution.py:341
  91.0 2.0 %collective-permute-start.3 = (bf16[512,128]{1,0:T(8,128)(2,1)S(1)}, bf16[512,128]{1,0:T(8,128)(2,1)S(1)}, u32[]{:S(2)}, u32[]{:S(2)}) collective-permute-start(bf16[512,128]{1,0:T(8,128)(2,1)S(1)} %get-tuple-element.14), channel_id=1, source_target_pairs={{0,192},{32,224},{64,0},{96,32},{128,64},{160,96},{192,128},{224,1... | collective-permute-start | bytes 393224 | tf_op jit(solution)/shard_map/ppermute | solution.py:341
  93.0 3.6 %collective-permute-done.1 = bf16[512,128]{1,0:T(8,128)(2,1)S(1)} collective-permute-done((bf16[512,128]{1,0:T(8,128)(2,1)S(1)}, bf16[512,128]{1,0:T(8,128)(2,1)S(1)}, u32[]{:S(2)}, u32[]{:S(2)}) %collective-permute-start.1) | collective-permute-done | bytes 131104 | tf_op jit(solution)/shard_map/ppermute | solution.py:341
  97.5 2.9 %scatter_custom_fusion = bf16[1024,128]{1,0:T(8,128)(2,1)} fusion(s32[512]{0:T(512)S(1)} %bitcast.146, bf16[512,128]{1,0:T(8,128)(2,1)S(1)} %collective-permute-done.3, bf16[512,128]{1,0:T(8,128)(2,1)S(1)} %collective-permute-done.2, bf16[512,128]{1,0:T(8,128)(2,1)S(1)} %collective-permute-done.1, f32[4,512,128]{2,1,0:T(8,128)} %get-tuple-element.12, ...), kind=kCustom, calls=%fused_computation.17 | custom fusion | flops 458752 | bytes 918532 | tf_op jit(solution)/shard_map/scatter | solution.py:413
  100.4 10.2 %all-to-all-start.2 = ((bf16[32,32,128]{2,1,0:T(8,128)(2,1)}), bf16[32,32,128]{2,1,0:T(8,128)(2,1)S(1)}, u32[]{:S(2)}, u32[]{:S(2)}) async-start(bf16[32,32,128]{2,1,0:T(8,128)(2,1)} %bitcast.48), calls=%async_computation.2 | async-start | bytes 524288 | tf_op jit(solution)/shard_map/all_to_all | solution.py:415
  111.5 2.5 %collective-permute-start.16 = (bf16[32,64,128]{2,1,0:T(8,128)(2,1)S(1)}, bf16[32,64,128]{2,1,0:T(8,128)(2,1)}, u32[]{:S(2)}, u32[]{:S(2)}) collective-permute-start(bf16[32,64,128]{2,1,0:T(8,128)(2,1)S(1)} %slice.76.refs_4_), channel_id=1, source_target_pairs={{0,192},{32,224},{64,0},{96,32},{128,64},{160,96},{192,128},{224,1... | collective-permute-start | bytes 1572872 | tf_op jit(solution)/shard_map/ppermute | solution.py:60
  114.0 6.4 %all-to-all-done.2 = bf16[32,32,128]{2,1,0:T(8,128)(2,1)S(1)} async-done(((bf16[32,32,128]{2,1,0:T(8,128)(2,1)}), bf16[32,32,128]{2,1,0:T(8,128)(2,1)S(1)}, u32[]{:S(2)}, u32[]{:S(2)}) %all-to-all-start.2) | async-done | bytes 262176 | tf_op jit(solution)/shard_map/all_to_all | solution.py:415
  120.4 1.1 broadcast_in_dim.33
  121.6 4.2 %all-to-all-start.3 = ((bf16[4,32,32,128]{3,2,1,0:T(8,128)(2,1)}), bf16[4,32,32,128]{3,2,1,0:T(8,128)(2,1)}, u32[]{:S(2)}, u32[]{:S(2)}) async-start(bf16[4,32,32,128]{3,2,1,0:T(8,128)(2,1)} %broadcast_in_dim.33), calls=%async_computation.3 | async-start | bytes 2097152 | tf_op jit(solution)/shard_map/all_to_all | solution.py:51
  125.8 2.0 %collective-permute-start.13 = (bf16[8,32,512]{2,1,0:T(8,128)(2,1)S(1)}, bf16[8,32,512]{2,1,0:T(8,128)(2,1)S(1)}, u32[]{:S(2)}, u32[]{:S(2)}) collective-permute-start(bf16[8,32,512]{2,1,0:T(8,128)(2,1)S(1)} %all-to-all-done.4.refs_0_), channel_id=1, source_target_pairs={{0,3},{1,0},{2,1},{3,2},{4,7},{5,4},{6,5},{7,6},{8,11},{9,8},{10,9... | collective-permute-start | bytes 786440 | tf_op jit(solution)/shard_map/ppermute | solution.py:391
  127.9 1.0 collective-permute-start.14
  128.8 1.8 %collective-permute-start.15 = (bf16[8,32,512]{2,1,0:T(8,128)(2,1)S(1)}, bf16[8,32,512]{2,1,0:T(8,128)(2,1)}, u32[]{:S(2)}, u32[]{:S(2)}) collective-permute-start(bf16[8,32,512]{2,1,0:T(8,128)(2,1)S(1)} %all-to-all-done.4.refs_0_), channel_id=1, source_target_pairs={{0,1},{1,2},{2,3},{3,0},{4,5},{5,6},{6,7},{7,4},{8,9},{9,10},{10,1... | collective-permute-start | bytes 786440 | tf_op jit(solution)/shard_map/ppermute | solution.py:391
  130.7 2.0 %collective-permute-start.18 = (bf16[16,64,128]{2,1,0:T(8,128)(2,1)S(1)}, bf16[16,64,128]{2,1,0:T(8,128)(2,1)}, u32[]{:S(2)}, u32[]{:S(2)}) collective-permute-start(bf16[16,64,128]{2,1,0:T(8,128)(2,1)S(1)} %slice.77), channel_id=1, source_target_pairs={{0,64},{32,96},{64,128},{96,160},{128,192},{160,224},{192,0},{224,... | collective-permute-start | bytes 786440 | tf_op jit(solution)/shard_map/ppermute | solution.py:60
  132.7 1.0 slice.78
  134.4 1.8 %collective-permute-start.19 = (bf16[16,64,128]{2,1,0:T(8,128)(2,1)S(1)}, bf16[16,64,128]{2,1,0:T(8,128)(2,1)}, u32[]{:S(2)}, u32[]{:S(2)}) collective-permute-start(bf16[16,64,128]{2,1,0:T(8,128)(2,1)S(1)} %slice.78), channel_id=1, source_target_pairs={{0,192},{32,224},{64,0},{96,32},{128,64},{160,96},{192,128},{224,1... | collective-permute-start | bytes 786440 | tf_op jit(solution)/shard_map/ppermute | solution.py:60
  136.1 1.3 dynamic_slice.91
  138.6 3.8 %collective-permute-done.18.refs_7_ = bf16[16,64,128]{2,1,0:T(8,128)(2,1)} collective-permute-done((bf16[16,64,128]{2,1,0:T(8,128)(2,1)S(1)}, bf16[16,64,128]{2,1,0:T(8,128)(2,1)}, u32[]{:S(2)}, u32[]{:S(2)}) %collective-permute-start.18) | collective-permute-done | bytes 262176 | tf_op jit(solution)/shard_map/ppermute | solution.py:60
  143.6 1.3 reshape.351.scale
  145.0 20.2 %shard_map.145.dual_map = bf16[1024,512]{1,0:T(8,128)(2,1)} custom-call(s32[4]{0:T(128)} %pad_add_fusion.here, f32[1024,1]{1,0:T(8,128)} %reshape.351.scale, f32[1,512]{1,0:T(1,128)} %bitcast.147, bf16[8,32,512]{2,1,0:T(8,128)(2,1)} %copy-done.4, bf16[8,32,512]{2,1,0:T(8,128)(2,1)} %copy-done.11, bf16[8,32,512]{2,1,0:T(8,128)(2,1)} %collective-permute-done.14.refs_2_, ...), custom_call_target="tpu_custom_call" | custom-call | flops 9663676416 | bytes 8388608 | tf_op jit(solution)/shard_map/pallas_call | solution.py:199
  165.2 5.5 %shard_map.146 = bf16[1024,512]{1,0:T(8,128)(2,1)} custom-call(s32[4]{0:T(128)} %pad_add_fusion.here, bf16[4,32,32,128]{3,2,1,0:T(8,128)(2,1)} %all-to-all-done.3.own, bf16[4,32,32,128]{3,2,1,0:T(8,128)(2,1)} %collective-permute-done.12.other, bf16[1024,512]{1,0:T(8,128)(2,1)} %shard_map.145.dual_map), custom_call_target="tpu_custom_call" | custom-call | flops 1073741824 | bytes 8388608 | tf_op jit(solution)/shard_map/pallas_call | solution.py:199
  (112 shorter events, 15.9 us)
Async XLA Ops:
  0.0 16.8 %copy-start = (bf16[4096,128]{1,0:T(8,128)(2,1)S(1)}, bf16[4096,128]{1,0:T(8,128)(2,1)}, u32[]{:S(2)}) copy-start(bf16[4096,128]{1,0:T(8,128)(2,1)} %param.18) | copy-start | bytes 3145732
  0.0 19.2 %copy-start.1 = (bf16[32,4096]{1,0:T(8,128)(2,1)S(1)}, bf16[32,4096]{1,0:T(8,128)(2,1)}, u32[]{:S(2)}) copy-start(bf16[32,4096]{1,0:T(8,128)(2,1)} %param.15) | copy-start | bytes 786436
  0.0 19.2 %copy-start.5 = (f32[4096]{0:T(1024)S(1)}, f32[4096]{0:T(1024)}, u32[]{:S(2)}) copy-start(f32[4096]{0:T(1024)} %param.16) | copy-start | bytes 49156
  0.0 18.4 %copy-start.9 = (f32[128]{0:T(128)S(1)}, f32[128]{0:T(128)}, u32[]{:S(2)}) copy-start(f32[128]{0:T(128)} %param.22) | copy-start | bytes 1540
  2.0 41.7 %all-to-all-start = ((bf16[32,32,512]{2,1,0:T(8,128)(2,1)}), bf16[32,32,512]{2,1,0:T(8,128)(2,1)S(1)}, u32[]{:S(2)}, u32[]{:S(2)}) async-start(bf16[32,32,512]{2,1,0:T(8,128)(2,1)} %broadcast_in_dim.27), calls=%async_computation | async-start | bytes 2097152 | tf_op jit(solution)/shard_map/all_to_all | solution.py:51
  13.6 13.8 %copy-start.2 = (bf16[4096,128]{1,0:T(8,128)(2,1)S(1)}, bf16[4096,128]{1,0:T(8,128)(2,1)}, u32[]{:S(2)}) copy-start(bf16[4096,128]{1,0:T(8,128)(2,1)} %param.19) | copy-start | bytes 3145732
  16.8 2.4 %copy-start.8 = (f32[32]{0:T(128)}, f32[32]{0:T(128)S(1)}, u32[]{:S(2)}) copy-start(f32[32]{0:T(128)S(1)} %add_rsqrt_fusion.2) | copy-start | bytes 388
  33.5 1.4 collective-permute-start.4
  35.0 5.9 %collective-permute-start.5 = (bf16[32,512]{1,0:T(8,128)(2,1)S(1)}, bf16[32,512]{1,0:T(8,128)(2,1)S(1)}, u32[]{:S(2)}, u32[]{:S(2)}) collective-permute-start(bf16[32,512]{1,0:T(8,128)(2,1)S(1)} %get-tuple-element.16), channel_id=1, source_target_pairs={{0,64},{32,96},{64,128},{96,160},{128,192},{160,224},{192,0},{224,... | collective-permute-start | bytes 98312 | tf_op jit(solution)/shard_map/ppermute | solution.py:341
  36.7 5.4 %collective-permute-start.6 = (bf16[32,512]{1,0:T(8,128)(2,1)S(1)}, bf16[32,512]{1,0:T(8,128)(2,1)S(1)}, u32[]{:S(2)}, u32[]{:S(2)}) collective-permute-start(bf16[32,512]{1,0:T(8,128)(2,1)S(1)} %get-tuple-element.18), channel_id=1, source_target_pairs={{0,128},{32,160},{64,192},{96,224},{128,0},{160,32},{192,64},{224,... | collective-permute-start | bytes 98312 | tf_op jit(solution)/shard_map/ppermute | solution.py:341
  39.6 3.9 %collective-permute-start.7 = (bf16[32,512]{1,0:T(8,128)(2,1)S(1)}, bf16[32,512]{1,0:T(8,128)(2,1)S(1)}, u32[]{:S(2)}, u32[]{:S(2)}) collective-permute-start(bf16[32,512]{1,0:T(8,128)(2,1)S(1)} %get-tuple-element.17), channel_id=1, source_target_pairs={{0,192},{32,224},{64,0},{96,32},{128,64},{160,96},{192,128},{224,1... | collective-permute-start | bytes 98312 | tf_op jit(solution)/shard_map/ppermute | solution.py:341
  43.5 20.8 %copy-start.10 = (bf16[512,512]{1,0:T(8,128)(2,1)S(1)}, bf16[512,512]{1,0:T(8,128)(2,1)}, u32[]{:S(2)}) copy-start(bf16[512,512]{1,0:T(8,128)(2,1)} %param.28) | copy-start | bytes 1572868
  44.1 1.3 collective-permute-start.8
  45.5 22.5 %copy-start.7 = (s32[512,1]{0,1:T(1,128)S(1)}, s32[512,1]{0,1:T(1,128)}, u32[]{:S(2)}) copy-start(s32[512,1]{0,1:T(1,128)} %param.29) | copy-start | bytes 6148
  45.5 5.4 %collective-permute-start.10 = (f32[40,128]{1,0:T(8,128)S(1)}, f32[40,128]{1,0:T(8,128)S(1)}, u32[]{:S(2)}, u32[]{:S(2)}) collective-permute-start(f32[40,128]{1,0:T(8,128)S(1)} %get-tuple-element.34), channel_id=1, source_target_pairs={{0,128},{32,160},{64,192},{96,224},{128,0},{160,32},{192,64},{224,... | collective-permute-start | bytes 61448 | tf_op jit(solution)/shard_map/ppermute | solution.py:341
  47.1 3.9 %collective-permute-start.11 = (f32[40,128]{1,0:T(8,128)S(1)}, f32[40,128]{1,0:T(8,128)S(1)}, u32[]{:S(2)}, u32[]{:S(2)}) collective-permute-start(f32[40,128]{1,0:T(8,128)S(1)} %get-tuple-element.35), channel_id=1, source_target_pairs={{0,192},{32,224},{64,0},{96,32},{128,64},{160,96},{192,128},{224,1... | collective-permute-start | bytes 61448 | tf_op jit(solution)/shard_map/ppermute | solution.py:341
  48.5 5.0 %collective-permute-start.9 = (f32[40,128]{1,0:T(8,128)S(1)}, f32[40,128]{1,0:T(8,128)S(1)}, u32[]{:S(2)}, u32[]{:S(2)}) collective-permute-start(f32[40,128]{1,0:T(8,128)S(1)} %get-tuple-element.33), channel_id=1, source_target_pairs={{0,64},{32,96},{64,128},{96,160},{128,192},{160,224},{192,0},{224,... | collective-permute-start | bytes 61448 | tf_op jit(solution)/shard_map/ppermute | solution.py:341
  54.5 28.1 %all-to-all-start.1 = ((bf16[32,80,128]{2,1,0:T(8,128)(2,1)}), bf16[32,80,128]{2,1,0:T(8,128)(2,1)S(1)}, u32[]{:S(2)}, u32[]{:S(2)}) async-start(bf16[32,80,128]{2,1,0:T(8,128)(2,1)} %broadcast_in_dim.32), calls=%async_computation.1 | async-start | bytes 1310720 | tf_op jit(solution)/shard_map/all_to_all | solution.py:51
  67.7 19.1 %collective-permute-start = (bf16[2048,128]{1,0:T(8,128)(2,1)S(1)}, bf16[2048,128]{1,0:T(8,128)(2,1)}, u32[]{:S(2)}, u32[]{:S(2)}) collective-permute-start(bf16[2048,128]{1,0:T(8,128)(2,1)S(1)} %bitcast.133), channel_id=1, source_target_pairs={{0,32},{32,0},{64,96},{96,64},{128,160},{160,128},{192,224},{224,1... | collective-permute-start | bytes 1572872 | tf_op jit(solution)/shard_map/ppermute | solution.py:72
  83.4 17.0 %all-to-all-start.4 = ((bf16[8,32,512]{2,1,0:T(8,128)(2,1)}), bf16[8,32,512]{2,1,0:T(8,128)(2,1)S(1)}, u32[]{:S(2)}, u32[]{:S(2)}) async-start(bf16[8,32,512]{2,1,0:T(8,128)(2,1)} %broadcast_in_dim.34), calls=%async_computation.4 | async-start | bytes 524288 | tf_op jit(solution)/shard_map/all_to_all | solution.py:51
  89.0 7.7 %collective-permute-start.1 = (bf16[512,128]{1,0:T(8,128)(2,1)S(1)}, bf16[512,128]{1,0:T(8,128)(2,1)S(1)}, u32[]{:S(2)}, u32[]{:S(2)}) collective-permute-start(bf16[512,128]{1,0:T(8,128)(2,1)S(1)} %get-tuple-element.13), channel_id=1, source_target_pairs={{0,64},{32,96},{64,128},{96,160},{128,192},{160,224},{192,0},{224,... | collective-permute-start | bytes 393224 | tf_op jit(solution)/shard_map/ppermute | solution.py:341
  89.1 7.6 %collective-permute-start.2 = (bf16[512,128]{1,0:T(8,128)(2,1)S(1)}, bf16[512,128]{1,0:T(8,128)(2,1)S(1)}, u32[]{:S(2)}, u32[]{:S(2)}) collective-permute-start(bf16[512,128]{1,0:T(8,128)(2,1)S(1)} %get-tuple-element.15), channel_id=1, source_target_pairs={{0,128},{32,160},{64,192},{96,224},{128,0},{160,32},{192,64},{224,... | collective-permute-start | bytes 393224 | tf_op jit(solution)/shard_map/ppermute | solution.py:341
  91.0 6.5 %collective-permute-start.3 = (bf16[512,128]{1,0:T(8,128)(2,1)S(1)}, bf16[512,128]{1,0:T(8,128)(2,1)S(1)}, u32[]{:S(2)}, u32[]{:S(2)}) collective-permute-start(bf16[512,128]{1,0:T(8,128)(2,1)S(1)} %get-tuple-element.14), channel_id=1, source_target_pairs={{0,192},{32,224},{64,0},{96,32},{128,64},{160,96},{192,128},{224,1... | collective-permute-start | bytes 393224 | tf_op jit(solution)/shard_map/ppermute | solution.py:341
  100.4 44.6 %copy-start.4 = (bf16[8,32,512]{2,1,0:T(8,128)(2,1)}, bf16[8,32,512]{2,1,0:T(8,128)(2,1)S(1)}, u32[]{:S(2)}) copy-start(bf16[8,32,512]{2,1,0:T(8,128)(2,1)S(1)} %all-to-all-done.4.refs_0_) | copy-start | bytes 786436
  100.4 20.1 %all-to-all-start.2 = ((bf16[32,32,128]{2,1,0:T(8,128)(2,1)}), bf16[32,32,128]{2,1,0:T(8,128)(2,1)S(1)}, u32[]{:S(2)}, u32[]{:S(2)}) async-start(bf16[32,32,128]{2,1,0:T(8,128)(2,1)} %bitcast.48), calls=%async_computation.2 | async-start | bytes 524288 | tf_op jit(solution)/shard_map/all_to_all | solution.py:415
  110.7 34.3 %copy-start.3 = (bf16[32,64,128]{2,1,0:T(8,128)(2,1)}, bf16[32,64,128]{2,1,0:T(8,128)(2,1)S(1)}, u32[]{:S(2)}) copy-start(bf16[32,64,128]{2,1,0:T(8,128)(2,1)S(1)} %slice.76.refs_4_) | copy-start | bytes 1572868
  110.7 19.9 %collective-permute-start.17 = (bf16[32,64,128]{2,1,0:T(8,128)(2,1)S(1)}, bf16[32,64,128]{2,1,0:T(8,128)(2,1)S(1)}, u32[]{:S(2)}, u32[]{:S(2)}) collective-permute-start(bf16[32,64,128]{2,1,0:T(8,128)(2,1)S(1)} %slice.76.refs_4_), channel_id=1, source_target_pairs={{0,64},{32,96},{64,128},{96,160},{128,192},{160,224},{192,0},{224,... | collective-permute-start | bytes 1572872 | tf_op jit(solution)/shard_map/ppermute | solution.py:60
  111.5 19.2 %collective-permute-start.16 = (bf16[32,64,128]{2,1,0:T(8,128)(2,1)S(1)}, bf16[32,64,128]{2,1,0:T(8,128)(2,1)}, u32[]{:S(2)}, u32[]{:S(2)}) collective-permute-start(bf16[32,64,128]{2,1,0:T(8,128)(2,1)S(1)} %slice.76.refs_4_), channel_id=1, source_target_pairs={{0,192},{32,224},{64,0},{96,32},{128,64},{160,96},{192,128},{224,1... | collective-permute-start | bytes 1572872 | tf_op jit(solution)/shard_map/ppermute | solution.py:60
  121.6 21.4 %all-to-all-start.3 = ((bf16[4,32,32,128]{3,2,1,0:T(8,128)(2,1)}), bf16[4,32,32,128]{3,2,1,0:T(8,128)(2,1)}, u32[]{:S(2)}, u32[]{:S(2)}) async-start(bf16[4,32,32,128]{3,2,1,0:T(8,128)(2,1)} %broadcast_in_dim.33), calls=%async_computation.3 | async-start | bytes 2097152 | tf_op jit(solution)/shard_map/all_to_all | solution.py:51
  125.8 7.8 %collective-permute-start.13 = (bf16[8,32,512]{2,1,0:T(8,128)(2,1)S(1)}, bf16[8,32,512]{2,1,0:T(8,128)(2,1)S(1)}, u32[]{:S(2)}, u32[]{:S(2)}) collective-permute-start(bf16[8,32,512]{2,1,0:T(8,128)(2,1)S(1)} %all-to-all-done.4.refs_0_), channel_id=1, source_target_pairs={{0,3},{1,0},{2,1},{3,2},{4,7},{5,4},{6,5},{7,6},{8,11},{9,8},{10,9... | collective-permute-start | bytes 786440 | tf_op jit(solution)/shard_map/ppermute | solution.py:391
  127.9 9.6 %collective-permute-start.14 = (bf16[8,32,512]{2,1,0:T(8,128)(2,1)S(1)}, bf16[8,32,512]{2,1,0:T(8,128)(2,1)}, u32[]{:S(2)}, u32[]{:S(2)}) collective-permute-start(bf16[8,32,512]{2,1,0:T(8,128)(2,1)S(1)} %all-to-all-done.4.refs_0_), channel_id=1, source_target_pairs={{0,2},{1,3},{2,0},{3,1},{4,6},{5,7},{6,4},{7,5},{8,10},{9,11},{10,... | collective-permute-start | bytes 786440 | tf_op jit(solution)/shard_map/ppermute | solution.py:391
  128.8 8.6 %collective-permute-start.15 = (bf16[8,32,512]{2,1,0:T(8,128)(2,1)S(1)}, bf16[8,32,512]{2,1,0:T(8,128)(2,1)}, u32[]{:S(2)}, u32[]{:S(2)}) collective-permute-start(bf16[8,32,512]{2,1,0:T(8,128)(2,1)S(1)} %all-to-all-done.4.refs_0_), channel_id=1, source_target_pairs={{0,1},{1,2},{2,3},{3,0},{4,5},{5,6},{6,7},{7,4},{8,9},{9,10},{10,1... | collective-permute-start | bytes 786440 | tf_op jit(solution)/shard_map/ppermute | solution.py:391
  130.6 13.0 %copy-start.6 = (bf16[32,64,128]{2,1,0:T(8,128)(2,1)}, bf16[32,64,128]{2,1,0:T(8,128)(2,1)S(1)}, u32[]{:S(2)}) copy-start(bf16[32,64,128]{2,1,0:T(8,128)(2,1)S(1)} %collective-permute-done.17.refs_6_) | copy-start | bytes 1572868
  130.6 12.3 %collective-permute-start.20 = (bf16[32,64,128]{2,1,0:T(8,128)(2,1)S(1)}, bf16[32,64,128]{2,1,0:T(8,128)(2,1)}, u32[]{:S(2)}, u32[]{:S(2)}) collective-permute-start(bf16[32,64,128]{2,1,0:T(8,128)(2,1)S(1)} %slice.76.refs_4_), channel_id=1, source_target_pairs={{0,32},{32,0},{64,96},{96,64},{128,160},{160,128},{192,224},{224,1... | collective-permute-start | bytes 1572872 | tf_op jit(solution)/shard_map/ppermute | solution.py:72
  130.7 11.7 %collective-permute-start.18 = (bf16[16,64,128]{2,1,0:T(8,128)(2,1)S(1)}, bf16[16,64,128]{2,1,0:T(8,128)(2,1)}, u32[]{:S(2)}, u32[]{:S(2)}) collective-permute-start(bf16[16,64,128]{2,1,0:T(8,128)(2,1)S(1)} %slice.77), channel_id=1, source_target_pairs={{0,64},{32,96},{64,128},{96,160},{128,192},{160,224},{192,0},{224,... | collective-permute-start | bytes 786440 | tf_op jit(solution)/shard_map/ppermute | solution.py:60
  133.6 0.7 copy-start.11
  134.4 8.5 %collective-permute-start.19 = (bf16[16,64,128]{2,1,0:T(8,128)(2,1)S(1)}, bf16[16,64,128]{2,1,0:T(8,128)(2,1)}, u32[]{:S(2)}, u32[]{:S(2)}) collective-permute-start(bf16[16,64,128]{2,1,0:T(8,128)(2,1)S(1)} %slice.78), channel_id=1, source_target_pairs={{0,192},{32,224},{64,0},{96,32},{128,64},{160,96},{192,128},{224,1... | collective-permute-start | bytes 786440 | tf_op jit(solution)/shard_map/ppermute | solution.py:60
  137.5 7.5 %collective-permute-start.21 = (bf16[32,64,128]{2,1,0:T(8,128)(2,1)}, bf16[32,64,128]{2,1,0:T(8,128)(2,1)}, u32[]{:S(2)}, u32[]{:S(2)}) collective-permute-start(bf16[32,64,128]{2,1,0:T(8,128)(2,1)} %collective-permute-done.16.refs_5_), channel_id=1, source_target_pairs={{0,32},{32,0},{64,96},{96,64},{128,160},{160,128},{192,224},{224,1... | collective-permute-start | bytes 1572872 | tf_op jit(solution)/shard_map/ppermute | solution.py:72
  137.5 7.5 %collective-permute-start.22 = (bf16[32,64,128]{2,1,0:T(8,128)(2,1)S(1)}, bf16[32,64,128]{2,1,0:T(8,128)(2,1)}, u32[]{:S(2)}, u32[]{:S(2)}) collective-permute-start(bf16[32,64,128]{2,1,0:T(8,128)(2,1)S(1)} %collective-permute-done.17.refs_6_), channel_id=1, source_target_pairs={{0,32},{32,0},{64,96},{96,64},{128,160},{160,128},{192,224},{224,1... | collective-permute-start | bytes 1572872 | tf_op jit(solution)/shard_map/ppermute | solution.py:72
  142.4 2.6 %collective-permute-start.23 = (bf16[16,64,128]{2,1,0:T(8,128)(2,1)}, bf16[16,64,128]{2,1,0:T(8,128)(2,1)}, u32[]{:S(2)}, u32[]{:S(2)}) collective-permute-start(bf16[16,64,128]{2,1,0:T(8,128)(2,1)} %collective-permute-done.18.refs_7_), channel_id=1, source_target_pairs={{0,32},{32,0},{64,96},{96,64},{128,160},{160,128},{192,224},{224,1... | collective-permute-start | bytes 786440 | tf_op jit(solution)/shard_map/ppermute | solution.py:72
  142.9 2.1 %collective-permute-start.24 = (bf16[16,64,128]{2,1,0:T(8,128)(2,1)}, bf16[16,64,128]{2,1,0:T(8,128)(2,1)}, u32[]{:S(2)}, u32[]{:S(2)}) collective-permute-start(bf16[16,64,128]{2,1,0:T(8,128)(2,1)} %collective-permute-done.19.refs_8_), channel_id=1, source_target_pairs={{0,32},{32,0},{64,96},{96,64},{128,160},{160,128},{192,224},{224,1... | collective-permute-start | bytes 786440 | tf_op jit(solution)/shard_map/ppermute | solution.py:72
  143.0 22.3 %collective-permute-start.12 = (bf16[4,32,32,128]{3,2,1,0:T(8,128)(2,1)}, bf16[4,32,32,128]{3,2,1,0:T(8,128)(2,1)}, u32[]{:S(2)}, u32[]{:S(2)}) collective-permute-start(bf16[4,32,32,128]{3,2,1,0:T(8,128)(2,1)} %all-to-all-done.3.own), channel_id=1, source_target_pairs={{0,32},{32,0},{64,96},{96,64},{128,160},{160,128},{192,224},{224,1... | collective-permute-start | bytes 3145736 | tf_op jit(solution)/shard_map/ppermute | solution.py:72

commit v5 on v4

--- a/solution.py
+++ b/solution.py
@@ -40,12 +40,6 @@
 ANY = pl.BlockSpec(memory_space=pl.ANY)
 
 
-def contract_last(left, right):
-    return lax.dot_general(
-        left, right, (((1,), (1,)), ((), ())), preferred_element_type=jnp.float32
-    )
-
-
 def spread(block, axis, count, groups=None):
     copies = jnp.broadcast_to(block[None], (count,) + block.shape)
     return lax.all_to_all(copies, axis, 0, 0, tiled=True, axis_index_groups=groups)
@@ -59,10 +53,7 @@
             pairs.append((i, i + ((at + step) % count - at) * stride))
         return lax.ppermute(array, axis, pairs)
 
-    below, above = [block], [block]
-    for _ in range(count // 2 - 1):
-        below.append(move(below[-1], 1))
-        above.append(move(above[-1], -1))
+    below, above = [block, move(block, 1)], [block, move(block, -1)]
     middle = block.shape[0] // 2
     far = [move(below[-1][:middle], 1), move(above[-1][middle:], -1)]
     return above + below[:0:-1] + far
@@ -70,17 +61,6 @@
 
 def swap_cores(block, size):
     return lax.ppermute(block, "mp", [(i, i ^ 1) for i in range(size)])
-
-
-def halves(array):
-    high = lax.reduce_precision(array, 8, 7)
-    return high.astype(jnp.bfloat16), (array - high).astype(jnp.bfloat16)
-
-
-def norm_rows(squares, width):
-    high, low = halves(squares)
-    line = jnp.concatenate([high, low])
-    return jnp.pad(line[None, :], ((0, 15), (0, width - line.shape[0])))
 
 
 def tiles(body, init=0):
@@ -98,15 +78,100 @@
     return copies
 
 
+def flat_dot(left, right):
+    return lax.dot_general(
+        left, right, (((1,), (1,)), ((), ())), preferred_element_type=jnp.float32
+    )
+
+
+def both(value):
+    high = value.astype(jnp.bfloat16)
+    return high, (value - high.astype(jnp.float32)).astype(jnp.bfloat16)
+
+
+def norm_block(value):
+    high = value.astype(jnp.bfloat16).astype(jnp.float32)
+    row = lax.broadcasted_iota(jnp.int32, (16, value.shape[1]), 0)
+    block = jnp.where(row == 0, high, jnp.where(row == 1, value - high, 0.0))
+    return block.astype(jnp.bfloat16)
+
+
+def fill(target, slab, gram, norms):
+    target[:512] = slab.astype(jnp.bfloat16)
+    target[512:544], target[544:576] = both(gram)
+    target[576:592] = norms
+
+
+def parts_kernel(here, slab, old_mine, old_all, squares, theirs, kept):
+    norms = norm_block(squares[...])
+    for y in range(4):
+        for side in range(2):
+            at = 2 * y + (here[0] if side else 1 - here[0])
+            block = old_all[pl.ds(pl.multiple_of(at * 128, 128), 128), :]
+            slab_part, gram_part = flat_dot(slab[...], block), flat_dot(old_mine[...], block)
+            if side:
+                kept[y, :512] = slab_part
+                kept[y, 512:] = gram_part
+            else:
+                fill(theirs.at[y], slab_part, gram_part, norms)
+
+
+def wide_sum(block):
+    value = block.astype(jnp.float32)
+    return value[:512], value[512:544] + value[544:576]
+
+
+def pair_kernel(here, kept, theirs, squares, mine, total_squares, *pieces):
+    total = squares[...] + jnp.sum(theirs[0, 576:].astype(jnp.float32), axis=0, keepdims=True)
+    total_squares[...] = total
+    norms = norm_block(total)
+    for step in range(4):
+        at = lax.rem(here[1] + step, 4)
+        slab_part, gram_part = wide_sum(theirs[at])
+        slab_part = kept[at, :512] + slab_part
+        gram_part = kept[at, 512:] + gram_part
+        if step:
+            fill(pieces[step - 1], slab_part, gram_part, norms)
+        else:
+            mine[:512] = slab_part
+            mine[512:] = gram_part
+
+
+def route_kernel(target, mine, squares, *refs):
+    pieces, outgoing = refs[:3], refs[3]
+    slab_part, gram_part, total = mine[:512], mine[512:], squares[...]
+    for piece in pieces:
+        more_slab, more_gram = wide_sum(piece[...])
+        slab_part, gram_part = slab_part + more_slab, gram_part + more_gram
+        total = total + jnp.sum(piece[576:].astype(jnp.float32), axis=0, keepdims=True)
+    slab_part = slab_part.astype(jnp.bfloat16)
+    for tile in range(4):
+        row = lax.broadcasted_iota(jnp.int32, (256, 512), 0) + 256 * tile
+        chosen = jnp.where(row == target[...], 1.0, 0.0).astype(jnp.bfloat16)
+        block = jnp.dot(chosen, slab_part, preferred_element_type=jnp.float32)
+        outgoing[8 * tile : 8 * tile + 8, :32] = block.astype(jnp.bfloat16).reshape(8, 32, 128)
+    high, low = both(gram_part)
+    norms = norm_block(total)
+    for owner in range(32):
+        outgoing[owner, 32:64] = high
+        outgoing[owner, 64:96] = low
+        outgoing[owner, 96:112] = norms
+
+
+def join_kernel(here, *refs):
+    pieces, state = refs[:4], refs[4]
+    for step, piece in enumerate(pieces):
+        at = lax.rem(here[2] + step, 4)
+        for z in range(8):
+            state[z, at] = piece[z]
+
+
 def solve_kernel(here, scale, gain, *refs):
-    states, grams, result = refs[:4], refs[4:14], refs[14]
-    state, high, low, rho, rho_high, rho_low, image, way, way_image, total = refs[15:25]
-    state_sems, gram_sems = refs[25:]
+    source, grams, slabs, result = refs[0], refs[1:11], refs[11:13], refs[13]
+    state, high, low, rho, rho_high, rho_low, image, way, way_image, total = refs[14:24]
+    routed, dual_map, state_sems, gram_sems, slab_sems = refs[24:]
     ridge = 0.125 * D
-    placed = [
-        (piece, state.at[:, lax.rem(here[2] + step, 4)]) for step, piece in enumerate(states)
-    ]
-    state_copies = copy_all(placed, state_sems)
+    state_copies = copy_all([(source, state)], state_sems)
     placed = []
     for index, piece in enumerate(grams):
         step, row = ((0, 0), (1, 0), (3, 0), (2, 0), (2, 16))[index % 5]
@@ -117,6 +182,12 @@
         placed.append((piece.at[:, :docs], high.at[rows, :, at]))
         placed.append((piece.at[:, docs:], low.at[rows, :, at]))
     gram_copies = copy_all(placed, gram_sems)
+    placed = []
+    for y in range(4):
+        for side, piece in enumerate(slabs):
+            at = 2 * y + (1 - here[0] if side else here[0])
+            placed.append((piece.at[y], routed.at[:, :, columns(at)]))
+    slab_copies = copy_all(placed, slab_sems)
     for copy in state_copies:
         copy.wait()
 
@@ -185,7 +256,7 @@
                 total[rows, :] = moved
                 split(rows, rho[rows, :] - alpha * (way_image[rows, :] + ridge * step))
             else:
-                result[rows, :] = moved.astype(jnp.bfloat16)
+                dual_map[rows, :] = moved.astype(jnp.bfloat16)
             return carry
 
         tiles(update)
@@ -194,17 +265,52 @@
             ratio = new_sq / res_sq
             res_sq = new_sq
 
-
-def call(kernel, out_shape, in_specs, scratch, operands, flops):
+    for copy in slab_copies:
+        copy.wait()
+
+    def last(i, carry):
+        result[rows_of(i), :] = dot(gram_rows(routed, i), dual_map[...]).astype(jnp.bfloat16)
+        return carry
+
+    tiles(last)
+
+
+def call(kernel, shapes, in_specs, scratch, operands, flops, limit):
     return pl.pallas_call(
         kernel,
-        out_shape=out_shape,
+        out_shape=shapes,
         in_specs=in_specs,
-        out_specs=VMEM,
+        out_specs=jax.tree.map(lambda _: VMEM, shapes),
         scratch_shapes=scratch,
-        cost_estimate=pl.CostEstimate(flops=flops, bytes_accessed=1 << 23, transcendentals=0),
-        compiler_params=pltpu.CompilerParams(vmem_limit_bytes=62 << 20),
+        cost_estimate=pl.CostEstimate(flops=flops, bytes_accessed=1 << 21, transcendentals=0),
+        compiler_params=pltpu.CompilerParams(vmem_limit_bytes=limit << 20),
     )(*operands)
+
+
+def join(*operands):
+    shape = jax.ShapeDtypeStruct((8, 4) + operands[1].shape[1:], jnp.bfloat16)
+    return call(join_kernel, shape, [SMEM] + [VMEM] * 4, [], operands, 1 << 20, 16)
+
+
+def make_parts(*operands):
+    shapes = (
+        jax.ShapeDtypeStruct((4, 592, 128), jnp.bfloat16),
+        jax.ShapeDtypeStruct((4, 544, 128), jnp.float32),
+    )
+    return call(parts_kernel, shapes, [SMEM] + [VMEM] * 4, [], operands, 1 << 30, 62)
+
+
+def add_pair(*operands):
+    shapes = (
+        jax.ShapeDtypeStruct((544, 128), jnp.float32),
+        jax.ShapeDtypeStruct((1, 128), jnp.float32),
+    ) + (jax.ShapeDtypeStruct((592, 128), jnp.bfloat16),) * 3
+    return call(pair_kernel, shapes, [SMEM] + [VMEM] * 3, [], operands, 1 << 20, 16)
+
+
+def route(*operands):
+    shape = jax.ShapeDtypeStruct((32, 112, 128), jnp.bfloat16)
+    return call(route_kernel, shape, [VMEM] * 6, [], operands, 1 << 27, 16)
 
 
 def solve(*operands):
@@ -215,45 +321,14 @@
     return call(
         solve_kernel,
         jax.ShapeDtypeStruct((anchors, cols), jnp.bfloat16),
-        [SMEM, VMEM, VMEM] + [ANY] * 14,
+        [SMEM, VMEM, VMEM] + [ANY] * 13,
         [pltpu.VMEM((8, 4, anchors // 32, cols), jnp.bfloat16), wide, wide, full, half, half]
         + [full] * 4
-        + [pltpu.SemaphoreType.DMA((4,)), pltpu.SemaphoreType.DMA((20,))],
+        + [wide, half]
+        + [pltpu.SemaphoreType.DMA((count,)) for count in (1, 20, 8)],
         operands,
         18 * anchors * anchors * cols,
-    )
-
-
-def apply_kernel(here, own, other, dual_map, result, routed, sems):
-    placed = []
-    for y in range(4):
-        placed.append((own.at[y], routed.at[:, :, columns(2 * y + here[0])]))
-        placed.append((other.at[y], routed.at[:, :, columns(2 * y + 1 - here[0])]))
-    for copy in copy_all(placed, sems):
-        copy.wait()
-
-    def product(i, carry):
-        rows = routed[pl.ds(8 * i, 8)].reshape(TILE, -1)
-        value = jnp.dot(rows, dual_map[...], preferred_element_type=jnp.float32)
-        result[pl.ds(pl.multiple_of(i * TILE, TILE), TILE), :] = value.astype(jnp.bfloat16)
-        return carry
-
-    tiles(product)
-
-
-def apply_map(*operands):
-    anchors, cols = operands[3].shape
-    blocks, slots = operands[1].shape[1:3]
-    return call(
-        apply_kernel,
-        jax.ShapeDtypeStruct((blocks * slots, cols), jnp.bfloat16),
-        [SMEM, ANY, ANY, VMEM],
-        [
-            pltpu.VMEM((blocks, slots, anchors), jnp.bfloat16),
-            pltpu.SemaphoreType.DMA((8,)),
-        ],
-        operands,
-        2 * anchors * anchors * cols,
+        62,
     )
 
 
@@ -363,26 +438,6 @@
     part = anchors // mp_count
     old_all = old_all.reshape(anchors, cols)
 
-    def by_part(array):
-        return array.reshape(-1, mp_count, part).transpose(1, 0, 2).reshape(chips, 2, -1, part)
-
-    def reduce_mp(parts, extra):
-        count, kind = parts.shape[2], parts.dtype
-        theirs = lax.dynamic_index_in_dim(parts, 1 - core, 1, False)
-        theirs = jnp.concatenate([theirs.reshape(chips * count, part), *extra], axis=0)
-        theirs = swap_cores(theirs, mp_count).astype(jnp.float32)
-        parts = lax.dynamic_index_in_dim(parts, core, 1, False).astype(jnp.float32)
-        parts = parts + theirs[: chips * count].reshape(parts.shape)
-        extra = [rows + theirs[chips * count :] for rows in extra]
-        total = lax.dynamic_index_in_dim(parts, chip, 0, False)
-        parts = parts.astype(kind)
-        total = jnp.concatenate([total, *extra], axis=0)
-        for step in range(1, chips):
-            piece = lax.dynamic_index_in_dim(parts, (chip + step) % chips, 0, False)
-            piece = shift_chips(jnp.concatenate([piece, *extra], axis=0), step)
-            total = total + piece.astype(jnp.float32)
-        return total
-
     state = state.astype(half)
     state_column = spread(state, "rows", column, by_z)
     states = [state_column]
@@ -390,41 +445,39 @@
         pairs = [(i, i // line * line + (i - step) % line) for i in range(rows_count)]
         states.append(lax.ppermute(state_column, "rows", pairs))
 
-    extra = jnp.pad(squares[None, :], ((0, 7), (0, part - docs)))
-    gram = reduce_mp(by_part(contract_last(old_mine, old_all)), [extra])
-    gram = jnp.concatenate([*halves(gram[:docs]), norm_rows(gram[docs, :docs], part)], axis=0)
-    arrived = spread(gram, "rows", rows_count)
-    gram = arrived[:, : 2 * docs]
-    squares = arrived[:, 2 * docs].astype(jnp.float32)
-    squares = squares[:, :docs] + squares[:, docs : 2 * docs]
-    scale_rows = lax.rsqrt(squares / width + 1e-06).reshape(anchors, 1)
-
-    count = slab.shape[0]
-    slab_part = by_part(contract_last(slab, old_all).astype(half))
-    slab_dual = reduce_mp(slab_part, []).astype(half)
-    capacity = 2 * count // rows_count
+    here = jnp.stack([core, chip, lax.axis_index("rows") % line, jnp.zeros_like(core)])
+    here = here.astype(jnp.int32)
+    state_all = join(here, *states)
+
+    capacity = 2 * slab.shape[0] // rows_count
     owner_ids = owners[:, 0]
     onehot = (owner_ids[:, None] == jnp.arange(rows_count, dtype=jnp.int32)[None, :]).astype(
         jnp.int32
     )
     counted = jnp.cumsum(onehot, axis=0)
     slot = jnp.sum((counted - 1) * onehot, axis=-1)
-    target = owner_ids * capacity + slot
-    routed = jnp.zeros((rows_count * capacity, part), half).at[target].set(slab_dual)
-    routed, _ = lax.optimization_barrier((routed, arrived))
-    routed = lax.all_to_all(routed.reshape(rows_count, capacity, part), "rows", 0, 0, tiled=True)
+    target = (owner_ids * capacity + slot).reshape(1, -1)
+
+    squares = jnp.pad(squares[None, :], ((0, 0), (0, part - docs)))
+    theirs, kept = make_parts(here, slab, old_mine, old_all, squares)
+    theirs = swap_cores(theirs, mp_count)
+    kept, squares, *pieces = add_pair(here, kept, theirs, squares)
+    pieces = [shift_chips(piece, step) for step, piece in enumerate(pieces, 1)]
+    outgoing = route(target, kept, squares, *pieces)
+    arrived = lax.all_to_all(outgoing, "rows", 0, 0, tiled=True)
+    routed = arrived[:, :capacity]
+    gram = arrived[:, capacity : capacity + 2 * docs]
+    squares = arrived[:, capacity + 2 * docs : capacity + 2 * docs + 2, :docs]
+    squares = jnp.sum(squares.astype(jnp.float32), axis=1)
+    scale_rows = lax.rsqrt(squares / width + 1e-06).reshape(anchors, 1)
 
     grams = ring(gram, "mp", chips, mp_count, 2)
     grams = grams + [swap_cores(piece, mp_count) for piece in grams]
-    routed_own = spread(routed, "mp", chips, by_y)
-    routed_other = swap_cores(routed_own, mp_count)
-
-    zero = jnp.zeros_like(core)
-    here = jnp.stack([core, chip, lax.axis_index("rows") % line, zero]).astype(jnp.int32)
-    dual_map = solve(
-        here, scale_rows, my_cols(final_gain, 0).reshape(1, cols), *states, *grams
-    )
-    return apply_map(here, routed_own, routed_other, dual_map)
+    slabs = spread(routed, "mp", chips, by_y)
+    slabs = [slabs, swap_cores(slabs, mp_count)]
+    return solve(
+        here, scale_rows, my_cols(final_gain, 0).reshape(1, cols), state_all, *grams, *slabs
+    )
 
 
 def solution(mesh):

time: 174 us -> 173 us (level)
  the two profiles are of different devices: /device:TPU:2 before, /device:TPU:1 now
where the time goes in v5:
time: 173 us; the launch traced here: 172 us
  starting transfers between devices  59.3 us (34%)
  waiting for transfers between devices  28.7 us (17%)
  blocking collectives  28.4 us (16%)
  Pallas kernels  27.9 us (16%)
  local copies, waits for them, and re-layouts  12.6 us (7%)
  matrix products  8.72 us (5%)
  other arithmetic  5.81 us (3%)
    all_to_all x1, blocking collectives, local(): arrived = lax.all_to_all(outgoing, 'rows', 0, 0, tiled=True)  28.4 us
    pallas_call x5, Pallas kernels, call(): pl.pallas_call(kernel, out_shape=shapes, in_specs=in_specs, out_specs=jax...  27.9 us
    all_to_all x3, starting transfers between devices, spread(): lax.all_to_all(copies, axis, 0, 0, tiled=True, axis_index_groups=groups)  21.9 us
    ppermute x8, starting transfers between devices, swap_cores(): return lax.ppermute(block, 'mp', [(i, i ^ 1) for i in range(size)])  16.7 us
    all_to_all x3, waiting for transfers between devices, spread(): lax.all_to_all(copies, axis, 0, 0, tiled=True, axis_index_groups=groups)  15.7 us
    ppermute x6, starting transfers between devices, shift_chips(): lax.ppermute(block, 'mp', [(i, (i + 2 * step) % mp_count) for i in range(...  9.51 us
    ppermute x6, waiting for transfers between devices, shift_chips(): lax.ppermute(block, 'mp', [(i, (i + 2 * step) % mp_count) for i in range(...  8.14 us
    ppermute x4, starting transfers between devices, move(): return lax.ppermute(array, axis, pairs)  6.34 us
  transfers between devices with their start and end apart: 24, of which 11 were waited for; matrix products, arithmetic and copies ran while one was open for 13% of the time, Pallas kernels for 0%

profile of v5, /device:TPU:1, one launch (start us, length us, event | category | flops | bytes accessed | tf_op | source)
XLA Modules:
  0.0 172.0 jit_solution(15150962595467462536)
XLA Ops:
  0.0 0.9 constant_dynamic-slice_fusion.2.old_mine
  0.9 1.1 broadcast_in_dim.16
  2.0 12.1 %all-to-all-start = ((bf16[32,32,512]{2,1,0:T(8,128)(2,1)}), bf16[32,32,512]{2,1,0:T(8,128)(2,1)}, u32[]{:S(2)}, u32[]{:S(2)}) async-start(bf16[32,32,512]{2,1,0:T(8,128)(2,1)} %broadcast_in_dim.16), calls=%async_computation | async-start | bytes 2097152 | tf_op jit(solution)/shard_map/all_to_all | solution.py:45
  14.1 0.7 convert_element_type.80
  14.9 0.7 iota_compare_fusion.2
  15.6 1.1 multiply_reduce_fusion
  16.8 1.5 multiply_reduce_fusion.3
  18.6 3.1 %fusion.31 = f32[32,512]{1,0:T(8,128)S(1)} fusion(bf16[4096,512]{1,0:T(8,128)(2,1)} %param.17, f32[4096]{0:T(1024)S(1)} %copy-done.9, f32[32]{0:T(128)S(1)} %add_rsqrt_fusion.3, bf16[32,4096]{1,0:T(8,128)(2,1)S(1)} %copy-done.5), kind=kOutput, calls=%fused_computation.77 | convolution fusion | flops 134742016 | bytes 4538496 | tf_op jit(solution)/shard_map/dot_general | solution.py:366
  23.6 3.0 %fusion.11 = f32[32,4096]{1,0:T(8,128)S(1)} fusion(bf16[512,4096]{1,0:T(8,128)(2,1)} %param.20, bf16[4,8,4,128]{3,2,1,0:T(4,128)(2,1)S(1)} %bitcast.70), kind=kOutput, calls=%fused_computation.31 | convolution fusion | flops 134217728 | bytes 4751360 | tf_op jit(solution)/shard_map/dot_general | solution.py:406
  27.5 1.0 collective-permute-start
  28.8 0.7 collective-permute-done
  29.6 1.4 collective-permute-start.1
  31.0 1.5 collective-permute-start.3
  32.5 1.6 collective-permute-start.2
  34.7 2.3 %collective-permute-done.2 = bf16[32,512]{1,0:T(8,128)(2,1)S(1)} collective-permute-done((bf16[32,512]{1,0:T(8,128)(2,1)S(1)}, bf16[32,512]{1,0:T(8,128)(2,1)S(1)}, u32[]{:S(2)}, u32[]{:S(2)}) %collective-permute-start.2) | collective-permute-done | bytes 32800 | tf_op jit(solution)/shard_map/ppermute | solution.py:416
  37.7 2.6 %all-to-all-done = bf16[32,32,512]{2,1,0:T(8,128)(2,1)} async-done(((bf16[32,32,512]{2,1,0:T(8,128)(2,1)}), bf16[32,32,512]{2,1,0:T(8,128)(2,1)}, u32[]{:S(2)}, u32[]{:S(2)}) %all-to-all-start) | async-done | bytes 1048608 | tf_op jit(solution)/shard_map/all_to_all | solution.py:45
  40.3 4.1 %shard_map.145 = (bf16[4,592,128]{2,1,0:T(8,128)(2,1)}, f32[4,544,128]{2,1,0:T(8,128)}) custom-call(s32[4]{0:T(128)} %pad_add_fusion.here, bf16[512,512]{1,0:T(8,128)(2,1)} %slab.1, bf16[32,512]{1,0:T(8,128)(2,1)} %copy-done.10, bf16[1024,512]{1,0:T(8,128)(2,1)} %bitcast.8.old_all, f32[1,128]{1,0:T(1,128)} %pad.4.squares), custom_call_target="tpu_custom_call" | custom-call | flops 1073741824 | bytes 2097152 | tf_op jit(solution)/shard_map/pallas_call | solution.py:279
  44.4 2.8 %collective-permute-start.4 = (bf16[4,592,128]{2,1,0:T(8,128)(2,1)}, bf16[4,592,128]{2,1,0:T(8,128)(2,1)S(1)}, u32[]{:S(2)}, u32[]{:S(2)}) collective-permute-start(bf16[4,592,128]{2,1,0:T(8,128)(2,1)} %get-tuple-element.13), channel_id=1, source_target_pairs={{0,32},{32,0},{64,96},{96,64},{128,160},{160,128},{192,224},{224,1... | collective-permute-start | bytes 1818632 | tf_op jit(solution)/shard_map/ppermute | solution.py:63
  47.2 1.2 reduce-window.6
  49.1 1.2 copy-done.1
  51.0 1.4 collective-permute-start.5
  52.4 2.6 %collective-permute-start.6 = (bf16[592,128]{1,0:T(8,128)(2,1)S(1)}, bf16[592,128]{1,0:T(8,128)(2,1)S(1)}, u32[]{:S(2)}, u32[]{:S(2)}) collective-permute-start(bf16[592,128]{1,0:T(8,128)(2,1)S(1)} %get-tuple-element.17), channel_id=1, source_target_pairs={{0,128},{32,160},{64,192},{96,224},{128,0},{160,32},{192,64},{224,... | collective-permute-start | bytes 454664 | tf_op jit(solution)/shard_map/ppermute | solution.py:416
  55.0 1.1 collective-permute-start.7
  56.0 1.5 collective-permute-done.5.refs_0_
  57.5 4.4 %collective-permute-done.6.refs_1_ = bf16[592,128]{1,0:T(8,128)(2,1)S(1)} collective-permute-done((bf16[592,128]{1,0:T(8,128)(2,1)S(1)}, bf16[592,128]{1,0:T(8,128)(2,1)S(1)}, u32[]{:S(2)}, u32[]{:S(2)}) %collective-permute-start.6) | collective-permute-done | bytes 151584 | tf_op jit(solution)/shard_map/ppermute | solution.py:416
  62.4 28.4 %all_to_all.20 = bf16[32,112,128]{2,1,0:T(8,128)(2,1)S(1)} all-to-all(bf16[32,112,128]{2,1,0:T(8,128)(2,1)S(1)} %shard_map.147), channel_id=1, replica_groups=mesh['mp'=8,'rows'=32] {'rows'}, dimensions={0} | all-to-all | bytes 1835008 | tf_op jit(solution)/shard_map/all_to_all | solution.py:467
  90.8 1.1 broadcast_in_dim.25
  91.9 4.2 %all-to-all-start.3 = ((bf16[4,32,32,128]{3,2,1,0:T(8,128)(2,1)}), bf16[4,32,32,128]{3,2,1,0:T(8,128)(2,1)}, u32[]{:S(2)}, u32[]{:S(2)}) async-start(bf16[4,32,32,128]{3,2,1,0:T(8,128)(2,1)} %broadcast_in_dim.25), calls=%async_computation.3 | async-start | bytes 2097152 | tf_op jit(solution)/shard_map/all_to_all | solution.py:45
  96.2 1.6 collective-permute-start.12
  97.9 10.2 %all-to-all-done.3.refs_11_ = bf16[4,32,32,128]{3,2,1,0:T(8,128)(2,1)} async-done(((bf16[4,32,32,128]{3,2,1,0:T(8,128)(2,1)}), bf16[4,32,32,128]{3,2,1,0:T(8,128)(2,1)}, u32[]{:S(2)}, u32[]{:S(2)}) %all-to-all-start.3) | async-done | bytes 1048608 | tf_op jit(solution)/shard_map/all_to_all | solution.py:45
  108.0 0.7 broadcast_in_dim.24
  108.8 5.5 %all-to-all-start.2 = ((bf16[8,32,512]{2,1,0:T(8,128)(2,1)}), bf16[8,32,512]{2,1,0:T(8,128)(2,1)S(1)}, u32[]{:S(2)}, u32[]{:S(2)}) async-start(bf16[8,32,512]{2,1,0:T(8,128)(2,1)} %broadcast_in_dim.24), calls=%async_computation.2 | async-start | bytes 524288 | tf_op jit(solution)/shard_map/all_to_all | solution.py:45
  114.3 1.5 collective-permute-start.11
  115.8 4.8 %collective-permute-start.15 = (bf16[32,64,128]{2,1,0:T(8,128)(2,1)S(1)}, bf16[32,64,128]{2,1,0:T(8,128)(2,1)}, u32[]{:S(2)}, u32[]{:S(2)}) collective-permute-start(bf16[32,64,128]{2,1,0:T(8,128)(2,1)S(1)} %slice.50.refs_1_), channel_id=1, source_target_pairs={{0,32},{32,0},{64,96},{96,64},{128,160},{160,128},{192,224},{224,1... | collective-permute-start | bytes 1572872 | tf_op jit(solution)/shard_map/ppermute | solution.py:63
  120.7 2.9 %all-to-all-done.2.refs_0_ = bf16[8,32,512]{2,1,0:T(8,128)(2,1)S(1)} async-done(((bf16[8,32,512]{2,1,0:T(8,128)(2,1)}), bf16[8,32,512]{2,1,0:T(8,128)(2,1)S(1)}, u32[]{:S(2)}, u32[]{:S(2)}) %all-to-all-start.2) | async-done | bytes 262176 | tf_op jit(solution)/shard_map/all_to_all | solution.py:45
  123.6 1.8 %collective-permute-start.10 = (bf16[8,32,512]{2,1,0:T(8,128)(2,1)S(1)}, bf16[8,32,512]{2,1,0:T(8,128)(2,1)S(1)}, u32[]{:S(2)}, u32[]{:S(2)}) collective-permute-start(bf16[8,32,512]{2,1,0:T(8,128)(2,1)S(1)} %all-to-all-done.2.refs_0_), channel_id=1, source_target_pairs={{0,1},{1,2},{2,3},{3,0},{4,5},{5,6},{6,7},{7,4},{8,9},{9,10},{10,1... | collective-permute-start | bytes 786440 | tf_op jit(solution)/shard_map/ppermute | solution.py:446
  125.4 2.5 %collective-permute-start.9 = (bf16[8,32,512]{2,1,0:T(8,128)(2,1)S(1)}, bf16[8,32,512]{2,1,0:T(8,128)(2,1)S(1)}, u32[]{:S(2)}, u32[]{:S(2)}) collective-permute-start(bf16[8,32,512]{2,1,0:T(8,128)(2,1)S(1)} %all-to-all-done.2.refs_0_), channel_id=1, source_target_pairs={{0,2},{1,3},{2,0},{3,1},{4,6},{5,7},{6,4},{7,5},{8,10},{9,11},{10,... | collective-permute-start | bytes 786440 | tf_op jit(solution)/shard_map/ppermute | solution.py:446
  128.5 1.0 slice.51
  129.5 1.0 slice.52
  130.9 3.6 %collective-permute-done.9.refs_2_ = bf16[8,32,512]{2,1,0:T(8,128)(2,1)S(1)} collective-permute-done((bf16[8,32,512]{2,1,0:T(8,128)(2,1)S(1)}, bf16[8,32,512]{2,1,0:T(8,128)(2,1)S(1)}, u32[]{:S(2)}, u32[]{:S(2)}) %collective-permute-start.9) | collective-permute-done | bytes 262176 | tf_op jit(solution)/shard_map/ppermute | solution.py:446
  134.5 2.9 %collective-permute-start.14 = (bf16[16,64,128]{2,1,0:T(8,128)(2,1)S(1)}, bf16[16,64,128]{2,1,0:T(8,128)(2,1)}, u32[]{:S(2)}, u32[]{:S(2)}) collective-permute-start(bf16[16,64,128]{2,1,0:T(8,128)(2,1)S(1)} %slice.52), channel_id=1, source_target_pairs={{0,192},{32,224},{64,0},{96,32},{128,64},{160,96},{192,128},{224,1... | collective-permute-start | bytes 786440 | tf_op jit(solution)/shard_map/ppermute | solution.py:54
  137.4 4.9 %collective-permute-start.17 = (bf16[32,64,128]{2,1,0:T(8,128)(2,1)}, bf16[32,64,128]{2,1,0:T(8,128)(2,1)}, u32[]{:S(2)}, u32[]{:S(2)}) collective-permute-start(bf16[32,64,128]{2,1,0:T(8,128)(2,1)} %collective-permute-done.12.refs_3_), channel_id=1, source_target_pairs={{0,32},{32,0},{64,96},{96,64},{128,160},{160,128},{192,224},{224,1... | collective-permute-start | bytes 1572872 | tf_op jit(solution)/shard_map/ppermute | solution.py:63
  142.3 1.3 dynamic_slice.38
  144.3 1.0 copy-done.2
  145.3 1.0 collective-permute-start.18
  146.3 2.0 %collective-permute-start.19 = (bf16[16,64,128]{2,1,0:T(8,128)(2,1)}, bf16[16,64,128]{2,1,0:T(8,128)(2,1)}, u32[]{:S(2)}, u32[]{:S(2)}) collective-permute-start(bf16[16,64,128]{2,1,0:T(8,128)(2,1)} %collective-permute-done.14.refs_5_), channel_id=1, source_target_pairs={{0,32},{32,0},{64,96},{96,64},{128,160},{160,128},{192,224},{224,1... | collective-permute-start | bytes 786440 | tf_op jit(solution)/shard_map/ppermute | solution.py:63
  148.4 1.3 rsqrt.42.scale
  149.8 22.0 %shard_map.149 = bf16[1024,512]{1,0:T(8,128)(2,1)} custom-call(s32[4]{0:T(128)} %pad_add_fusion.here, f32[1024,1]{1,0:T(8,128)} %rsqrt.42.scale, f32[1,512]{1,0:T(1,128)} %bitcast.74, bf16[8,4,32,512]{3,2,1,0:T(8,128)(2,1)} %copy-done.2, bf16[32,64,128]{2,1,0:T(8,128)(2,1)} %copy-done.7, bf16[32,64,128]{2,1,0:T(8,128)(2,1)} %collective-permute-done.11.refs_2_, ...), custom_call_target="tpu_custom_call" | custom-call | flops 9663676416 | bytes 2097152 | tf_op jit(solution)/shard_map/pallas_call | solution.py:279
  (91 shorter events, 8.7 us)
Async XLA Ops:
  0.0 16.7 %copy-start = (bf16[4096,128]{1,0:T(8,128)(2,1)S(1)}, bf16[4096,128]{1,0:T(8,128)(2,1)}, u32[]{:S(2)}) copy-start(bf16[4096,128]{1,0:T(8,128)(2,1)} %param.18) | copy-start | bytes 3145732
  0.0 18.6 %copy-start.5 = (bf16[32,4096]{1,0:T(8,128)(2,1)S(1)}, bf16[32,4096]{1,0:T(8,128)(2,1)}, u32[]{:S(2)}) copy-start(bf16[32,4096]{1,0:T(8,128)(2,1)} %param.15) | copy-start | bytes 786436
  0.0 18.6 %copy-start.9 = (f32[4096]{0:T(1024)S(1)}, f32[4096]{0:T(1024)}, u32[]{:S(2)}) copy-start(f32[4096]{0:T(1024)} %param.16) | copy-start | bytes 49156
  0.0 18.4 %copy-start.12 = (f32[128]{0:T(128)S(1)}, f32[128]{0:T(128)}, u32[]{:S(2)}) copy-start(f32[128]{0:T(128)} %param.22) | copy-start | bytes 1540
  0.9 20.8 %copy-start.10 = (bf16[32,512]{1,0:T(8,128)(2,1)}, bf16[32,512]{1,0:T(8,128)(2,1)S(1)}, u32[]{:S(2)}) copy-start(bf16[32,512]{1,0:T(8,128)(2,1)S(1)} %constant_dynamic-slice_fusion.2.old_mine) | copy-start | bytes 98308
  2.0 19.9 %copy-start.13 = (f32[128]{0:T(128)S(1)}, f32[128]{0:T(128)}, u32[]{:S(2)}) copy-start(f32[128]{0:T(128)} %param.21) | copy-start | bytes 1540
  2.0 20.4 %copy-start.8 = (bf16[32,32,128]{2,1,0:T(8,128)(2,1)S(1)}, bf16[32,32,128]{2,1,0:T(8,128)(2,1)}, u32[]{:S(2)}) copy-start(bf16[32,32,128]{2,1,0:T(8,128)(2,1)} %param.23) | copy-start | bytes 786436
  2.0 38.3 %all-to-all-start = ((bf16[32,32,512]{2,1,0:T(8,128)(2,1)}), bf16[32,32,512]{2,1,0:T(8,128)(2,1)}, u32[]{:S(2)}, u32[]{:S(2)}) async-start(bf16[32,32,512]{2,1,0:T(8,128)(2,1)} %broadcast_in_dim.16), calls=%async_computation | async-start | bytes 2097152 | tf_op jit(solution)/shard_map/all_to_all | solution.py:45
  14.1 8.9 %copy-start.6 = (bf16[4096,128]{1,0:T(8,128)(2,1)S(1)}, bf16[4096,128]{1,0:T(8,128)(2,1)}, u32[]{:S(2)}) copy-start(bf16[4096,128]{1,0:T(8,128)(2,1)} %param.19) | copy-start | bytes 3145732
  16.7 6.6 %copy-start.14 = (bf16[32,32,128]{2,1,0:T(8,128)(2,1)S(1)}, bf16[32,32,128]{2,1,0:T(8,128)(2,1)}, u32[]{:S(2)}) copy-start(bf16[32,32,128]{2,1,0:T(8,128)(2,1)} %param.24) | copy-start | bytes 786436
  26.6 20.5 %copy-start.11 = (s32[512,1]{0,1:T(1,128)S(1)}, s32[512,1]{0,1:T(1,128)}, u32[]{:S(2)}) copy-start(s32[512,1]{0,1:T(1,128)} %param.29) | copy-start | bytes 6148
  27.5 2.0 %collective-permute-start = (bf16[32,4,512]{2,0,1:T(8,128)(2,1)S(1)}, bf16[32,4,512]{2,0,1:T(8,128)(2,1)S(1)}, u32[]{:S(2)}, u32[]{:S(2)}) collective-permute-start(bf16[32,4,512]{2,0,1:T(8,128)(2,1)S(1)} %bitcast.67), channel_id=1, source_target_pairs={{0,32},{32,0},{64,96},{96,64},{128,160},{160,128},{192,224},{224,1... | collective-permute-start | bytes 393224 | tf_op jit(solution)/shard_map/ppermute | solution.py:63
  29.6 5.1 %collective-permute-start.1 = (bf16[32,512]{1,0:T(8,128)(2,1)S(1)}, bf16[32,512]{1,0:T(8,128)(2,1)S(1)}, u32[]{:S(2)}, u32[]{:S(2)}) collective-permute-start(bf16[32,512]{1,0:T(8,128)(2,1)S(1)} %get-tuple-element.23), channel_id=1, source_target_pairs={{0,64},{32,96},{64,128},{96,160},{128,192},{160,224},{192,0},{224,... | collective-permute-start | bytes 98312 | tf_op jit(solution)/shard_map/ppermute | solution.py:416
  31.0 3.7 %collective-permute-start.3 = (bf16[32,512]{1,0:T(8,128)(2,1)S(1)}, bf16[32,512]{1,0:T(8,128)(2,1)S(1)}, u32[]{:S(2)}, u32[]{:S(2)}) collective-permute-start(bf16[32,512]{1,0:T(8,128)(2,1)S(1)} %get-tuple-element.24), channel_id=1, source_target_pairs={{0,192},{32,224},{64,0},{96,32},{128,64},{160,96},{192,128},{224,1... | collective-permute-start | bytes 98312 | tf_op jit(solution)/shard_map/ppermute | solution.py:416
  32.5 4.5 %collective-permute-start.2 = (bf16[32,512]{1,0:T(8,128)(2,1)S(1)}, bf16[32,512]{1,0:T(8,128)(2,1)S(1)}, u32[]{:S(2)}, u32[]{:S(2)}) collective-permute-start(bf16[32,512]{1,0:T(8,128)(2,1)S(1)} %get-tuple-element.25), channel_id=1, source_target_pairs={{0,128},{32,160},{64,192},{96,224},{128,0},{160,32},{192,64},{224,... | collective-permute-start | bytes 98312 | tf_op jit(solution)/shard_map/ppermute | solution.py:416
  34.6 14.4 %copy-start.3 = (s32[4]{0:T(128)S(1)}, s32[4]{0:T(128)}, u32[]{:S(2)}) copy-start(s32[4]{0:T(128)} %pad_add_fusion.here) | copy-start | bytes 52
  37.7 11.3 %copy-start.4 = (f32[1,128]{1,0:T(1,128)S(1)}, f32[1,128]{1,0:T(1,128)}, u32[]{:S(2)}) copy-start(f32[1,128]{1,0:T(1,128)} %pad.4.squares) | copy-start | bytes 1540
  44.4 4.7 %collective-permute-start.4 = (bf16[4,592,128]{2,1,0:T(8,128)(2,1)}, bf16[4,592,128]{2,1,0:T(8,128)(2,1)S(1)}, u32[]{:S(2)}, u32[]{:S(2)}) collective-permute-start(bf16[4,592,128]{2,1,0:T(8,128)(2,1)} %get-tuple-element.13), channel_id=1, source_target_pairs={{0,32},{32,0},{64,96},{96,64},{128,160},{160,128},{192,224},{224,1... | collective-permute-start | bytes 1818632 | tf_op jit(solution)/shard_map/ppermute | solution.py:63
  49.1 1.2 copy-start.1
  51.0 6.5 %collective-permute-start.5 = (bf16[592,128]{1,0:T(8,128)(2,1)S(1)}, bf16[592,128]{1,0:T(8,128)(2,1)S(1)}, u32[]{:S(2)}, u32[]{:S(2)}) collective-permute-start(bf16[592,128]{1,0:T(8,128)(2,1)S(1)} %get-tuple-element.16), channel_id=1, source_target_pairs={{0,64},{32,96},{64,128},{96,160},{128,192},{160,224},{192,0},{224,... | collective-permute-start | bytes 454664 | tf_op jit(solution)/shard_map/ppermute | solution.py:416
  52.4 9.5 %collective-permute-start.6 = (bf16[592,128]{1,0:T(8,128)(2,1)S(1)}, bf16[592,128]{1,0:T(8,128)(2,1)S(1)}, u32[]{:S(2)}, u32[]{:S(2)}) collective-permute-start(bf16[592,128]{1,0:T(8,128)(2,1)S(1)} %get-tuple-element.17), channel_id=1, source_target_pairs={{0,128},{32,160},{64,192},{96,224},{128,0},{160,32},{192,64},{224,... | collective-permute-start | bytes 454664 | tf_op jit(solution)/shard_map/ppermute | solution.py:416
  55.0 6.9 %collective-permute-start.7 = (bf16[592,128]{1,0:T(8,128)(2,1)S(1)}, bf16[592,128]{1,0:T(8,128)(2,1)S(1)}, u32[]{:S(2)}, u32[]{:S(2)}) collective-permute-start(bf16[592,128]{1,0:T(8,128)(2,1)S(1)} %get-tuple-element.18), channel_id=1, source_target_pairs={{0,192},{32,224},{64,0},{96,32},{128,64},{160,96},{192,128},{224,1... | collective-permute-start | bytes 454664 | tf_op jit(solution)/shard_map/ppermute | solution.py:416
  91.9 16.1 %all-to-all-start.3 = ((bf16[4,32,32,128]{3,2,1,0:T(8,128)(2,1)}), bf16[4,32,32,128]{3,2,1,0:T(8,128)(2,1)}, u32[]{:S(2)}, u32[]{:S(2)}) async-start(bf16[4,32,32,128]{3,2,1,0:T(8,128)(2,1)} %broadcast_in_dim.25), calls=%async_computation.3 | async-start | bytes 2097152 | tf_op jit(solution)/shard_map/all_to_all | solution.py:45
  96.2 53.6 %copy-start.7 = (bf16[32,64,128]{2,1,0:T(8,128)(2,1)}, bf16[32,64,128]{2,1,0:T(8,128)(2,1)S(1)}, u32[]{:S(2)}) copy-start(bf16[32,64,128]{2,1,0:T(8,128)(2,1)S(1)} %slice.50.refs_1_) | copy-start | bytes 1572868
  96.2 29.2 %collective-permute-start.12 = (bf16[32,64,128]{2,1,0:T(8,128)(2,1)S(1)}, bf16[32,64,128]{2,1,0:T(8,128)(2,1)}, u32[]{:S(2)}, u32[]{:S(2)}) collective-permute-start(bf16[32,64,128]{2,1,0:T(8,128)(2,1)S(1)} %slice.50.refs_1_), channel_id=1, source_target_pairs={{0,64},{32,96},{64,128},{96,160},{128,192},{160,224},{192,0},{224,... | collective-permute-start | bytes 1572872 | tf_op jit(solution)/shard_map/ppermute | solution.py:54
  108.8 14.9 %all-to-all-start.2 = ((bf16[8,32,512]{2,1,0:T(8,128)(2,1)}), bf16[8,32,512]{2,1,0:T(8,128)(2,1)S(1)}, u32[]{:S(2)}, u32[]{:S(2)}) async-start(bf16[8,32,512]{2,1,0:T(8,128)(2,1)} %broadcast_in_dim.24), calls=%async_computation.2 | async-start | bytes 524288 | tf_op jit(solution)/shard_map/all_to_all | solution.py:45
  114.3 13.6 %collective-permute-start.11 = (bf16[32,64,128]{2,1,0:T(8,128)(2,1)S(1)}, bf16[32,64,128]{2,1,0:T(8,128)(2,1)}, u32[]{:S(2)}, u32[]{:S(2)}) collective-permute-start(bf16[32,64,128]{2,1,0:T(8,128)(2,1)S(1)} %slice.50.refs_1_), channel_id=1, source_target_pairs={{0,192},{32,224},{64,0},{96,32},{128,64},{160,96},{192,128},{224,1... | collective-permute-start | bytes 1572872 | tf_op jit(solution)/shard_map/ppermute | solution.py:54
  115.8 26.5 %collective-permute-start.15 = (bf16[32,64,128]{2,1,0:T(8,128)(2,1)S(1)}, bf16[32,64,128]{2,1,0:T(8,128)(2,1)}, u32[]{:S(2)}, u32[]{:S(2)}) collective-permute-start(bf16[32,64,128]{2,1,0:T(8,128)(2,1)S(1)} %slice.50.refs_1_), channel_id=1, source_target_pairs={{0,32},{32,0},{64,96},{96,64},{128,160},{160,128},{192,224},{224,1... | collective-permute-start | bytes 1572872 | tf_op jit(solution)/shard_map/ppermute | solution.py:63
  120.6 29.2 %collective-permute-start.20 = (bf16[4,32,32,128]{3,2,1,0:T(8,128)(2,1)}, bf16[4,32,32,128]{3,2,1,0:T(8,128)(2,1)}, u32[]{:S(2)}, u32[]{:S(2)}) collective-permute-start(bf16[4,32,32,128]{3,2,1,0:T(8,128)(2,1)} %all-to-all-done.3.refs_11_), channel_id=1, source_target_pairs={{0,32},{32,0},{64,96},{96,64},{128,160},{160,128},{192,224},{224,1... | collective-permute-start | bytes 3145736 | tf_op jit(solution)/shard_map/ppermute | solution.py:63
  123.6 7.0 %collective-permute-start.10 = (bf16[8,32,512]{2,1,0:T(8,128)(2,1)S(1)}, bf16[8,32,512]{2,1,0:T(8,128)(2,1)S(1)}, u32[]{:S(2)}, u32[]{:S(2)}) collective-permute-start(bf16[8,32,512]{2,1,0:T(8,128)(2,1)S(1)} %all-to-all-done.2.refs_0_), channel_id=1, source_target_pairs={{0,1},{1,2},{2,3},{3,0},{4,5},{5,6},{6,7},{7,4},{8,9},{9,10},{10,1... | collective-permute-start | bytes 786440 | tf_op jit(solution)/shard_map/ppermute | solution.py:446
  125.4 9.1 %collective-permute-start.9 = (bf16[8,32,512]{2,1,0:T(8,128)(2,1)S(1)}, bf16[8,32,512]{2,1,0:T(8,128)(2,1)S(1)}, u32[]{:S(2)}, u32[]{:S(2)}) collective-permute-start(bf16[8,32,512]{2,1,0:T(8,128)(2,1)S(1)} %all-to-all-done.2.refs_0_), channel_id=1, source_target_pairs={{0,2},{1,3},{2,0},{3,1},{4,6},{5,7},{6,4},{7,5},{8,10},{9,11},{10,... | collective-permute-start | bytes 786440 | tf_op jit(solution)/shard_map/ppermute | solution.py:446
  127.9 9.5 %collective-permute-start.8 = (bf16[8,32,512]{2,1,0:T(8,128)(2,1)S(1)}, bf16[8,32,512]{2,1,0:T(8,128)(2,1)S(1)}, u32[]{:S(2)}, u32[]{:S(2)}) collective-permute-start(bf16[8,32,512]{2,1,0:T(8,128)(2,1)S(1)} %all-to-all-done.2.refs_0_), channel_id=1, source_target_pairs={{0,3},{1,0},{2,1},{3,2},{4,7},{5,4},{6,5},{7,6},{8,11},{9,8},{10,9... | collective-permute-start | bytes 786440 | tf_op jit(solution)/shard_map/ppermute | solution.py:446
  130.6 14.7 %collective-permute-start.13 = (bf16[16,64,128]{2,1,0:T(8,128)(2,1)S(1)}, bf16[16,64,128]{2,1,0:T(8,128)(2,1)}, u32[]{:S(2)}, u32[]{:S(2)}) collective-permute-start(bf16[16,64,128]{2,1,0:T(8,128)(2,1)S(1)} %slice.51), channel_id=1, source_target_pairs={{0,64},{32,96},{64,128},{96,160},{128,192},{160,224},{192,0},{224,... | collective-permute-start | bytes 786440 | tf_op jit(solution)/shard_map/ppermute | solution.py:54
  134.5 11.8 %collective-permute-start.14 = (bf16[16,64,128]{2,1,0:T(8,128)(2,1)S(1)}, bf16[16,64,128]{2,1,0:T(8,128)(2,1)}, u32[]{:S(2)}, u32[]{:S(2)}) collective-permute-start(bf16[16,64,128]{2,1,0:T(8,128)(2,1)S(1)} %slice.52), channel_id=1, source_target_pairs={{0,192},{32,224},{64,0},{96,32},{128,64},{160,96},{192,128},{224,1... | collective-permute-start | bytes 786440 | tf_op jit(solution)/shard_map/ppermute | solution.py:54
  137.4 12.3 %collective-permute-start.17 = (bf16[32,64,128]{2,1,0:T(8,128)(2,1)}, bf16[32,64,128]{2,1,0:T(8,128)(2,1)}, u32[]{:S(2)}, u32[]{:S(2)}) collective-permute-start(bf16[32,64,128]{2,1,0:T(8,128)(2,1)} %collective-permute-done.12.refs_3_), channel_id=1, source_target_pairs={{0,32},{32,0},{64,96},{96,64},{128,160},{160,128},{192,224},{224,1... | collective-permute-start | bytes 1572872 | tf_op jit(solution)/shard_map/ppermute | solution.py:63
  142.2 7.4 %collective-permute-start.16 = (bf16[32,64,128]{2,1,0:T(8,128)(2,1)}, bf16[32,64,128]{2,1,0:T(8,128)(2,1)}, u32[]{:S(2)}, u32[]{:S(2)}) collective-permute-start(bf16[32,64,128]{2,1,0:T(8,128)(2,1)} %collective-permute-done.11.refs_2_), channel_id=1, source_target_pairs={{0,32},{32,0},{64,96},{96,64},{128,160},{160,128},{192,224},{224,1... | collective-permute-start | bytes 1572872 | tf_op jit(solution)/shard_map/ppermute | solution.py:63
  144.3 1.0 copy-start.2
  145.3 4.4 %collective-permute-start.18 = (bf16[16,64,128]{2,1,0:T(8,128)(2,1)}, bf16[16,64,128]{2,1,0:T(8,128)(2,1)}, u32[]{:S(2)}, u32[]{:S(2)}) collective-permute-start(bf16[16,64,128]{2,1,0:T(8,128)(2,1)} %collective-permute-done.13.refs_4_), channel_id=1, source_target_pairs={{0,32},{32,0},{64,96},{96,64},{128,160},{160,128},{192,224},{224,1... | collective-permute-start | bytes 786440 | tf_op jit(solution)/shard_map/ppermute | solution.py:63
  146.3 3.5 %collective-permute-start.19 = (bf16[16,64,128]{2,1,0:T(8,128)(2,1)}, bf16[16,64,128]{2,1,0:T(8,128)(2,1)}, u32[]{:S(2)}, u32[]{:S(2)}) collective-permute-start(bf16[16,64,128]{2,1,0:T(8,128)(2,1)} %collective-permute-done.14.refs_5_), channel_id=1, source_target_pairs={{0,32},{32,0},{64,96},{96,64},{128,160},{160,128},{192,224},{224,1... | collective-permute-start | bytes 786440 | tf_op jit(solution)/shard_map/ppermute | solution.py:63

commit v6 on v5

--- a/solution.py
+++ b/solution.py
@@ -34,7 +34,8 @@
     return values * scale * gain
 
 
-TILE = 256
+TILE = 1024
+STRIP = 32
 SMEM = pl.BlockSpec(memory_space=pltpu.SMEM)
 VMEM = pl.BlockSpec(memory_space=pltpu.VMEM)
 ANY = pl.BlockSpec(memory_space=pl.ANY)
@@ -67,6 +68,10 @@
     return lax.fori_loop(0, 1024 // TILE, body, init)
 
 
+def strips(body, init=0):
+    return lax.fori_loop(0, 1024 // STRIP, body, init, unroll=4)
+
+
 def columns(place):
     return pl.ds(pl.multiple_of(place * 128, 128), 128)
 
@@ -104,16 +109,17 @@
 
 def parts_kernel(here, slab, old_mine, old_all, squares, theirs, kept):
     norms = norm_block(squares[...])
+    first = here[0] == 0
     for y in range(4):
-        for side in range(2):
-            at = 2 * y + (here[0] if side else 1 - here[0])
-            block = old_all[pl.ds(pl.multiple_of(at * 128, 128), 128), :]
-            slab_part, gram_part = flat_dot(slab[...], block), flat_dot(old_mine[...], block)
-            if side:
-                kept[y, :512] = slab_part
-                kept[y, 512:] = gram_part
-            else:
-                fill(theirs.at[y], slab_part, gram_part, norms)
+        block = old_all[256 * y : 256 * (y + 1), :]
+        slab_part, gram_part = flat_dot(slab[...], block), flat_dot(old_mine[...], block)
+        left, right = slab_part[:, :128], slab_part[:, 128:]
+        low, high = gram_part[:, :128], gram_part[:, 128:]
+        kept[y, :512] = jnp.where(first, left, right)
+        kept[y, 512:] = jnp.where(first, low, high)
+        fill(
+            theirs.at[y], jnp.where(first, right, left), jnp.where(first, high, low), norms
+        )
 
 
 def wide_sum(block):
@@ -191,8 +197,8 @@
     for copy in state_copies:
         copy.wait()
 
-    def rows_of(i):
-        return pl.ds(pl.multiple_of(i * TILE, TILE), TILE)
+    def rows_of(i, size=STRIP):
+        return pl.ds(pl.multiple_of(i * size, size), size)
 
     def split(rows, value):
         rho[rows, :] = value
@@ -202,66 +208,75 @@
 
     def start(i, carry):
         rows = rows_of(i)
-        value = state[pl.ds(2 * i, 2)].reshape(TILE, -1).astype(jnp.float32)
-        value = value * scale[rows, :] * gain[...]
-        split(rows, value)
-        way[rows, :] = value
+        value = state[i // 4, i % 4].astype(jnp.float32)
+        value = (value * scale[rows, :] * gain[...]).astype(jnp.bfloat16)
+        rho_high[rows, :] = value
+        rho[rows, :] = value.astype(jnp.float32)
         return carry
 
-    tiles(start)
+    strips(start)
     for copy in gram_copies:
         copy.wait()
 
     def gram_rows(block, i):
-        return block[pl.ds(8 * i, 8)].reshape(TILE, -1)
+        return block[pl.ds(TILE // 32 * i, TILE // 32)].reshape(TILE, -1)
 
     def dot(left, right):
         return jnp.dot(left, right, preferred_element_type=jnp.float32)
 
-    def product(i, square):
-        rows = rows_of(i)
+    def product(i, sums, exact=False):
+        rows = rows_of(i, TILE)
         top = gram_rows(high, i)
-        value = dot(top, rho_low[...]) + dot(gram_rows(low, i), rho_high[...])
+        value = dot(gram_rows(low, i), rho_high[...])
+        if not exact:
+            value = value + dot(top, rho_low[...])
         value = value + dot(top, rho_high[...])
         image[rows, :] = value
-        return square + jnp.sum(rho[rows, :] * value, axis=0, keepdims=True)
+        here_rho = rho[rows, :]
+        square, bend = sums
+        return (
+            square + jnp.sum(here_rho * value, axis=0, keepdims=True),
+            bend + jnp.sum(value * (value + ridge * here_rho), axis=0, keepdims=True),
+        )
 
     zero = jnp.zeros((1, rho.shape[1]), jnp.float32)
-    res_sq = tiles(product, zero)
-    ratio = zero
+    res_sq, curvature = tiles(lambda i, sums: product(i, sums, True), (zero, zero))
     for sweep in range(ITERS):
-
-        def turn(i, curvature):
-            rows = rows_of(i)
-            if sweep == 0:
-                step, step_image = way[rows, :], image[rows, :]
-            else:
+        if sweep:
+
+            def turn(i, bend):
+                rows = rows_of(i)
                 step = rho[rows, :] + ratio * way[rows, :]
                 step_image = image[rows, :] + ratio * way_image[rows, :]
                 way[rows, :] = step
-            way_image[rows, :] = step_image
-            return curvature + jnp.sum(
-                step_image * (step_image + ridge * step), axis=0, keepdims=True
-            )
-
-        alpha = res_sq / tiles(turn, zero)
+                way_image[rows, :] = step_image
+                return bend + jnp.sum(
+                    step_image * (step_image + ridge * step), axis=0, keepdims=True
+                )
+
+            curvature = strips(turn, zero)
+        alpha = res_sq / curvature
 
         def update(i, carry):
             rows = rows_of(i)
-            step = way[rows, :]
-            moved = alpha * step
             if sweep:
-                moved = total[rows, :] + moved
+                step, step_image = way[rows, :], way_image[rows, :]
+                moved = total[rows, :] + alpha * step
+            else:
+                step, step_image = rho[rows, :], image[rows, :]
+                way[rows, :] = step
+                way_image[rows, :] = step_image
+                moved = alpha * step
             if sweep + 1 < ITERS:
                 total[rows, :] = moved
-                split(rows, rho[rows, :] - alpha * (way_image[rows, :] + ridge * step))
+                split(rows, rho[rows, :] - alpha * (step_image + ridge * step))
             else:
                 dual_map[rows, :] = moved.astype(jnp.bfloat16)
             return carry
 
-        tiles(update)
+        strips(update)
         if sweep + 1 < ITERS:
-            new_sq = tiles(product, zero)
+            new_sq, _ = tiles(product, (zero, zero))
             ratio = new_sq / res_sq
             res_sq = new_sq
 
@@ -269,7 +284,7 @@
         copy.wait()
 
     def last(i, carry):
-        result[rows_of(i), :] = dot(gram_rows(routed, i), dual_map[...]).astype(jnp.bfloat16)
+        result[rows_of(i, TILE), :] = dot(gram_rows(routed, i), dual_map[...]).astype(jnp.bfloat16)
         return carry
 
     tiles(last)
@@ -432,6 +447,7 @@
     column = rows_count // line
     by_z = [[x + line * z for z in range(column)] for x in range(line)]
     by_y = [list(range(at, mp_count, 2)) for at in range(2)]
+    gain = my_cols(final_gain, 0).reshape(1, cols)
     old_mine = my_cols(old_embed, 1)
     old_all = spread(old_mine, "rows", rows_count)
     anchors = rows_count * docs
@@ -476,7 +492,7 @@
     slabs = spread(routed, "mp", chips, by_y)
     slabs = [slabs, swap_cores(slabs, mp_count)]
     return solve(
-        here, scale_rows, my_cols(final_gain, 0).reshape(1, cols), state_all, *grams, *slabs
+        here, scale_rows, gain, state_all, *grams, *slabs
     )
 
 

time: 173 us -> 169 us (0.977)
  Pallas kernels: 27.9 us -> 24 us
    pallas_call x5, Pallas kernels: 27.9 us -> 24 us  [call(): pl.pallas_call(kernel, out_shape=shapes, in_specs=in_specs, out_specs=jax...]
where the time goes in v6:
time: 169 us; the launch traced here: 168 us
  starting transfers between devices  59.3 us (35%)
  waiting for transfers between devices  28.7 us (17%)
  blocking collectives  28.4 us (17%)
  Pallas kernels  24 us (14%)
  local copies, waits for them, and re-layouts  12.6 us (7%)
  matrix products  8.72 us (5%)
  other arithmetic  5.81 us (3%)
    all_to_all x1, blocking collectives, local(): arrived = lax.all_to_all(outgoing, 'rows', 0, 0, tiled=True)  28.4 us
    pallas_call x5, Pallas kernels, call(): pl.pallas_call(kernel, out_shape=shapes, in_specs=in_specs, out_specs=jax...  24 us
    all_to_all x3, starting transfers between devices, spread(): lax.all_to_all(copies, axis, 0, 0, tiled=True, axis_index_groups=groups)  21.9 us
    ppermute x8, starting transfers between devices, swap_cores(): return lax.ppermute(block, 'mp', [(i, i ^ 1) for i in range(size)])  16.8 us
    all_to_all x3, waiting for transfers between devices, spread(): lax.all_to_all(copies, axis, 0, 0, tiled=True, axis_index_groups=groups)  15.7 us
    ppermute x6, starting transfers between devices, shift_chips(): lax.ppermute(block, 'mp', [(i, (i + 2 * step) % mp_count) for i in range(...  9.51 us
    ppermute x6, waiting for transfers between devices, shift_chips(): lax.ppermute(block, 'mp', [(i, (i + 2 * step) % mp_count) for i in range(...  8.14 us
    ppermute x4, starting transfers between devices, move(): return lax.ppermute(array, axis, pairs)  6.28 us
  transfers between devices with their start and end apart: 24, of which 11 were waited for; matrix products, arithmetic and copies ran while one was open for 13% of the time, Pallas kernels for 0%

profile of v6, /device:TPU:1, one launch (start us, length us, event | category | flops | bytes accessed | tf_op | source)
XLA Modules:
  0.0 168.1 jit_solution(14945135292228256863)
XLA Ops:
  0.0 0.9 constant_dynamic-slice_fusion.2.old_mine
  0.9 1.1 broadcast_in_dim.16
  2.0 12.1 %all-to-all-start = ((bf16[32,32,512]{2,1,0:T(8,128)(2,1)}), bf16[32,32,512]{2,1,0:T(8,128)(2,1)}, u32[]{:S(2)}, u32[]{:S(2)}) async-start(bf16[32,32,512]{2,1,0:T(8,128)(2,1)} %broadcast_in_dim.16), calls=%async_computation | async-start | bytes 2097152 | tf_op jit(solution)/shard_map/all_to_all | solution.py:46
  14.1 0.7 convert_element_type.80
  14.9 0.7 iota_compare_fusion.2
  15.6 1.1 multiply_reduce_fusion
  16.8 1.5 multiply_reduce_fusion.3
  18.6 3.1 %fusion.31 = f32[32,512]{1,0:T(8,128)S(1)} fusion(bf16[4096,512]{1,0:T(8,128)(2,1)} %param.17, f32[4096]{0:T(1024)S(1)} %copy-done.9, f32[32]{0:T(128)S(1)} %add_rsqrt_fusion.3, bf16[32,4096]{1,0:T(8,128)(2,1)S(1)} %copy-done.5), kind=kOutput, calls=%fused_computation.77 | convolution fusion | flops 134742016 | bytes 4538496 | tf_op jit(solution)/shard_map/dot_general | solution.py:381
  23.6 3.0 %fusion.11 = f32[32,4096]{1,0:T(8,128)S(1)} fusion(bf16[512,4096]{1,0:T(8,128)(2,1)} %param.20, bf16[4,8,4,128]{3,2,1,0:T(4,128)(2,1)S(1)} %bitcast.70), kind=kOutput, calls=%fused_computation.31 | convolution fusion | flops 134217728 | bytes 4751360 | tf_op jit(solution)/shard_map/dot_general | solution.py:421
  27.5 1.0 collective-permute-start
  28.8 0.7 collective-permute-done
  29.6 1.4 collective-permute-start.1
  31.0 1.5 collective-permute-start.3
  32.5 1.6 collective-permute-start.2
  34.7 2.3 %collective-permute-done.2 = bf16[32,512]{1,0:T(8,128)(2,1)S(1)} collective-permute-done((bf16[32,512]{1,0:T(8,128)(2,1)S(1)}, bf16[32,512]{1,0:T(8,128)(2,1)S(1)}, u32[]{:S(2)}, u32[]{:S(2)}) %collective-permute-start.2) | collective-permute-done | bytes 32800 | tf_op jit(solution)/shard_map/ppermute | solution.py:431
  37.7 2.6 %all-to-all-done = bf16[32,32,512]{2,1,0:T(8,128)(2,1)} async-done(((bf16[32,32,512]{2,1,0:T(8,128)(2,1)}), bf16[32,32,512]{2,1,0:T(8,128)(2,1)}, u32[]{:S(2)}, u32[]{:S(2)}) %all-to-all-start) | async-done | bytes 1048608 | tf_op jit(solution)/shard_map/all_to_all | solution.py:46
  40.3 3.6 %shard_map.145 = (bf16[4,592,128]{2,1,0:T(8,128)(2,1)}, f32[4,544,128]{2,1,0:T(8,128)}) custom-call(s32[4]{0:T(128)} %pad_add_fusion.here, bf16[512,512]{1,0:T(8,128)(2,1)} %slab.1, bf16[32,512]{1,0:T(8,128)(2,1)} %copy-done.10, bf16[1024,512]{1,0:T(8,128)(2,1)} %bitcast.8.old_all, f32[1,128]{1,0:T(1,128)} %pad.4.squares), custom_call_target="tpu_custom_call" | custom-call | flops 1073741824 | bytes 2097152 | tf_op jit(solution)/shard_map/pallas_call | solution.py:294
  43.9 2.8 %collective-permute-start.4 = (bf16[4,592,128]{2,1,0:T(8,128)(2,1)}, bf16[4,592,128]{2,1,0:T(8,128)(2,1)S(1)}, u32[]{:S(2)}, u32[]{:S(2)}) collective-permute-start(bf16[4,592,128]{2,1,0:T(8,128)(2,1)} %get-tuple-element.13), channel_id=1, source_target_pairs={{0,32},{32,0},{64,96},{96,64},{128,160},{160,128},{192,224},{224,1... | collective-permute-start | bytes 1818632 | tf_op jit(solution)/shard_map/ppermute | solution.py:64
  46.7 1.2 reduce-window.6
  48.6 1.2 copy-done.1
  50.5 1.4 collective-permute-start.5
  51.9 2.6 %collective-permute-start.6 = (bf16[592,128]{1,0:T(8,128)(2,1)S(1)}, bf16[592,128]{1,0:T(8,128)(2,1)S(1)}, u32[]{:S(2)}, u32[]{:S(2)}) collective-permute-start(bf16[592,128]{1,0:T(8,128)(2,1)S(1)} %get-tuple-element.17), channel_id=1, source_target_pairs={{0,128},{32,160},{64,192},{96,224},{128,0},{160,32},{192,64},{224,... | collective-permute-start | bytes 454664 | tf_op jit(solution)/shard_map/ppermute | solution.py:431
  54.5 1.1 collective-permute-start.7
  55.6 1.5 collective-permute-done.5.refs_0_
  57.0 4.4 %collective-permute-done.6.refs_1_ = bf16[592,128]{1,0:T(8,128)(2,1)S(1)} collective-permute-done((bf16[592,128]{1,0:T(8,128)(2,1)S(1)}, bf16[592,128]{1,0:T(8,128)(2,1)S(1)}, u32[]{:S(2)}, u32[]{:S(2)}) %collective-permute-start.6) | collective-permute-done | bytes 151584 | tf_op jit(solution)/shard_map/ppermute | solution.py:431
  61.9 28.4 %all_to_all.20 = bf16[32,112,128]{2,1,0:T(8,128)(2,1)S(1)} all-to-all(bf16[32,112,128]{2,1,0:T(8,128)(2,1)S(1)} %shard_map.147), channel_id=1, replica_groups=mesh['mp'=8,'rows'=32] {'rows'}, dimensions={0} | all-to-all | bytes 1835008 | tf_op jit(solution)/shard_map/all_to_all | solution.py:483
  90.3 1.1 broadcast_in_dim.25
  91.4 4.2 %all-to-all-start.3 = ((bf16[4,32,32,128]{3,2,1,0:T(8,128)(2,1)}), bf16[4,32,32,128]{3,2,1,0:T(8,128)(2,1)}, u32[]{:S(2)}, u32[]{:S(2)}) async-start(bf16[4,32,32,128]{3,2,1,0:T(8,128)(2,1)} %broadcast_in_dim.25), calls=%async_computation.3 | async-start | bytes 2097152 | tf_op jit(solution)/shard_map/all_to_all | solution.py:46
  95.8 1.6 collective-permute-start.12
  97.4 10.2 %all-to-all-done.3.refs_11_ = bf16[4,32,32,128]{3,2,1,0:T(8,128)(2,1)} async-done(((bf16[4,32,32,128]{3,2,1,0:T(8,128)(2,1)}), bf16[4,32,32,128]{3,2,1,0:T(8,128)(2,1)}, u32[]{:S(2)}, u32[]{:S(2)}) %all-to-all-start.3) | async-done | bytes 1048608 | tf_op jit(solution)/shard_map/all_to_all | solution.py:46
  107.6 0.7 broadcast_in_dim.24
  108.3 5.6 %all-to-all-start.2 = ((bf16[8,32,512]{2,1,0:T(8,128)(2,1)}), bf16[8,32,512]{2,1,0:T(8,128)(2,1)S(1)}, u32[]{:S(2)}, u32[]{:S(2)}) async-start(bf16[8,32,512]{2,1,0:T(8,128)(2,1)} %broadcast_in_dim.24), calls=%async_computation.2 | async-start | bytes 524288 | tf_op jit(solution)/shard_map/all_to_all | solution.py:46
  113.9 1.4 collective-permute-start.11
  115.3 4.8 %collective-permute-start.15 = (bf16[32,64,128]{2,1,0:T(8,128)(2,1)S(1)}, bf16[32,64,128]{2,1,0:T(8,128)(2,1)}, u32[]{:S(2)}, u32[]{:S(2)}) collective-permute-start(bf16[32,64,128]{2,1,0:T(8,128)(2,1)S(1)} %slice.50.refs_1_), channel_id=1, source_target_pairs={{0,32},{32,0},{64,96},{96,64},{128,160},{160,128},{192,224},{224,1... | collective-permute-start | bytes 1572872 | tf_op jit(solution)/shard_map/ppermute | solution.py:64
  120.2 3.0 %all-to-all-done.2.refs_0_ = bf16[8,32,512]{2,1,0:T(8,128)(2,1)S(1)} async-done(((bf16[8,32,512]{2,1,0:T(8,128)(2,1)}), bf16[8,32,512]{2,1,0:T(8,128)(2,1)S(1)}, u32[]{:S(2)}, u32[]{:S(2)}) %all-to-all-start.2) | async-done | bytes 262176 | tf_op jit(solution)/shard_map/all_to_all | solution.py:46
  123.2 1.7 %collective-permute-start.10 = (bf16[8,32,512]{2,1,0:T(8,128)(2,1)S(1)}, bf16[8,32,512]{2,1,0:T(8,128)(2,1)S(1)}, u32[]{:S(2)}, u32[]{:S(2)}) collective-permute-start(bf16[8,32,512]{2,1,0:T(8,128)(2,1)S(1)} %all-to-all-done.2.refs_0_), channel_id=1, source_target_pairs={{0,1},{1,2},{2,3},{3,0},{4,5},{5,6},{6,7},{7,4},{8,9},{9,10},{10,1... | collective-permute-start | bytes 786440 | tf_op jit(solution)/shard_map/ppermute | solution.py:462
  124.9 2.5 %collective-permute-start.9 = (bf16[8,32,512]{2,1,0:T(8,128)(2,1)S(1)}, bf16[8,32,512]{2,1,0:T(8,128)(2,1)S(1)}, u32[]{:S(2)}, u32[]{:S(2)}) collective-permute-start(bf16[8,32,512]{2,1,0:T(8,128)(2,1)S(1)} %all-to-all-done.2.refs_0_), channel_id=1, source_target_pairs={{0,2},{1,3},{2,0},{3,1},{4,6},{5,7},{6,4},{7,5},{8,10},{9,11},{10,... | collective-permute-start | bytes 786440 | tf_op jit(solution)/shard_map/ppermute | solution.py:462
  128.0 1.0 slice.51
  129.0 1.0 slice.52
  130.5 3.5 %collective-permute-done.9.refs_2_ = bf16[8,32,512]{2,1,0:T(8,128)(2,1)S(1)} collective-permute-done((bf16[8,32,512]{2,1,0:T(8,128)(2,1)S(1)}, bf16[8,32,512]{2,1,0:T(8,128)(2,1)S(1)}, u32[]{:S(2)}, u32[]{:S(2)}) %collective-permute-start.9) | collective-permute-done | bytes 262176 | tf_op jit(solution)/shard_map/ppermute | solution.py:462
  134.0 2.9 %collective-permute-start.14 = (bf16[16,64,128]{2,1,0:T(8,128)(2,1)S(1)}, bf16[16,64,128]{2,1,0:T(8,128)(2,1)}, u32[]{:S(2)}, u32[]{:S(2)}) collective-permute-start(bf16[16,64,128]{2,1,0:T(8,128)(2,1)S(1)} %slice.52), channel_id=1, source_target_pairs={{0,192},{32,224},{64,0},{96,32},{128,64},{160,96},{192,128},{224,1... | collective-permute-start | bytes 786440 | tf_op jit(solution)/shard_map/ppermute | solution.py:55
  136.9 4.9 %collective-permute-start.17 = (bf16[32,64,128]{2,1,0:T(8,128)(2,1)}, bf16[32,64,128]{2,1,0:T(8,128)(2,1)}, u32[]{:S(2)}, u32[]{:S(2)}) collective-permute-start(bf16[32,64,128]{2,1,0:T(8,128)(2,1)} %collective-permute-done.12.refs_3_), channel_id=1, source_target_pairs={{0,32},{32,0},{64,96},{96,64},{128,160},{160,128},{192,224},{224,1... | collective-permute-start | bytes 1572872 | tf_op jit(solution)/shard_map/ppermute | solution.py:64
  141.8 1.3 dynamic_slice.38
  143.8 1.0 copy-done.2
  144.8 1.0 collective-permute-start.18
  145.8 2.0 %collective-permute-start.19 = (bf16[16,64,128]{2,1,0:T(8,128)(2,1)}, bf16[16,64,128]{2,1,0:T(8,128)(2,1)}, u32[]{:S(2)}, u32[]{:S(2)}) collective-permute-start(bf16[16,64,128]{2,1,0:T(8,128)(2,1)} %collective-permute-done.14.refs_5_), channel_id=1, source_target_pairs={{0,32},{32,0},{64,96},{96,64},{128,160},{160,128},{192,224},{224,1... | collective-permute-start | bytes 786440 | tf_op jit(solution)/shard_map/ppermute | solution.py:64
  147.9 1.3 rsqrt.42.scale
  149.3 18.6 %shard_map.149 = bf16[1024,512]{1,0:T(8,128)(2,1)} custom-call(s32[4]{0:T(128)} %pad_add_fusion.here, f32[1024,1]{1,0:T(8,128)} %rsqrt.42.scale, f32[1,512]{1,0:T(1,128)} %bitcast.74, bf16[8,4,32,512]{3,2,1,0:T(8,128)(2,1)} %copy-done.2, bf16[32,64,128]{2,1,0:T(8,128)(2,1)} %copy-done.7, bf16[32,64,128]{2,1,0:T(8,128)(2,1)} %collective-permute-done.11.refs_2_, ...), custom_call_target="tpu_custom_call" | custom-call | flops 9663676416 | bytes 2097152 | tf_op jit(solution)/shard_map/pallas_call | solution.py:294
  (91 shorter events, 8.7 us)
Async XLA Ops:
  0.0 16.7 %copy-start = (bf16[4096,128]{1,0:T(8,128)(2,1)S(1)}, bf16[4096,128]{1,0:T(8,128)(2,1)}, u32[]{:S(2)}) copy-start(bf16[4096,128]{1,0:T(8,128)(2,1)} %param.18) | copy-start | bytes 3145732
  0.0 18.6 %copy-start.5 = (bf16[32,4096]{1,0:T(8,128)(2,1)S(1)}, bf16[32,4096]{1,0:T(8,128)(2,1)}, u32[]{:S(2)}) copy-start(bf16[32,4096]{1,0:T(8,128)(2,1)} %param.15) | copy-start | bytes 786436
  0.0 18.6 %copy-start.9 = (f32[4096]{0:T(1024)S(1)}, f32[4096]{0:T(1024)}, u32[]{:S(2)}) copy-start(f32[4096]{0:T(1024)} %param.16) | copy-start | bytes 49156
  0.0 18.4 %copy-start.12 = (f32[128]{0:T(128)S(1)}, f32[128]{0:T(128)}, u32[]{:S(2)}) copy-start(f32[128]{0:T(128)} %param.22) | copy-start | bytes 1540
  0.9 20.8 %copy-start.10 = (bf16[32,512]{1,0:T(8,128)(2,1)}, bf16[32,512]{1,0:T(8,128)(2,1)S(1)}, u32[]{:S(2)}) copy-start(bf16[32,512]{1,0:T(8,128)(2,1)S(1)} %constant_dynamic-slice_fusion.2.old_mine) | copy-start | bytes 98308
  2.0 19.9 %copy-start.13 = (f32[128]{0:T(128)S(1)}, f32[128]{0:T(128)}, u32[]{:S(2)}) copy-start(f32[128]{0:T(128)} %param.21) | copy-start | bytes 1540
  2.0 20.4 %copy-start.8 = (bf16[32,32,128]{2,1,0:T(8,128)(2,1)S(1)}, bf16[32,32,128]{2,1,0:T(8,128)(2,1)}, u32[]{:S(2)}) copy-start(bf16[32,32,128]{2,1,0:T(8,128)(2,1)} %param.23) | copy-start | bytes 786436
  2.0 38.3 %all-to-all-start = ((bf16[32,32,512]{2,1,0:T(8,128)(2,1)}), bf16[32,32,512]{2,1,0:T(8,128)(2,1)}, u32[]{:S(2)}, u32[]{:S(2)}) async-start(bf16[32,32,512]{2,1,0:T(8,128)(2,1)} %broadcast_in_dim.16), calls=%async_computation | async-start | bytes 2097152 | tf_op jit(solution)/shard_map/all_to_all | solution.py:46
  14.1 8.9 %copy-start.6 = (bf16[4096,128]{1,0:T(8,128)(2,1)S(1)}, bf16[4096,128]{1,0:T(8,128)(2,1)}, u32[]{:S(2)}) copy-start(bf16[4096,128]{1,0:T(8,128)(2,1)} %param.19) | copy-start | bytes 3145732
  16.7 6.6 %copy-start.14 = (bf16[32,32,128]{2,1,0:T(8,128)(2,1)S(1)}, bf16[32,32,128]{2,1,0:T(8,128)(2,1)}, u32[]{:S(2)}) copy-start(bf16[32,32,128]{2,1,0:T(8,128)(2,1)} %param.24) | copy-start | bytes 786436
  26.6 20.1 %copy-start.11 = (s32[512,1]{0,1:T(1,128)S(1)}, s32[512,1]{0,1:T(1,128)}, u32[]{:S(2)}) copy-start(s32[512,1]{0,1:T(1,128)} %param.29) | copy-start | bytes 6148
  27.5 2.0 %collective-permute-start = (bf16[32,4,512]{2,0,1:T(8,128)(2,1)S(1)}, bf16[32,4,512]{2,0,1:T(8,128)(2,1)S(1)}, u32[]{:S(2)}, u32[]{:S(2)}) collective-permute-start(bf16[32,4,512]{2,0,1:T(8,128)(2,1)S(1)} %bitcast.67), channel_id=1, source_target_pairs={{0,32},{32,0},{64,96},{96,64},{128,160},{160,128},{192,224},{224,1... | collective-permute-start | bytes 393224 | tf_op jit(solution)/shard_map/ppermute | solution.py:64
  29.6 5.1 %collective-permute-start.1 = (bf16[32,512]{1,0:T(8,128)(2,1)S(1)}, bf16[32,512]{1,0:T(8,128)(2,1)S(1)}, u32[]{:S(2)}, u32[]{:S(2)}) collective-permute-start(bf16[32,512]{1,0:T(8,128)(2,1)S(1)} %get-tuple-element.23), channel_id=1, source_target_pairs={{0,64},{32,96},{64,128},{96,160},{128,192},{160,224},{192,0},{224,... | collective-permute-start | bytes 98312 | tf_op jit(solution)/shard_map/ppermute | solution.py:431
  31.0 3.7 %collective-permute-start.3 = (bf16[32,512]{1,0:T(8,128)(2,1)S(1)}, bf16[32,512]{1,0:T(8,128)(2,1)S(1)}, u32[]{:S(2)}, u32[]{:S(2)}) collective-permute-start(bf16[32,512]{1,0:T(8,128)(2,1)S(1)} %get-tuple-element.24), channel_id=1, source_target_pairs={{0,192},{32,224},{64,0},{96,32},{128,64},{160,96},{192,128},{224,1... | collective-permute-start | bytes 98312 | tf_op jit(solution)/shard_map/ppermute | solution.py:431
  32.5 4.5 %collective-permute-start.2 = (bf16[32,512]{1,0:T(8,128)(2,1)S(1)}, bf16[32,512]{1,0:T(8,128)(2,1)S(1)}, u32[]{:S(2)}, u32[]{:S(2)}) collective-permute-start(bf16[32,512]{1,0:T(8,128)(2,1)S(1)} %get-tuple-element.25), channel_id=1, source_target_pairs={{0,128},{32,160},{64,192},{96,224},{128,0},{160,32},{192,64},{224,... | collective-permute-start | bytes 98312 | tf_op jit(solution)/shard_map/ppermute | solution.py:431
  34.6 13.9 %copy-start.3 = (s32[4]{0:T(128)S(1)}, s32[4]{0:T(128)}, u32[]{:S(2)}) copy-start(s32[4]{0:T(128)} %pad_add_fusion.here) | copy-start | bytes 52
  37.7 10.9 %copy-start.4 = (f32[1,128]{1,0:T(1,128)S(1)}, f32[1,128]{1,0:T(1,128)}, u32[]{:S(2)}) copy-start(f32[1,128]{1,0:T(1,128)} %pad.4.squares) | copy-start | bytes 1540
  43.9 4.7 %collective-permute-start.4 = (bf16[4,592,128]{2,1,0:T(8,128)(2,1)}, bf16[4,592,128]{2,1,0:T(8,128)(2,1)S(1)}, u32[]{:S(2)}, u32[]{:S(2)}) collective-permute-start(bf16[4,592,128]{2,1,0:T(8,128)(2,1)} %get-tuple-element.13), channel_id=1, source_target_pairs={{0,32},{32,0},{64,96},{96,64},{128,160},{160,128},{192,224},{224,1... | collective-permute-start | bytes 1818632 | tf_op jit(solution)/shard_map/ppermute | solution.py:64
  48.6 1.2 copy-start.1
  50.5 6.5 %collective-permute-start.5 = (bf16[592,128]{1,0:T(8,128)(2,1)S(1)}, bf16[592,128]{1,0:T(8,128)(2,1)S(1)}, u32[]{:S(2)}, u32[]{:S(2)}) collective-permute-start(bf16[592,128]{1,0:T(8,128)(2,1)S(1)} %get-tuple-element.16), channel_id=1, source_target_pairs={{0,64},{32,96},{64,128},{96,160},{128,192},{160,224},{192,0},{224,... | collective-permute-start | bytes 454664 | tf_op jit(solution)/shard_map/ppermute | solution.py:431
  51.9 9.5 %collective-permute-start.6 = (bf16[592,128]{1,0:T(8,128)(2,1)S(1)}, bf16[592,128]{1,0:T(8,128)(2,1)S(1)}, u32[]{:S(2)}, u32[]{:S(2)}) collective-permute-start(bf16[592,128]{1,0:T(8,128)(2,1)S(1)} %get-tuple-element.17), channel_id=1, source_target_pairs={{0,128},{32,160},{64,192},{96,224},{128,0},{160,32},{192,64},{224,... | collective-permute-start | bytes 454664 | tf_op jit(solution)/shard_map/ppermute | solution.py:431
  54.5 6.9 %collective-permute-start.7 = (bf16[592,128]{1,0:T(8,128)(2,1)S(1)}, bf16[592,128]{1,0:T(8,128)(2,1)S(1)}, u32[]{:S(2)}, u32[]{:S(2)}) collective-permute-start(bf16[592,128]{1,0:T(8,128)(2,1)S(1)} %get-tuple-element.18), channel_id=1, source_target_pairs={{0,192},{32,224},{64,0},{96,32},{128,64},{160,96},{192,128},{224,1... | collective-permute-start | bytes 454664 | tf_op jit(solution)/shard_map/ppermute | solution.py:431
  91.4 16.1 %all-to-all-start.3 = ((bf16[4,32,32,128]{3,2,1,0:T(8,128)(2,1)}), bf16[4,32,32,128]{3,2,1,0:T(8,128)(2,1)}, u32[]{:S(2)}, u32[]{:S(2)}) async-start(bf16[4,32,32,128]{3,2,1,0:T(8,128)(2,1)} %broadcast_in_dim.25), calls=%async_computation.3 | async-start | bytes 2097152 | tf_op jit(solution)/shard_map/all_to_all | solution.py:46
  95.7 53.6 %copy-start.7 = (bf16[32,64,128]{2,1,0:T(8,128)(2,1)}, bf16[32,64,128]{2,1,0:T(8,128)(2,1)S(1)}, u32[]{:S(2)}) copy-start(bf16[32,64,128]{2,1,0:T(8,128)(2,1)S(1)} %slice.50.refs_1_) | copy-start | bytes 1572868
  95.8 29.2 %collective-permute-start.12 = (bf16[32,64,128]{2,1,0:T(8,128)(2,1)S(1)}, bf16[32,64,128]{2,1,0:T(8,128)(2,1)}, u32[]{:S(2)}, u32[]{:S(2)}) collective-permute-start(bf16[32,64,128]{2,1,0:T(8,128)(2,1)S(1)} %slice.50.refs_1_), channel_id=1, source_target_pairs={{0,64},{32,96},{64,128},{96,160},{128,192},{160,224},{192,0},{224,... | collective-permute-start | bytes 1572872 | tf_op jit(solution)/shard_map/ppermute | solution.py:55
  108.3 14.9 %all-to-all-start.2 = ((bf16[8,32,512]{2,1,0:T(8,128)(2,1)}), bf16[8,32,512]{2,1,0:T(8,128)(2,1)S(1)}, u32[]{:S(2)}, u32[]{:S(2)}) async-start(bf16[8,32,512]{2,1,0:T(8,128)(2,1)} %broadcast_in_dim.24), calls=%async_computation.2 | async-start | bytes 524288 | tf_op jit(solution)/shard_map/all_to_all | solution.py:46
  113.9 13.6 %collective-permute-start.11 = (bf16[32,64,128]{2,1,0:T(8,128)(2,1)S(1)}, bf16[32,64,128]{2,1,0:T(8,128)(2,1)}, u32[]{:S(2)}, u32[]{:S(2)}) collective-permute-start(bf16[32,64,128]{2,1,0:T(8,128)(2,1)S(1)} %slice.50.refs_1_), channel_id=1, source_target_pairs={{0,192},{32,224},{64,0},{96,32},{128,64},{160,96},{192,128},{224,1... | collective-permute-start | bytes 1572872 | tf_op jit(solution)/shard_map/ppermute | solution.py:55
  115.3 26.5 %collective-permute-start.15 = (bf16[32,64,128]{2,1,0:T(8,128)(2,1)S(1)}, bf16[32,64,128]{2,1,0:T(8,128)(2,1)}, u32[]{:S(2)}, u32[]{:S(2)}) collective-permute-start(bf16[32,64,128]{2,1,0:T(8,128)(2,1)S(1)} %slice.50.refs_1_), channel_id=1, source_target_pairs={{0,32},{32,0},{64,96},{96,64},{128,160},{160,128},{192,224},{224,1... | collective-permute-start | bytes 1572872 | tf_op jit(solution)/shard_map/ppermute | solution.py:64
  120.1 29.2 %collective-permute-start.20 = (bf16[4,32,32,128]{3,2,1,0:T(8,128)(2,1)}, bf16[4,32,32,128]{3,2,1,0:T(8,128)(2,1)}, u32[]{:S(2)}, u32[]{:S(2)}) collective-permute-start(bf16[4,32,32,128]{3,2,1,0:T(8,128)(2,1)} %all-to-all-done.3.refs_11_), channel_id=1, source_target_pairs={{0,32},{32,0},{64,96},{96,64},{128,160},{160,128},{192,224},{224,1... | collective-permute-start | bytes 3145736 | tf_op jit(solution)/shard_map/ppermute | solution.py:64
  123.2 6.9 %collective-permute-start.10 = (bf16[8,32,512]{2,1,0:T(8,128)(2,1)S(1)}, bf16[8,32,512]{2,1,0:T(8,128)(2,1)S(1)}, u32[]{:S(2)}, u32[]{:S(2)}) collective-permute-start(bf16[8,32,512]{2,1,0:T(8,128)(2,1)S(1)} %all-to-all-done.2.refs_0_), channel_id=1, source_target_pairs={{0,1},{1,2},{2,3},{3,0},{4,5},{5,6},{6,7},{7,4},{8,9},{9,10},{10,1... | collective-permute-start | bytes 786440 | tf_op jit(solution)/shard_map/ppermute | solution.py:462
  124.9 9.1 %collective-permute-start.9 = (bf16[8,32,512]{2,1,0:T(8,128)(2,1)S(1)}, bf16[8,32,512]{2,1,0:T(8,128)(2,1)S(1)}, u32[]{:S(2)}, u32[]{:S(2)}) collective-permute-start(bf16[8,32,512]{2,1,0:T(8,128)(2,1)S(1)} %all-to-all-done.2.refs_0_), channel_id=1, source_target_pairs={{0,2},{1,3},{2,0},{3,1},{4,6},{5,7},{6,4},{7,5},{8,10},{9,11},{10,... | collective-permute-start | bytes 786440 | tf_op jit(solution)/shard_map/ppermute | solution.py:462
  127.4 9.4 %collective-permute-start.8 = (bf16[8,32,512]{2,1,0:T(8,128)(2,1)S(1)}, bf16[8,32,512]{2,1,0:T(8,128)(2,1)S(1)}, u32[]{:S(2)}, u32[]{:S(2)}) collective-permute-start(bf16[8,32,512]{2,1,0:T(8,128)(2,1)S(1)} %all-to-all-done.2.refs_0_), channel_id=1, source_target_pairs={{0,3},{1,0},{2,1},{3,2},{4,7},{5,4},{6,5},{7,6},{8,11},{9,8},{10,9... | collective-permute-start | bytes 786440 | tf_op jit(solution)/shard_map/ppermute | solution.py:462
  130.1 14.6 %collective-permute-start.13 = (bf16[16,64,128]{2,1,0:T(8,128)(2,1)S(1)}, bf16[16,64,128]{2,1,0:T(8,128)(2,1)}, u32[]{:S(2)}, u32[]{:S(2)}) collective-permute-start(bf16[16,64,128]{2,1,0:T(8,128)(2,1)S(1)} %slice.51), channel_id=1, source_target_pairs={{0,64},{32,96},{64,128},{96,160},{128,192},{160,224},{192,0},{224,... | collective-permute-start | bytes 786440 | tf_op jit(solution)/shard_map/ppermute | solution.py:55
  134.0 11.8 %collective-permute-start.14 = (bf16[16,64,128]{2,1,0:T(8,128)(2,1)S(1)}, bf16[16,64,128]{2,1,0:T(8,128)(2,1)}, u32[]{:S(2)}, u32[]{:S(2)}) collective-permute-start(bf16[16,64,128]{2,1,0:T(8,128)(2,1)S(1)} %slice.52), channel_id=1, source_target_pairs={{0,192},{32,224},{64,0},{96,32},{128,64},{160,96},{192,128},{224,1... | collective-permute-start | bytes 786440 | tf_op jit(solution)/shard_map/ppermute | solution.py:55
  136.9 12.3 %collective-permute-start.17 = (bf16[32,64,128]{2,1,0:T(8,128)(2,1)}, bf16[32,64,128]{2,1,0:T(8,128)(2,1)}, u32[]{:S(2)}, u32[]{:S(2)}) collective-permute-start(bf16[32,64,128]{2,1,0:T(8,128)(2,1)} %collective-permute-done.12.refs_3_), channel_id=1, source_target_pairs={{0,32},{32,0},{64,96},{96,64},{128,160},{160,128},{192,224},{224,1... | collective-permute-start | bytes 1572872 | tf_op jit(solution)/shard_map/ppermute | solution.py:64
  141.8 7.4 %collective-permute-start.16 = (bf16[32,64,128]{2,1,0:T(8,128)(2,1)}, bf16[32,64,128]{2,1,0:T(8,128)(2,1)}, u32[]{:S(2)}, u32[]{:S(2)}) collective-permute-start(bf16[32,64,128]{2,1,0:T(8,128)(2,1)} %collective-permute-done.11.refs_2_), channel_id=1, source_target_pairs={{0,32},{32,0},{64,96},{96,64},{128,160},{160,128},{192,224},{224,1... | collective-permute-start | bytes 1572872 | tf_op jit(solution)/shard_map/ppermute | solution.py:64
  143.8 1.0 copy-start.2
  144.8 4.4 %collective-permute-start.18 = (bf16[16,64,128]{2,1,0:T(8,128)(2,1)}, bf16[16,64,128]{2,1,0:T(8,128)(2,1)}, u32[]{:S(2)}, u32[]{:S(2)}) collective-permute-start(bf16[16,64,128]{2,1,0:T(8,128)(2,1)} %collective-permute-done.13.refs_4_), channel_id=1, source_target_pairs={{0,32},{32,0},{64,96},{96,64},{128,160},{160,128},{192,224},{224,1... | collective-permute-start | bytes 786440 | tf_op jit(solution)/shard_map/ppermute | solution.py:64
  145.8 3.5 %collective-permute-start.19 = (bf16[16,64,128]{2,1,0:T(8,128)(2,1)}, bf16[16,64,128]{2,1,0:T(8,128)(2,1)}, u32[]{:S(2)}, u32[]{:S(2)}) collective-permute-start(bf16[16,64,128]{2,1,0:T(8,128)(2,1)} %collective-permute-done.14.refs_5_), channel_id=1, source_target_pairs={{0,32},{32,0},{64,96},{96,64},{128,160},{160,128},{192,224},{224,1... | collective-permute-start | bytes 786440 | tf_op jit(solution)/shard_map/ppermute | solution.py:64

commit v7 on v6

--- a/solution.py
+++ b/solution.py
@@ -96,7 +96,7 @@
 
 def norm_block(value):
     high = value.astype(jnp.bfloat16).astype(jnp.float32)
-    row = lax.broadcasted_iota(jnp.int32, (16, value.shape[1]), 0)
+    row = lax.broadcasted_iota(jnp.int32, (8, value.shape[1]), 0)
     block = jnp.where(row == 0, high, jnp.where(row == 1, value - high, 0.0))
     return block.astype(jnp.bfloat16)
 
@@ -104,7 +104,7 @@
 def fill(target, slab, gram, norms):
     target[:512] = slab.astype(jnp.bfloat16)
     target[512:544], target[544:576] = both(gram)
-    target[576:592] = norms
+    target[576:584] = norms
 
 
 def parts_kernel(here, slab, old_mine, old_all, squares, theirs, kept):
@@ -161,7 +161,7 @@
     for owner in range(32):
         outgoing[owner, 32:64] = high
         outgoing[owner, 64:96] = low
-        outgoing[owner, 96:112] = norms
+        outgoing[owner, 96:104] = norms
 
 
 def join_kernel(here, *refs):
@@ -302,6 +302,20 @@
     )(*operands)
 
 
+def unpack_kernel(arrived, gram, routed):
+    gram[...] = arrived[:, 32:96]
+    for chip in range(4):
+        routed[chip] = arrived[:, :32]
+
+
+def unpack(arrived):
+    shapes = (
+        jax.ShapeDtypeStruct((32, 64, 128), jnp.bfloat16),
+        jax.ShapeDtypeStruct((4, 32, 32, 128), jnp.bfloat16),
+    )
+    return call(unpack_kernel, shapes, [VMEM], [], [arrived], 1 << 20, 62)
+
+
 def join(*operands):
     shape = jax.ShapeDtypeStruct((8, 4) + operands[1].shape[1:], jnp.bfloat16)
     return call(join_kernel, shape, [SMEM] + [VMEM] * 4, [], operands, 1 << 20, 16)
@@ -309,7 +323,7 @@
 
 def make_parts(*operands):
     shapes = (
-        jax.ShapeDtypeStruct((4, 592, 128), jnp.bfloat16),
+        jax.ShapeDtypeStruct((4, 584, 128), jnp.bfloat16),
         jax.ShapeDtypeStruct((4, 544, 128), jnp.float32),
     )
     return call(parts_kernel, shapes, [SMEM] + [VMEM] * 4, [], operands, 1 << 30, 62)
@@ -319,13 +333,13 @@
     shapes = (
         jax.ShapeDtypeStruct((544, 128), jnp.float32),
         jax.ShapeDtypeStruct((1, 128), jnp.float32),
-    ) + (jax.ShapeDtypeStruct((592, 128), jnp.bfloat16),) * 3
-    return call(pair_kernel, shapes, [SMEM] + [VMEM] * 3, [], operands, 1 << 20, 16)
+    ) + (jax.ShapeDtypeStruct((584, 128), jnp.bfloat16),) * 3
+    return call(pair_kernel, shapes, [SMEM] + [VMEM] * 3, [], operands, 1 << 20, 62)
 
 
 def route(*operands):
-    shape = jax.ShapeDtypeStruct((32, 112, 128), jnp.bfloat16)
-    return call(route_kernel, shape, [VMEM] * 6, [], operands, 1 << 27, 16)
+    shape = jax.ShapeDtypeStruct((32, 104, 128), jnp.bfloat16)
+    return call(route_kernel, shape, [VMEM] * 6, [], operands, 1 << 27, 62)
 
 
 def solve(*operands):
@@ -481,15 +495,14 @@
     pieces = [shift_chips(piece, step) for step, piece in enumerate(pieces, 1)]
     outgoing = route(target, kept, squares, *pieces)
     arrived = lax.all_to_all(outgoing, "rows", 0, 0, tiled=True)
-    routed = arrived[:, :capacity]
-    gram = arrived[:, capacity : capacity + 2 * docs]
+    gram, routed = unpack(arrived)
     squares = arrived[:, capacity + 2 * docs : capacity + 2 * docs + 2, :docs]
     squares = jnp.sum(squares.astype(jnp.float32), axis=1)
     scale_rows = lax.rsqrt(squares / width + 1e-06).reshape(anchors, 1)
 
     grams = ring(gram, "mp", chips, mp_count, 2)
     grams = grams + [swap_cores(piece, mp_count) for piece in grams]
-    slabs = spread(routed, "mp", chips, by_y)
+    slabs = lax.all_to_all(routed, "mp", 0, 0, tiled=True, axis_index_groups=by_y)
     slabs = [slabs, swap_cores(slabs, mp_count)]
     return solve(
         here, scale_rows, gain, state_all, *grams, *slabs

time: 169 us -> 174 us (1.030)
  Pallas kernels: 24 us -> 30.1 us
    all_to_all x0 -> x1, waiting for transfers between devices: none -> 10.3 us  [local(): lax.all_to_all(routed, 'mp', 0, 0, tiled=True, axis_index_groups=by_y)]
    all_to_all x3 -> x2, waiting for transfers between devices: 15.7 us -> 5.56 us  [spread(): lax.all_to_all(copies, axis, 0, 0, tiled=True, axis_index_groups=groups)]
    pallas_call x5 -> x6, Pallas kernels: 24 us -> 30.1 us  [call(): pl.pallas_call(kernel, out_shape=shapes, in_specs=in_specs, out_specs=jax...]
    all_to_all x3 -> x2, starting transfers between devices: 21.9 us -> 17.7 us  [spread(): lax.all_to_all(copies, axis, 0, 0, tiled=True, axis_index_groups=groups)]
    all_to_all x0 -> x1, starting transfers between devices: none -> 3.85 us  [local(): lax.all_to_all(routed, 'mp', 0, 0, tiled=True, axis_index_groups=by_y)]
    ppermute x4, starting transfers between devices: 6.28 us -> 4.29 us  [move(): return lax.ppermute(array, axis, pairs)]
    ppermute x8, starting transfers between devices: 16.8 us -> 18.8 us  [swap_cores(): return lax.ppermute(block, 'mp', [(i, i ^ 1) for i in range(size)])]
  transfers between devices with their start and end apart: 24 -> 24, of which waited for: 11 -> 10; matrix products, arithmetic and copies ran while one was open for 13% -> 13% of each run, Pallas kernels for 0% -> 0%
where the time goes in v7:
time: 174 us
  starting transfers between devices  58.5 us (34%)
  Pallas kernels  30.1 us (17%)
  waiting for transfers between devices  29.3 us (17%)
  blocking collectives  27.5 us (16%)
  local copies, waits for them, and re-layouts  11.5 us (7%)
  matrix products  8.72 us (5%)
  other arithmetic  7.28 us (4%)
    pallas_call x6, Pallas kernels, call(): pl.pallas_call(kernel, out_shape=shapes, in_specs=in_specs, out_specs=jax...  30.1 us
    all_to_all x1, blocking collectives, local(): arrived = lax.all_to_all(outgoing, 'rows', 0, 0, tiled=True)  27.5 us
    ppermute x8, starting transfers between devices, swap_cores(): return lax.ppermute(block, 'mp', [(i, i ^ 1) for i in range(size)])  18.8 us
    all_to_all x2, starting transfers between devices, spread(): lax.all_to_all(copies, axis, 0, 0, tiled=True, axis_index_groups=groups)  17.7 us
    all_to_all x1, waiting for transfers between devices, local(): lax.all_to_all(routed, 'mp', 0, 0, tiled=True, axis_index_groups=by_y)  10.3 us
    ppermute x6, starting transfers between devices, shift_chips(): lax.ppermute(block, 'mp', [(i, (i + 2 * step) % mp_count) for i in range(...  9.45 us
    ppermute x6, waiting for transfers between devices, shift_chips(): lax.ppermute(block, 'mp', [(i, (i + 2 * step) % mp_count) for i in range(...  7.62 us
    all_to_all x2, waiting for transfers between devices, spread(): lax.all_to_all(copies, axis, 0, 0, tiled=True, axis_index_groups=groups)  5.56 us
  transfers between devices with their start and end apart: 24, of which 10 were waited for; matrix products, arithmetic and copies ran while one was open for 13% of the time, Pallas kernels for 0%

profile of v7, /device:TPU:1, one launch (start us, length us, event | category | flops | bytes accessed | tf_op | source)
XLA Modules:
  0.0 173.5 jit_solution(10650114090993718091)
XLA Ops:
  0.0 0.9 constant_dynamic-slice_fusion.2.old_mine
  0.9 1.1 broadcast_in_dim.14
  2.0 12.1 %all-to-all-start = ((bf16[32,32,512]{2,1,0:T(8,128)(2,1)}), bf16[32,32,512]{2,1,0:T(8,128)(2,1)}, u32[]{:S(2)}, u32[]{:S(2)}) async-start(bf16[32,32,512]{2,1,0:T(8,128)(2,1)} %broadcast_in_dim.14), calls=%async_computation | async-start | bytes 2097152 | tf_op jit(solution)/shard_map/all_to_all | solution.py:46
  15.6 1.1 multiply_reduce_fusion
  16.8 1.4 multiply_reduce_fusion.3
  18.6 3.1 %fusion.31 = f32[32,512]{1,0:T(8,128)S(1)} fusion(bf16[4096,512]{1,0:T(8,128)(2,1)} %param.17, f32[4096]{0:T(1024)S(1)} %copy-done.11, f32[32]{0:T(128)S(1)} %add_rsqrt_fusion.3, bf16[32,4096]{1,0:T(8,128)(2,1)S(1)} %copy-done.3), kind=kOutput, calls=%fused_computation.77 | convolution fusion | flops 134742016 | bytes 4538496 | tf_op jit(solution)/shard_map/dot_general | solution.py:395
  23.6 3.0 %fusion.11 = f32[32,4096]{1,0:T(8,128)S(1)} fusion(bf16[512,4096]{1,0:T(8,128)(2,1)} %param.20, bf16[4,8,4,128]{3,2,1,0:T(4,128)(2,1)S(1)} %bitcast.70), kind=kOutput, calls=%fused_computation.31 | convolution fusion | flops 134217728 | bytes 4751360 | tf_op jit(solution)/shard_map/dot_general | solution.py:435
  27.5 1.0 collective-permute-start
  29.6 1.4 collective-permute-start.1
  31.0 1.5 collective-permute-start.3
  32.5 1.6 collective-permute-start.2
  34.8 2.3 %collective-permute-done.2 = bf16[32,512]{1,0:T(8,128)(2,1)S(1)} collective-permute-done((bf16[32,512]{1,0:T(8,128)(2,1)S(1)}, bf16[32,512]{1,0:T(8,128)(2,1)S(1)}, u32[]{:S(2)}, u32[]{:S(2)}) %collective-permute-start.2) | collective-permute-done | bytes 32800 | tf_op jit(solution)/shard_map/ppermute | solution.py:445
  37.7 2.6 %all-to-all-done = bf16[32,32,512]{2,1,0:T(8,128)(2,1)} async-done(((bf16[32,32,512]{2,1,0:T(8,128)(2,1)}), bf16[32,32,512]{2,1,0:T(8,128)(2,1)}, u32[]{:S(2)}, u32[]{:S(2)}) %all-to-all-start) | async-done | bytes 1048608 | tf_op jit(solution)/shard_map/all_to_all | solution.py:46
  40.3 3.6 %shard_map.145 = (bf16[4,584,128]{2,1,0:T(8,128)(2,1)}, f32[4,544,128]{2,1,0:T(8,128)}) custom-call(s32[4]{0:T(128)} %pad_add_fusion.here, bf16[512,512]{1,0:T(8,128)(2,1)} %slab.1, bf16[32,512]{1,0:T(8,128)(2,1)} %copy-done.12, bf16[1024,512]{1,0:T(8,128)(2,1)} %bitcast.8.old_all, f32[1,128]{1,0:T(1,128)} %pad.4.squares), custom_call_target="tpu_custom_call" | custom-call | flops 1073741824 | bytes 2097152 | tf_op jit(solution)/shard_map/pallas_call | solution.py:294
  43.9 2.8 %collective-permute-start.4 = (bf16[4,584,128]{2,1,0:T(8,128)(2,1)}, bf16[4,584,128]{2,1,0:T(8,128)(2,1)S(1)}, u32[]{:S(2)}, u32[]{:S(2)}) collective-permute-start(bf16[4,584,128]{2,1,0:T(8,128)(2,1)} %get-tuple-element.15), channel_id=1, source_target_pairs={{0,32},{32,0},{64,96},{96,64},{128,160},{160,128},{192,224},{224,1... | collective-permute-start | bytes 1794056 | tf_op jit(solution)/shard_map/ppermute | solution.py:64
  46.7 1.2 reduce-window.6
  48.6 0.8 copy-done.6
  49.4 2.4 %shard_map.146 = (f32[544,128]{1,0:T(8,128)}, f32[1,128]{1,0:T(1,128)}, bf16[584,128]{1,0:T(8,128)(2,1)}, bf16[584,128]{1,0:T(8,128)(2,1)}, bf16[584,128]{1,0:T(8,128)(2,1)}) custom-call(s32[4]{0:T(128)} %pad_add_fusion.here, f32[4,544,128]{2,1,0:T(8,128)} %get-tuple-element.14.kept, bf16[4,584,128]{2,1,0:T(8,128)(2,1)} %copy-done.6, f32[1,128]{1,0:T(1,128)} %pad.4.squares), custom_call_target="tpu_custom_call" | custom-call | flops 1048576 | bytes 2097152 | tf_op jit(solution)/shard_map/pallas_call | solution.py:294
  51.8 1.3 collective-permute-start.5
  53.1 2.6 %collective-permute-start.6 = (bf16[584,128]{1,0:T(8,128)(2,1)}, bf16[584,128]{1,0:T(8,128)(2,1)S(1)}, u32[]{:S(2)}, u32[]{:S(2)}) collective-permute-start(bf16[584,128]{1,0:T(8,128)(2,1)} %get-tuple-element.19), channel_id=1, source_target_pairs={{0,128},{32,160},{64,192},{96,224},{128,0},{160,32},{192,64},{224,... | collective-permute-start | bytes 448520 | tf_op jit(solution)/shard_map/ppermute | solution.py:445
  55.7 1.1 collective-permute-start.7
  57.4 1.0 collective-permute-done.5.refs_0_
  58.4 4.3 %collective-permute-done.6.refs_1_ = bf16[584,128]{1,0:T(8,128)(2,1)S(1)} collective-permute-done((bf16[584,128]{1,0:T(8,128)(2,1)}, bf16[584,128]{1,0:T(8,128)(2,1)S(1)}, u32[]{:S(2)}, u32[]{:S(2)}) %collective-permute-start.6) | collective-permute-done | bytes 149536 | tf_op jit(solution)/shard_map/ppermute | solution.py:445
  63.4 2.5 %shard_map.147 = bf16[32,104,128]{2,1,0:T(8,128)(2,1)} custom-call(s32[1,512]{1,0:T(1,128)} %bitcast_add_fusion.2.target, f32[544,128]{1,0:T(8,128)} %get-tuple-element.16.mine, f32[1,128]{1,0:T(1,128)} %get-tuple-element.17.squares, bf16[584,128]{1,0:T(8,128)(2,1)} %copy-done.8, bf16[584,128]{1,0:T(8,128)(2,1)} %copy-done.9, bf16[584,128]{1,0:T(8,128)(2,1)} %copy-done.10), custom_call_target="tpu_custom_call" | custom-call | flops 134217728 | bytes 2097152 | tf_op jit(solution)/shard_map/pallas_call | solution.py:294
  65.9 27.5 %all_to_all.20.arrived = bf16[32,104,128]{2,1,0:T(8,128)(2,1)} all-to-all(bf16[32,104,128]{2,1,0:T(8,128)(2,1)} %shard_map.147), channel_id=1, replica_groups=mesh['mp'=8,'rows'=32] {'rows'}, dimensions={0} | all-to-all | bytes 1703936 | tf_op jit(solution)/shard_map/all_to_all | solution.py:497
  93.5 2.4 %shard_map.149 = (bf16[32,64,128]{2,1,0:T(8,128)(2,1)}, bf16[4,32,32,128]{3,2,1,0:T(8,128)(2,1)}) custom-call(bf16[32,104,128]{2,1,0:T(8,128)(2,1)} %all_to_all.20.arrived), custom_call_target="tpu_custom_call" | custom-call | flops 1048576 | bytes 2097152 | tf_op jit(solution)/shard_map/pallas_call | solution.py:294
  95.9 3.8 %all-to-all-start.3 = ((bf16[4,32,32,128]{3,2,1,0:T(8,128)(2,1)}), bf16[4,32,32,128]{3,2,1,0:T(8,128)(2,1)S(1)}, u32[]{:S(2)}, u32[]{:S(2)}) async-start(bf16[4,32,32,128]{3,2,1,0:T(8,128)(2,1)} %get-tuple-element.22), calls=%async_computation.3 | async-start | bytes 2097152 | tf_op jit(solution)/shard_map/all_to_all | solution.py:505
  99.7 1.5 collective-permute-start.12
  101.2 10.3 %all-to-all-done.3.refs_11_ = bf16[4,32,32,128]{3,2,1,0:T(8,128)(2,1)S(1)} async-done(((bf16[4,32,32,128]{3,2,1,0:T(8,128)(2,1)}), bf16[4,32,32,128]{3,2,1,0:T(8,128)(2,1)S(1)}, u32[]{:S(2)}, u32[]{:S(2)}) %all-to-all-start.3) | async-done | bytes 1048608 | tf_op jit(solution)/shard_map/all_to_all | solution.py:505
  111.5 0.8 broadcast_in_dim.22
  112.3 5.6 %all-to-all-start.2 = ((bf16[8,32,512]{2,1,0:T(8,128)(2,1)}), bf16[8,32,512]{2,1,0:T(8,128)(2,1)S(1)}, u32[]{:S(2)}, u32[]{:S(2)}) async-start(bf16[8,32,512]{2,1,0:T(8,128)(2,1)} %broadcast_in_dim.22), calls=%async_computation.2 | async-start | bytes 524288 | tf_op jit(solution)/shard_map/all_to_all | solution.py:46
  117.8 0.8 collective-permute-start.11
  118.7 5.4 %collective-permute-start.15 = (bf16[32,64,128]{2,1,0:T(8,128)(2,1)}, bf16[32,64,128]{2,1,0:T(8,128)(2,1)}, u32[]{:S(2)}, u32[]{:S(2)}) collective-permute-start(bf16[32,64,128]{2,1,0:T(8,128)(2,1)} %get-tuple-element.21.refs_1_), channel_id=1, source_target_pairs={{0,32},{32,0},{64,96},{96,64},{128,160},{160,128},{192,224},{224,1... | collective-permute-start | bytes 1572872 | tf_op jit(solution)/shard_map/ppermute | solution.py:64
  124.2 3.0 %all-to-all-done.2.refs_0_ = bf16[8,32,512]{2,1,0:T(8,128)(2,1)S(1)} async-done(((bf16[8,32,512]{2,1,0:T(8,128)(2,1)}), bf16[8,32,512]{2,1,0:T(8,128)(2,1)S(1)}, u32[]{:S(2)}, u32[]{:S(2)}) %all-to-all-start.2) | async-done | bytes 262176 | tf_op jit(solution)/shard_map/all_to_all | solution.py:46
  127.2 2.0 %collective-permute-start.10 = (bf16[8,32,512]{2,1,0:T(8,128)(2,1)S(1)}, bf16[8,32,512]{2,1,0:T(8,128)(2,1)S(1)}, u32[]{:S(2)}, u32[]{:S(2)}) collective-permute-start(bf16[8,32,512]{2,1,0:T(8,128)(2,1)S(1)} %all-to-all-done.2.refs_0_), channel_id=1, source_target_pairs={{0,1},{1,2},{2,3},{3,0},{4,5},{5,6},{6,7},{7,4},{8,9},{9,10},{10,1... | collective-permute-start | bytes 786440 | tf_op jit(solution)/shard_map/ppermute | solution.py:476
  129.2 1.8 %collective-permute-start.9 = (bf16[8,32,512]{2,1,0:T(8,128)(2,1)S(1)}, bf16[8,32,512]{2,1,0:T(8,128)(2,1)S(1)}, u32[]{:S(2)}, u32[]{:S(2)}) collective-permute-start(bf16[8,32,512]{2,1,0:T(8,128)(2,1)S(1)} %all-to-all-done.2.refs_0_), channel_id=1, source_target_pairs={{0,2},{1,3},{2,0},{3,1},{4,6},{5,7},{6,4},{7,5},{8,10},{9,11},{10,... | collective-permute-start | bytes 786440 | tf_op jit(solution)/shard_map/ppermute | solution.py:476
  131.7 1.0 slice.43
  132.6 1.2 collective-permute-done.10.refs_3_
  133.9 3.6 %collective-permute-done.9.refs_2_ = bf16[8,32,512]{2,1,0:T(8,128)(2,1)S(1)} collective-permute-done((bf16[8,32,512]{2,1,0:T(8,128)(2,1)S(1)}, bf16[8,32,512]{2,1,0:T(8,128)(2,1)S(1)}, u32[]{:S(2)}, u32[]{:S(2)}) %collective-permute-start.9) | collective-permute-done | bytes 262176 | tf_op jit(solution)/shard_map/ppermute | solution.py:476
  137.5 1.9 %collective-permute-start.14 = (bf16[16,64,128]{2,1,0:T(8,128)(2,1)S(1)}, bf16[16,64,128]{2,1,0:T(8,128)(2,1)}, u32[]{:S(2)}, u32[]{:S(2)}) collective-permute-start(bf16[16,64,128]{2,1,0:T(8,128)(2,1)S(1)} %slice.43), channel_id=1, source_target_pairs={{0,192},{32,224},{64,0},{96,32},{128,64},{160,96},{192,128},{224,1... | collective-permute-start | bytes 786440 | tf_op jit(solution)/shard_map/ppermute | solution.py:55
  139.4 6.3 %collective-permute-start.17 = (bf16[32,64,128]{2,1,0:T(8,128)(2,1)S(1)}, bf16[32,64,128]{2,1,0:T(8,128)(2,1)}, u32[]{:S(2)}, u32[]{:S(2)}) collective-permute-start(bf16[32,64,128]{2,1,0:T(8,128)(2,1)S(1)} %collective-permute-done.12.refs_3_), channel_id=1, source_target_pairs={{0,32},{32,0},{64,96},{96,64},{128,160},{160,128},{192,224},{224,1... | collective-permute-start | bytes 1572872 | tf_op jit(solution)/shard_map/ppermute | solution.py:64
  145.7 1.3 dynamic_slice.38
  147.7 1.0 copy-done.1
  148.7 1.0 collective-permute-start.18
  149.7 2.1 %collective-permute-start.19 = (bf16[16,64,128]{2,1,0:T(8,128)(2,1)}, bf16[16,64,128]{2,1,0:T(8,128)(2,1)}, u32[]{:S(2)}, u32[]{:S(2)}) collective-permute-start(bf16[16,64,128]{2,1,0:T(8,128)(2,1)} %collective-permute-done.14.refs_5_), channel_id=1, source_target_pairs={{0,32},{32,0},{64,96},{96,64},{128,160},{160,128},{192,224},{224,1... | collective-permute-start | bytes 786440 | tf_op jit(solution)/shard_map/ppermute | solution.py:64
  151.8 0.9 convert_reduce_fusion
  152.7 1.3 rsqrt.42.scale
  154.8 18.6 %shard_map.150 = bf16[1024,512]{1,0:T(8,128)(2,1)} custom-call(s32[4]{0:T(128)} %pad_add_fusion.here, f32[1024,1]{1,0:T(8,128)} %rsqrt.42.scale, f32[1,512]{1,0:T(1,128)} %bitcast.74, bf16[8,4,32,512]{3,2,1,0:T(8,128)(2,1)} %copy-done.1, bf16[32,64,128]{2,1,0:T(8,128)(2,1)} %get-tuple-element.21.refs_1_, ...), custom_call_target="tpu_custom_call" | custom-call | flops 9663676416 | bytes 2097152 | tf_op jit(solution)/shard_map/pallas_call | solution.py:294
  (97 shorter events, 11.1 us)
Async XLA Ops:
  0.0 16.7 %copy-start = (bf16[4096,128]{1,0:T(8,128)(2,1)S(1)}, bf16[4096,128]{1,0:T(8,128)(2,1)}, u32[]{:S(2)}) copy-start(bf16[4096,128]{1,0:T(8,128)(2,1)} %param.18) | copy-start | bytes 3145732
  0.0 18.6 %copy-start.3 = (bf16[32,4096]{1,0:T(8,128)(2,1)S(1)}, bf16[32,4096]{1,0:T(8,128)(2,1)}, u32[]{:S(2)}) copy-start(bf16[32,4096]{1,0:T(8,128)(2,1)} %param.15) | copy-start | bytes 786436
  0.0 18.6 %copy-start.11 = (f32[4096]{0:T(1024)S(1)}, f32[4096]{0:T(1024)}, u32[]{:S(2)}) copy-start(f32[4096]{0:T(1024)} %param.16) | copy-start | bytes 49156
  0.0 18.4 %copy-start.15 = (f32[128]{0:T(128)S(1)}, f32[128]{0:T(128)}, u32[]{:S(2)}) copy-start(f32[128]{0:T(128)} %param.22) | copy-start | bytes 1540
  0.9 20.8 %copy-start.12 = (bf16[32,512]{1,0:T(8,128)(2,1)}, bf16[32,512]{1,0:T(8,128)(2,1)S(1)}, u32[]{:S(2)}) copy-start(bf16[32,512]{1,0:T(8,128)(2,1)S(1)} %constant_dynamic-slice_fusion.2.old_mine) | copy-start | bytes 98308
  2.0 19.9 %copy-start.16 = (f32[128]{0:T(128)S(1)}, f32[128]{0:T(128)}, u32[]{:S(2)}) copy-start(f32[128]{0:T(128)} %param.21) | copy-start | bytes 1540
  2.0 20.4 %copy-start.7 = (bf16[32,32,128]{2,1,0:T(8,128)(2,1)S(1)}, bf16[32,32,128]{2,1,0:T(8,128)(2,1)}, u32[]{:S(2)}) copy-start(bf16[32,32,128]{2,1,0:T(8,128)(2,1)} %param.23) | copy-start | bytes 786436
  2.0 38.3 %all-to-all-start = ((bf16[32,32,512]{2,1,0:T(8,128)(2,1)}), bf16[32,32,512]{2,1,0:T(8,128)(2,1)}, u32[]{:S(2)}, u32[]{:S(2)}) async-start(bf16[32,32,512]{2,1,0:T(8,128)(2,1)} %broadcast_in_dim.14), calls=%async_computation | async-start | bytes 2097152 | tf_op jit(solution)/shard_map/all_to_all | solution.py:46
  14.1 8.9 %copy-start.4 = (bf16[4096,128]{1,0:T(8,128)(2,1)S(1)}, bf16[4096,128]{1,0:T(8,128)(2,1)}, u32[]{:S(2)}) copy-start(bf16[4096,128]{1,0:T(8,128)(2,1)} %param.19) | copy-start | bytes 3145732
  16.7 6.6 %copy-start.17 = (bf16[32,32,128]{2,1,0:T(8,128)(2,1)S(1)}, bf16[32,32,128]{2,1,0:T(8,128)(2,1)}, u32[]{:S(2)}) copy-start(bf16[32,32,128]{2,1,0:T(8,128)(2,1)} %param.24) | copy-start | bytes 786436
  26.6 20.1 %copy-start.14 = (s32[512,1]{0,1:T(1,128)S(1)}, s32[512,1]{0,1:T(1,128)}, u32[]{:S(2)}) copy-start(s32[512,1]{0,1:T(1,128)} %param.29) | copy-start | bytes 6148
  27.5 2.0 %collective-permute-start = (bf16[32,4,512]{2,0,1:T(8,128)(2,1)S(1)}, bf16[32,4,512]{2,0,1:T(8,128)(2,1)S(1)}, u32[]{:S(2)}, u32[]{:S(2)}) collective-permute-start(bf16[32,4,512]{2,0,1:T(8,128)(2,1)S(1)} %bitcast.67), channel_id=1, source_target_pairs={{0,32},{32,0},{64,96},{96,64},{128,160},{160,128},{192,224},{224,1... | collective-permute-start | bytes 393224 | tf_op jit(solution)/shard_map/ppermute | solution.py:64
  29.6 5.1 %collective-permute-start.1 = (bf16[32,512]{1,0:T(8,128)(2,1)S(1)}, bf16[32,512]{1,0:T(8,128)(2,1)S(1)}, u32[]{:S(2)}, u32[]{:S(2)}) collective-permute-start(bf16[32,512]{1,0:T(8,128)(2,1)S(1)} %get-tuple-element.27), channel_id=1, source_target_pairs={{0,64},{32,96},{64,128},{96,160},{128,192},{160,224},{192,0},{224,... | collective-permute-start | bytes 98312 | tf_op jit(solution)/shard_map/ppermute | solution.py:445
  31.0 3.8 %collective-permute-start.3 = (bf16[32,512]{1,0:T(8,128)(2,1)S(1)}, bf16[32,512]{1,0:T(8,128)(2,1)S(1)}, u32[]{:S(2)}, u32[]{:S(2)}) collective-permute-start(bf16[32,512]{1,0:T(8,128)(2,1)S(1)} %get-tuple-element.28), channel_id=1, source_target_pairs={{0,192},{32,224},{64,0},{96,32},{128,64},{160,96},{192,128},{224,1... | collective-permute-start | bytes 98312 | tf_op jit(solution)/shard_map/ppermute | solution.py:445
  32.5 4.5 %collective-permute-start.2 = (bf16[32,512]{1,0:T(8,128)(2,1)S(1)}, bf16[32,512]{1,0:T(8,128)(2,1)S(1)}, u32[]{:S(2)}, u32[]{:S(2)}) collective-permute-start(bf16[32,512]{1,0:T(8,128)(2,1)S(1)} %get-tuple-element.29), channel_id=1, source_target_pairs={{0,128},{32,160},{64,192},{96,224},{128,0},{160,32},{192,64},{224,... | collective-permute-start | bytes 98312 | tf_op jit(solution)/shard_map/ppermute | solution.py:445
  43.9 4.7 %collective-permute-start.4 = (bf16[4,584,128]{2,1,0:T(8,128)(2,1)}, bf16[4,584,128]{2,1,0:T(8,128)(2,1)S(1)}, u32[]{:S(2)}, u32[]{:S(2)}) collective-permute-start(bf16[4,584,128]{2,1,0:T(8,128)(2,1)} %get-tuple-element.15), channel_id=1, source_target_pairs={{0,32},{32,0},{64,96},{96,64},{128,160},{160,128},{192,224},{224,1... | collective-permute-start | bytes 1794056 | tf_op jit(solution)/shard_map/ppermute | solution.py:64
  48.6 0.8 copy-start.6
  51.8 95.3 %copy-start.2 = (s32[4]{0:T(128)S(1)}, s32[4]{0:T(128)}, u32[]{:S(2)}) copy-start(s32[4]{0:T(128)} %pad_add_fusion.here) | copy-start | bytes 52
  51.8 6.6 %collective-permute-start.5 = (bf16[584,128]{1,0:T(8,128)(2,1)}, bf16[584,128]{1,0:T(8,128)(2,1)S(1)}, u32[]{:S(2)}, u32[]{:S(2)}) collective-permute-start(bf16[584,128]{1,0:T(8,128)(2,1)} %get-tuple-element.18), channel_id=1, source_target_pairs={{0,64},{32,96},{64,128},{96,160},{128,192},{160,224},{192,0},{224,... | collective-permute-start | bytes 448520 | tf_op jit(solution)/shard_map/ppermute | solution.py:445
  53.1 9.6 %collective-permute-start.6 = (bf16[584,128]{1,0:T(8,128)(2,1)}, bf16[584,128]{1,0:T(8,128)(2,1)S(1)}, u32[]{:S(2)}, u32[]{:S(2)}) collective-permute-start(bf16[584,128]{1,0:T(8,128)(2,1)} %get-tuple-element.19), channel_id=1, source_target_pairs={{0,128},{32,160},{64,192},{96,224},{128,0},{160,32},{192,64},{224,... | collective-permute-start | bytes 448520 | tf_op jit(solution)/shard_map/ppermute | solution.py:445
  55.7 7.0 %collective-permute-start.7 = (bf16[584,128]{1,0:T(8,128)(2,1)}, bf16[584,128]{1,0:T(8,128)(2,1)S(1)}, u32[]{:S(2)}, u32[]{:S(2)}) collective-permute-start(bf16[584,128]{1,0:T(8,128)(2,1)} %get-tuple-element.20), channel_id=1, source_target_pairs={{0,192},{32,224},{64,0},{96,32},{128,64},{160,96},{192,128},{224,1... | collective-permute-start | bytes 448520 | tf_op jit(solution)/shard_map/ppermute | solution.py:445
  58.4 4.3 %copy-start.8 = (bf16[584,128]{1,0:T(8,128)(2,1)}, bf16[584,128]{1,0:T(8,128)(2,1)S(1)}, u32[]{:S(2)}) copy-start(bf16[584,128]{1,0:T(8,128)(2,1)S(1)} %collective-permute-done.5.refs_0_) | copy-start | bytes 448516
  62.7 0.7 copy-start.9
  62.7 0.7 copy-start.10
  95.9 15.6 %all-to-all-start.3 = ((bf16[4,32,32,128]{3,2,1,0:T(8,128)(2,1)}), bf16[4,32,32,128]{3,2,1,0:T(8,128)(2,1)S(1)}, u32[]{:S(2)}, u32[]{:S(2)}) async-start(bf16[4,32,32,128]{3,2,1,0:T(8,128)(2,1)} %get-tuple-element.22), calls=%async_computation.3 | async-start | bytes 2097152 | tf_op jit(solution)/shard_map/all_to_all | solution.py:505
  99.7 29.4 %collective-permute-start.12 = (bf16[32,64,128]{2,1,0:T(8,128)(2,1)}, bf16[32,64,128]{2,1,0:T(8,128)(2,1)S(1)}, u32[]{:S(2)}, u32[]{:S(2)}) collective-permute-start(bf16[32,64,128]{2,1,0:T(8,128)(2,1)} %get-tuple-element.21.refs_1_), channel_id=1, source_target_pairs={{0,64},{32,96},{64,128},{96,160},{128,192},{160,224},{192,0},{224,... | collective-permute-start | bytes 1572872 | tf_op jit(solution)/shard_map/ppermute | solution.py:55
  111.5 36.2 %copy-start.5 = (bf16[4,32,32,128]{3,2,1,0:T(8,128)(2,1)}, bf16[4,32,32,128]{3,2,1,0:T(8,128)(2,1)S(1)}, u32[]{:S(2)}) copy-start(bf16[4,32,32,128]{3,2,1,0:T(8,128)(2,1)S(1)} %all-to-all-done.3.refs_11_) | copy-start | bytes 3145732
  112.3 14.9 %all-to-all-start.2 = ((bf16[8,32,512]{2,1,0:T(8,128)(2,1)}), bf16[8,32,512]{2,1,0:T(8,128)(2,1)S(1)}, u32[]{:S(2)}, u32[]{:S(2)}) async-start(bf16[8,32,512]{2,1,0:T(8,128)(2,1)} %broadcast_in_dim.22), calls=%async_computation.2 | async-start | bytes 524288 | tf_op jit(solution)/shard_map/all_to_all | solution.py:46
  117.8 13.1 %collective-permute-start.11 = (bf16[32,64,128]{2,1,0:T(8,128)(2,1)}, bf16[32,64,128]{2,1,0:T(8,128)(2,1)}, u32[]{:S(2)}, u32[]{:S(2)}) collective-permute-start(bf16[32,64,128]{2,1,0:T(8,128)(2,1)} %get-tuple-element.21.refs_1_), channel_id=1, source_target_pairs={{0,192},{32,224},{64,0},{96,32},{128,64},{160,96},{192,128},{224,1... | collective-permute-start | bytes 1572872 | tf_op jit(solution)/shard_map/ppermute | solution.py:55
  118.7 27.1 %collective-permute-start.15 = (bf16[32,64,128]{2,1,0:T(8,128)(2,1)}, bf16[32,64,128]{2,1,0:T(8,128)(2,1)}, u32[]{:S(2)}, u32[]{:S(2)}) collective-permute-start(bf16[32,64,128]{2,1,0:T(8,128)(2,1)} %get-tuple-element.21.refs_1_), channel_id=1, source_target_pairs={{0,32},{32,0},{64,96},{96,64},{128,160},{160,128},{192,224},{224,1... | collective-permute-start | bytes 1572872 | tf_op jit(solution)/shard_map/ppermute | solution.py:64
  124.1 30.0 %collective-permute-start.20 = (bf16[4,32,32,128]{3,2,1,0:T(8,128)(2,1)S(1)}, bf16[4,32,32,128]{3,2,1,0:T(8,128)(2,1)}, u32[]{:S(2)}, u32[]{:S(2)}) collective-permute-start(bf16[4,32,32,128]{3,2,1,0:T(8,128)(2,1)S(1)} %all-to-all-done.3.refs_11_), channel_id=1, source_target_pairs={{0,32},{32,0},{64,96},{96,64},{128,160},{160,128},{192,224},{224,1... | collective-permute-start | bytes 3145736 | tf_op jit(solution)/shard_map/ppermute | solution.py:64
  127.2 6.7 %collective-permute-start.10 = (bf16[8,32,512]{2,1,0:T(8,128)(2,1)S(1)}, bf16[8,32,512]{2,1,0:T(8,128)(2,1)S(1)}, u32[]{:S(2)}, u32[]{:S(2)}) collective-permute-start(bf16[8,32,512]{2,1,0:T(8,128)(2,1)S(1)} %all-to-all-done.2.refs_0_), channel_id=1, source_target_pairs={{0,1},{1,2},{2,3},{3,0},{4,5},{5,6},{6,7},{7,4},{8,9},{9,10},{10,1... | collective-permute-start | bytes 786440 | tf_op jit(solution)/shard_map/ppermute | solution.py:476
  129.2 25.6 %copy-start.13 = (bf16[32,64,128]{2,1,0:T(8,128)(2,1)}, bf16[32,64,128]{2,1,0:T(8,128)(2,1)S(1)}, u32[]{:S(2)}) copy-start(bf16[32,64,128]{2,1,0:T(8,128)(2,1)S(1)} %collective-permute-done.12.refs_3_) | copy-start | bytes 1572868
  129.2 8.3 %collective-permute-start.9 = (bf16[8,32,512]{2,1,0:T(8,128)(2,1)S(1)}, bf16[8,32,512]{2,1,0:T(8,128)(2,1)S(1)}, u32[]{:S(2)}, u32[]{:S(2)}) collective-permute-start(bf16[8,32,512]{2,1,0:T(8,128)(2,1)S(1)} %all-to-all-done.2.refs_0_), channel_id=1, source_target_pairs={{0,2},{1,3},{2,0},{3,1},{4,6},{5,7},{6,4},{7,5},{8,10},{9,11},{10,... | collective-permute-start | bytes 786440 | tf_op jit(solution)/shard_map/ppermute | solution.py:476
  130.9 8.5 %collective-permute-start.8 = (bf16[8,32,512]{2,1,0:T(8,128)(2,1)S(1)}, bf16[8,32,512]{2,1,0:T(8,128)(2,1)S(1)}, u32[]{:S(2)}, u32[]{:S(2)}) collective-permute-start(bf16[8,32,512]{2,1,0:T(8,128)(2,1)S(1)} %all-to-all-done.2.refs_0_), channel_id=1, source_target_pairs={{0,3},{1,0},{2,1},{3,2},{4,7},{5,4},{6,5},{7,6},{8,11},{9,8},{10,9... | collective-permute-start | bytes 786440 | tf_op jit(solution)/shard_map/ppermute | solution.py:476
  133.9 14.8 %collective-permute-start.13 = (bf16[16,64,128]{2,1,0:T(8,128)(2,1)S(1)}, bf16[16,64,128]{2,1,0:T(8,128)(2,1)}, u32[]{:S(2)}, u32[]{:S(2)}) collective-permute-start(bf16[16,64,128]{2,1,0:T(8,128)(2,1)S(1)} %slice.42), channel_id=1, source_target_pairs={{0,64},{32,96},{64,128},{96,160},{128,192},{160,224},{192,0},{224,... | collective-permute-start | bytes 786440 | tf_op jit(solution)/shard_map/ppermute | solution.py:55
  137.5 12.2 %collective-permute-start.14 = (bf16[16,64,128]{2,1,0:T(8,128)(2,1)S(1)}, bf16[16,64,128]{2,1,0:T(8,128)(2,1)}, u32[]{:S(2)}, u32[]{:S(2)}) collective-permute-start(bf16[16,64,128]{2,1,0:T(8,128)(2,1)S(1)} %slice.43), channel_id=1, source_target_pairs={{0,192},{32,224},{64,0},{96,32},{128,64},{160,96},{192,128},{224,1... | collective-permute-start | bytes 786440 | tf_op jit(solution)/shard_map/ppermute | solution.py:55
  139.4 14.6 %collective-permute-start.17 = (bf16[32,64,128]{2,1,0:T(8,128)(2,1)S(1)}, bf16[32,64,128]{2,1,0:T(8,128)(2,1)}, u32[]{:S(2)}, u32[]{:S(2)}) collective-permute-start(bf16[32,64,128]{2,1,0:T(8,128)(2,1)S(1)} %collective-permute-done.12.refs_3_), channel_id=1, source_target_pairs={{0,32},{32,0},{64,96},{96,64},{128,160},{160,128},{192,224},{224,1... | collective-permute-start | bytes 1572872 | tf_op jit(solution)/shard_map/ppermute | solution.py:64
  145.7 8.3 %collective-permute-start.16 = (bf16[32,64,128]{2,1,0:T(8,128)(2,1)}, bf16[32,64,128]{2,1,0:T(8,128)(2,1)}, u32[]{:S(2)}, u32[]{:S(2)}) collective-permute-start(bf16[32,64,128]{2,1,0:T(8,128)(2,1)} %collective-permute-done.11.refs_2_), channel_id=1, source_target_pairs={{0,32},{32,0},{64,96},{96,64},{128,160},{160,128},{192,224},{224,1... | collective-permute-start | bytes 1572872 | tf_op jit(solution)/shard_map/ppermute | solution.py:64
  147.7 1.0 copy-start.1
  148.7 5.4 %collective-permute-start.18 = (bf16[16,64,128]{2,1,0:T(8,128)(2,1)}, bf16[16,64,128]{2,1,0:T(8,128)(2,1)S(1)}, u32[]{:S(2)}, u32[]{:S(2)}) collective-permute-start(bf16[16,64,128]{2,1,0:T(8,128)(2,1)} %collective-permute-done.13.refs_4_), channel_id=1, source_target_pairs={{0,32},{32,0},{64,96},{96,64},{128,160},{160,128},{192,224},{224,1... | collective-permute-start | bytes 786440 | tf_op jit(solution)/shard_map/ppermute | solution.py:64
  149.7 4.3 %collective-permute-start.19 = (bf16[16,64,128]{2,1,0:T(8,128)(2,1)}, bf16[16,64,128]{2,1,0:T(8,128)(2,1)}, u32[]{:S(2)}, u32[]{:S(2)}) collective-permute-start(bf16[16,64,128]{2,1,0:T(8,128)(2,1)} %collective-permute-done.14.refs_5_), channel_id=1, source_target_pairs={{0,32},{32,0},{64,96},{96,64},{128,160},{160,128},{192,224},{224,1... | collective-permute-start | bytes 786440 | tf_op jit(solution)/shard_map/ppermute | solution.py:64
  154.1 0.7 copy-start.18
